TPU v7x, 256 devices: a whole 4x4x8 slice. The times are simulated.
256 devices in a mesh: win: 32 (over x, z), ch: 8 (over y, core).
Axes of the slice: x: 4, y: 4, z: 8, core: 2. Of those that a mesh axis runs over, the one named last changes fastest.
Arguments:
- spectra: bfloat16 [384, 1024, 512], P('win', 'ch'), may hold values from -40 to 40
- sources: int32 [8], replicated, may hold values from 0 to 1023
- valid: int32 [384], P('win'), may hold values from 0 to 1, as said below
Outputs:
- weights: float32 [384, 8, 1024], P('win', None, 'ch')
- beamed: float32 [256, 8, 2, 512], P(('win', 'ch'))
Inputs may be any that keep to these rules, and one draw needn't show every extreme that they name: At least one window is valid.
All inputs are finite; a program needn't handle non-finite values.
Results may differ from a plain program's by a relative error of at most 0.0003.
The roundings to bfloat16 on the way count: a program that leaves them out, or rounds other values in their place, can miss the bound.
Values may be sent and summed in bfloat16 or wider, within the bound.
No kernel may reach another device: no remote copies, remote signals or barrier semaphores. Data moves between devices by JAX's collectives and lax.ppermute only.
A program may use at most 64 MiB of HBM per device.

v0:
```python
import math

import jax
import jax.numpy as jnp
from jax import lax
from jax.sharding import PartitionSpec as P

L = 256
P_SIZE = 512
ITERS = 3


degrees = 3.0
epsilon = 1e-06


def inverse_table(freq_count, lag_count):
    freq_ids = jnp.arange(freq_count, dtype=jnp.int32)
    delay_indices = jnp.arange(lag_count, dtype=jnp.int32) - lag_count // 2
    phase_ids = jnp.mod(freq_ids[:, None] * delay_indices[None, :], 2 * freq_count)
    angles = 2.0 * math.pi / (2 * freq_count) * phase_ids.astype(jnp.float32)
    factor = 1.0 / math.sqrt(freq_count)
    return jnp.concatenate([jnp.cos(angles) * factor, -jnp.sin(angles) * factor], axis=0).astype(
        jnp.bfloat16
    )


def cross_rows(source_rows, channel_rows):
    freq_count = channel_rows.shape[-1] // 2
    source_f = source_rows.astype(jnp.float32)
    channel_f = channel_rows.astype(jnp.float32)
    source_real = source_f[:, None, :freq_count]
    source_imag = source_f[:, None, freq_count:]
    real_channel_rows = channel_f[None, :, :freq_count]
    channel_imag = channel_f[None, :, freq_count:]
    real_part = source_real * real_channel_rows + source_imag * channel_imag
    imag_part = source_imag * real_channel_rows - source_real * channel_imag
    return jnp.concatenate([real_part, imag_part], axis=-1).astype(jnp.bfloat16)


def correlate(paired, inverse):
    crossed = cross_rows(paired[0], paired[1])
    flattened_rows = crossed.reshape(-1, crossed.shape[-1])
    product = jnp.dot(flattened_rows, inverse, preferred_element_type=jnp.float32)
    return product.astype(jnp.bfloat16).reshape(
        crossed.shape[0], crossed.shape[1], inverse.shape[1]
    )


def forward_table(first_row, row_count, freq_count, lag_count):
    freq_ids = first_row + jnp.arange(row_count, dtype=jnp.int32)
    delay_indices = jnp.arange(lag_count, dtype=jnp.int32) - lag_count // 2
    phase_ids = jnp.mod(freq_ids[:, None] * delay_indices[None, :], 2 * freq_count)
    angles = 2.0 * math.pi / (2 * freq_count) * phase_ids.astype(jnp.float32)
    factor = 1.0 / math.sqrt(lag_count)
    return jnp.stack([jnp.cos(angles) * factor, -jnp.sin(angles) * factor], axis=1)


def transform(stacked, first_row, row_count, freq_count):
    table_rows = forward_table(first_row, row_count, freq_count, stacked.shape[-1])
    return jnp.einsum("kal,scl->kasc", table_rows, stacked, precision=lax.Precision.HIGHEST)


def beam_one(freq_id, spectrum, freq_count, slow_count, beam_gain):
    chan_count = spectrum.shape[-1]
    chan_ids = jnp.arange(chan_count, dtype=jnp.int32)
    slow_ids = jnp.arange(slow_count, dtype=jnp.int32) - slow_count // 2
    modulus = 4 * freq_count * slow_count
    phase_ids = jnp.mod((freq_id * chan_ids)[:, None] * slow_ids[None, :], modulus)
    angles = 2.0 * math.pi / modulus * phase_ids.astype(jnp.float32)
    cosines = jnp.cos(angles)
    sines = jnp.sin(angles)
    highest = lax.Precision.HIGHEST
    beam_cosine_part = jnp.dot(
        spectrum[0], cosines, precision=highest, preferred_element_type=jnp.float32
    ) - jnp.dot(spectrum[1], sines, precision=highest, preferred_element_type=jnp.float32)
    imag_beam = jnp.dot(
        spectrum[0], sines, precision=highest, preferred_element_type=jnp.float32
    ) + jnp.dot(spectrum[1], cosines, precision=highest, preferred_element_type=jnp.float32)
    return jnp.stack([beam_cosine_part, imag_beam], axis=1) * beam_gain


def body(spectra, sources, valid):
    chan_dev = spectra.shape[1]
    freq_count = spectra.shape[2] // 2
    source_total = sources.shape[0]
    n_win = lax.axis_size("win")
    n_ch = lax.axis_size("ch")
    chans = chan_dev * n_ch
    shift_amount = lax.axis_index("ch") * chan_dev
    picker = (
        sources[:, None] - shift_amount == jnp.arange(chan_dev, dtype=jnp.int32)[None, :]
    ).astype(jnp.bfloat16)
    picked = jnp.einsum("sc,wcf->wsf", picker, spectra, preferred_element_type=jnp.float32)
    source_spectra = lax.psum(picked.astype(jnp.bfloat16), "ch")
    inverse = inverse_table(freq_count, L)
    correlations = lax.map(lambda paired: correlate(paired, inverse), (source_spectra, spectra))
    freq_win = freq_count // n_win
    first_freq = lax.axis_index("win") * freq_win
    window_mask = valid.astype(jnp.float32)
    first_local = jnp.sum(
        window_mask[:, None, None, None] * correlations.astype(jnp.float32), axis=0
    )
    count_local = jnp.sum(window_mask)
    first_num, valid_count = lax.psum((first_local, count_local), "win")
    stacked = first_num / valid_count
    for iteration in range(ITERS):
        residual_sq = jnp.mean(
            jnp.square(correlations.astype(jnp.float32) - stacked[None]), axis=-1
        )
        summed = lax.psum(jnp.sum(window_mask[:, None, None] * residual_sq), ("win", "ch"))
        spread_sq = summed / (source_total * chans * valid_count) + epsilon
        weights = window_mask[:, None, None] * (degrees + 1.0) / (degrees + residual_sq / spread_sq)
        numer_local = jnp.sum(weights[..., None] * correlations.astype(jnp.float32), axis=0)
        denom_local = jnp.sum(weights, axis=0)
        if iteration + 1 < ITERS:
            numer, denom = lax.psum((numer_local, denom_local), "win")
            stacked = numer / denom[..., None]
    numer, denom = lax.psum((numer_local, denom_local), "win")
    spectrum = transform(numer / denom[..., None], first_freq, freq_win, freq_count)
    freq_dev = freq_win // n_ch
    freq_base = first_freq + lax.axis_index("ch") * freq_dev
    beam_gain = chans ** (-0.5)
    pieces = lax.all_to_all(spectrum, "ch", split_axis=0, concat_axis=3, tiled=True)
    freq_ids = freq_base + jnp.arange(pieces.shape[0], dtype=jnp.int32)
    beamed = lax.map(
        lambda paired: beam_one(paired[0], paired[1], freq_count, P_SIZE, beam_gain),
        (freq_ids, pieces),
    )
    return (weights, beamed)


def solution(mesh):
    return jax.shard_map(
        body,
        mesh=mesh,
        in_specs=(P("win", "ch", None), P(), P("win")),
        out_specs=(P("win", None, "ch"), P(("win", "ch"), None, None, None)),
        check_vma=False,
    )
```

profile of v0, /device:TPU:1, one launch (start us, length us, event | category | flops | bytes accessed | tf_op | source)
XLA Modules:
  0.0 1028.9 jit_solution(14313308815586127588)
XLA Ops:
  7.9 2.4 fusion.17
  10.4 1.1 multiply_convert_fusion.1
  11.6 64.0 %all-reduce.6.cloned.1.call-done = bf16[12,8,512]{2,1,0:T(8,128)(2,1)} async-done(((bf16[12,8,512]{2,1,0:T(8,128)(2,1)}), bf16[12,8,512]{2,1,0:T(8,128)(2,1)}) %all-reduce.6.cloned.1.call-update) | async-done | bytes 98320 | tf_op jit(solution)/shard_map/psum | solution.py:95
  75.6 38.9 %while.2 = (s32[]{:T(128)}, bf16[12,8,128,256]{3,2,1,0:T(8,128)(2,1)}, bf16[12,8,512]{2,1,0:T(8,128)(2,1)}, bf16[12,128,512]{2,1,0:T(8,128)(2,1)}, bf16[512,256]{1,0:T(8,128)(2,1)S(1)}, /*index=5*/s32[]{:T(128)}) while((s32[]{:T(128)}, bf16[12,8,128,256]{3,2,1,0:T(8,128)(2,1)}, bf16[12,8,512]{2,1,0:T(8,128)(2,1)}, ...), condition=%wide.region_2.3_spmd, body=%wide.region_1.2_spmd.sunk | while | flops 272961536 | bytes 5186125 | solution.py:97
  75.6 0.9 bitcast_convert_fusion.4
  78.9 0.9 bitcast_convert_fusion.4
  82.1 0.9 bitcast_convert_fusion.4
  84.5 0.9 constant_dynamic-update-slice_fusion.2
  85.4 0.9 bitcast_convert_fusion.4
  87.8 0.9 constant_dynamic-update-slice_fusion.2
  88.6 0.9 bitcast_convert_fusion.4
  91.9 0.9 bitcast_convert_fusion.4
  95.1 0.9 bitcast_convert_fusion.4
  98.3 0.9 bitcast_convert_fusion.4
  100.7 0.9 constant_dynamic-update-slice_fusion.2
  101.6 0.9 bitcast_convert_fusion.4
  104.8 0.9 bitcast_convert_fusion.4
  107.2 0.9 constant_dynamic-update-slice_fusion.2
  108.1 0.9 bitcast_convert_fusion.4
  111.3 0.9 bitcast_convert_fusion.4
  114.6 5.2 fusion.4
  120.4 61.5 %psum.86 = f32[]{:T(128)} all-reduce(f32[]{:T(128)} %get-tuple-element.73), channel_id=1, replica_groups=mesh['win'=32,'ch'=8] {'win'}, use_global_device_ids=true, to_apply=%region_6.7 | all-reduce | flops 1 | bytes 8 | tf_op jit(solution)/shard_map/psum | solution.py:105
  181.9 84.3 %all-reduce.8.cloned.1.call-done = f32[8,128,256]{2,1,0:T(8,128)} async-done(((f32[8,128,256]{2,1,0:T(8,128)}), f32[8,128,256]{2,1,0:T(8,128)}) %all-reduce.8.cloned.1.call-update) | async-done | bytes 1048592 | tf_op jit(solution)/shard_map/psum | solution.py:105
  266.2 2.0 broadcast_divide_fusion.2
  268.2 4.7 fusion.6
  274.2 78.9 %psum.87 = f32[]{:T(128)} all-reduce(f32[]{:T(128)} %multiply_reduce_fusion.2), channel_id=1, replica_groups=mesh['win'=32,'ch'=8] {'win','ch'}, use_global_device_ids=true, to_apply=%region_9.10 | all-reduce | flops 1 | bytes 8 | tf_op jit(solution)/shard_map/psum | solution.py:111
  353.9 5.5 fusion.7
  359.5 57.5 %psum.89 = f32[8,128]{1,0:T(8,128)S(1)} all-reduce(f32[8,128]{1,0:T(8,128)S(1)} %get-tuple-element.60), channel_id=1, replica_groups=mesh['win'=32,'ch'=8] {'win'}, use_global_device_ids=true, to_apply=%region_13.14 | all-reduce | flops 1024 | bytes 8192 | tf_op jit(solution)/shard_map/psum | solution.py:117
  416.9 84.1 %all-reduce.10.cloned.1.call-done = f32[8,128,256]{2,1,0:T(8,128)} async-done(((f32[8,128,256]{2,1,0:T(8,128)}), f32[8,128,256]{2,1,0:T(8,128)}) %all-reduce.10.cloned.1.call-update) | async-done | bytes 1048592 | tf_op jit(solution)/shard_map/psum | solution.py:117
  501.1 1.4 broadcast_divide_fusion.1
  502.5 4.7 fusion.9
  507.9 78.9 %psum.90 = f32[]{:T(128)} all-reduce(f32[]{:T(128)} %multiply_reduce_fusion.1), channel_id=1, replica_groups=mesh['win'=32,'ch'=8] {'win','ch'}, use_global_device_ids=true, to_apply=%region_16.17 | all-reduce | flops 1 | bytes 8 | tf_op jit(solution)/shard_map/psum | solution.py:111
  587.5 5.5 fusion.10
  593.1 69.1 %psum.92 = f32[8,128]{1,0:T(8,128)S(1)} all-reduce(f32[8,128]{1,0:T(8,128)S(1)} %get-tuple-element.58), channel_id=1, replica_groups=mesh['win'=32,'ch'=8] {'win'}, use_global_device_ids=true, to_apply=%region_20.21 | all-reduce | flops 1024 | bytes 8192 | tf_op jit(solution)/shard_map/psum | solution.py:117
  662.3 72.4 %all-reduce.12.cloned.1.call-done = f32[8,128,256]{2,1,0:T(8,128)} async-done(((f32[8,128,256]{2,1,0:T(8,128)}), f32[8,128,256]{2,1,0:T(8,128)}) %all-reduce.12.cloned.1.call-update) | async-done | bytes 1048592 | tf_op jit(solution)/shard_map/psum | solution.py:117
  734.7 1.4 broadcast_divide_fusion
  736.1 4.7 fusion.12
  741.5 78.9 %psum.93 = f32[]{:T(128)} all-reduce(f32[]{:T(128)} %multiply_reduce_fusion), channel_id=1, replica_groups=mesh['win'=32,'ch'=8] {'win','ch'}, use_global_device_ids=true, to_apply=%region_23.24 | all-reduce | flops 1 | bytes 8 | tf_op jit(solution)/shard_map/psum | solution.py:111
  821.1 5.5 fusion.13
  826.8 57.5 %psum.95 = f32[8,128]{1,0:T(8,128)S(1)} all-reduce(f32[8,128]{1,0:T(8,128)S(1)} %get-tuple-element.56), channel_id=1, replica_groups=mesh['win'=32,'ch'=8] {'win'}, use_global_device_ids=true, to_apply=%region_27.28 | all-reduce | flops 1024 | bytes 8192 | tf_op jit(solution)/shard_map/psum | solution.py:119
  884.3 84.0 %all-reduce.14.cloned.1.call-done = f32[8,128,256]{2,1,0:T(8,128)} async-done(((f32[8,128,256]{2,1,0:T(8,128)}), f32[8,128,256]{2,1,0:T(8,128)}) %all-reduce.14.cloned.1.call-update) | async-done | bytes 1048592 | tf_op jit(solution)/shard_map/psum | solution.py:119
  968.3 2.2 fusion.20
  971.1 9.8 all-to-all-start
  980.9 4.8 all-to-all-done
  985.8 8.7 fusion.25
  994.5 9.2 fusion.27
  1003.8 9.0 fusion.19
  1012.7 8.8 fusion.18
  (101 shorter events, 29.5 us)
Async XLA Ops:
  7.2 4.4 copy-start.1
  7.2 68.5 %all-reduce.6.cloned.1.call-start = ((), (), s32[]{:S(2)}) async-start(), calls=%async_computation.1 | async-start | bytes 196608 | tf_op jit(solution)/shard_map/psum | solution.py:95
  10.3 255.9 %all-reduce.8.cloned.1.call-start = ((), (), s32[]{:S(2)}) async-start(), calls=%async_computation.2 | async-start | bytes 2097152 | tf_op jit(solution)/shard_map/psum | solution.py:105
  119.8 381.3 %all-reduce.10.cloned.1.call-start = ((), (), s32[]{:S(2)}) async-start(), calls=%async_computation.3 | async-start | bytes 2097152 | tf_op jit(solution)/shard_map/psum | solution.py:117
  359.4 375.2 %all-reduce.12.cloned.1.call-start = ((), (), s32[]{:S(2)}) async-start(), calls=%async_computation.4 | async-start | bytes 2097152 | tf_op jit(solution)/shard_map/psum | solution.py:117
  593.1 375.2 %all-reduce.14.cloned.1.call-start = ((), (), s32[]{:S(2)}) async-start(), calls=%async_computation.5 | async-start | bytes 2097152 | tf_op jit(solution)/shard_map/psum | solution.py:119
  821.1 5.5 copy-start
  971.1 14.7 %all-to-all-start = ((f32[8,2,8,128]{3,2,1,0:T(8,128)}), f32[8,2,8,128]{3,2,1,0:T(8,128)S(1)}, u32[]{:S(2)}, u32[]{:S(2)}) async-start(f32[8,2,8,128]{3,2,1,0:T(8,128)} %copy.6), calls=%async_computation | async-start | bytes 131072 | tf_op jit(solution)/shard_map/all_to_all | solution.py:124
Sparse Core Ops, SparseCore 0:
  10.5 65.1 all-reduce.5
  119.9 146.2 all-reduce.7
  359.5 141.4 all-reduce.9
  593.2 141.4 all-reduce.11
  826.8 141.4 all-reduce.13
where the time goes:
time: 1040 us; the launch traced here: 1030 us
  blocking collectives  482 us (46%)
  waiting for transfers between devices  394 us (38%)
  other arithmetic  68.5 us (7%)
  matrix products  45.6 us (4%)
  between operations  16.7 us (2%)
  local copies, waits for them, and re-layouts  11.7 us (1%)
    psum x3, waiting for transfers between devices, body(): numer, denom = lax.psum((numer_local, denom_local), 'win')  240 us
    psum x3, blocking collectives, body(): lax.psum(jnp.sum(window_mask[:, None, None] * residual_sq), ('win', 'ch'))  237 us
    psum x3, blocking collectives, body(): numer, denom = lax.psum((numer_local, denom_local), 'win')  184 us
    psum x1, waiting for transfers between devices, body(): first_num, valid_count = lax.psum((first_local, count_local), 'win')  84.3 us
    psum x1, waiting for transfers between devices, body(): source_spectra = lax.psum(picked.astype(jnp.bfloat16), 'ch')  64 us
    psum x1, blocking collectives, body(): first_num, valid_count = lax.psum((first_local, count_local), 'win')  61.5 us
  transfers between devices with their start and end apart: 6, of which 6 were waited for; matrix products, arithmetic and copies ran while one was open for 0% of the time, Pallas kernels for 0%

commit v1 on v0

v1 whole, which is shorter than its diff:
```python
import math

import jax
import jax.numpy as jnp
import numpy as np
from jax import lax
from jax.experimental import pallas as pl
from jax.experimental.pallas import tpu as pltpu
from jax.sharding import PartitionSpec as P

L = 256
P_SIZE = 512
ITERS = 3
Q = 4
LANES = 128

degrees = 3.0
epsilon = 1e-06
HIGHEST = lax.Precision.HIGHEST
NT = (((1,), (1,)), ((), ()))
TN = (((0,), (0,)), ((), ()))


def tables(freq_count, lag_count):
    freq_ids = np.arange(freq_count, dtype=np.int64)
    delays = np.arange(lag_count, dtype=np.int64) - lag_count // 2
    phase_ids = np.mod(freq_ids[:, None] * delays[None, :], 2 * freq_count)
    angles = np.float32(2.0 * math.pi / (2 * freq_count)) * phase_ids.astype(np.float32)
    cosines = np.cos(angles.astype(np.float64)).astype(np.float32)
    sines = np.sin(angles.astype(np.float64)).astype(np.float32)
    inverse_factor = np.float32(1.0 / math.sqrt(freq_count))
    forward_factor = np.float32(1.0 / math.sqrt(lag_count))
    inverse = np.concatenate([cosines * inverse_factor, -sines * inverse_factor], axis=0)
    forward = np.concatenate([cosines * forward_factor, -sines * forward_factor], axis=0)
    return np.ascontiguousarray(inverse.T), forward


def pick_kernel(ids_ref, x_ref, o_ref):
    rows, chan_dev = x_ref.shape[0], 128
    win_dev = rows // chan_dev
    row = lax.broadcasted_iota(jnp.int32, (16, rows), 0)
    col = lax.broadcasted_iota(jnp.int32, (16, rows), 1)
    shift = ids_ref[o_ref.shape[0]]
    blocks = []
    for s in range(o_ref.shape[0]):
        base = ids_ref[s] - shift
        base = jnp.where((base >= 0) & (base < chan_dev), base, -(1 << 20))
        hit = (col == row * chan_dev + base) & (row < win_dev)
        blocks.append(jnp.where(hit, 1.0, 0.0))
    picker = jnp.concatenate(blocks, axis=0).astype(jnp.bfloat16)
    picked = jnp.dot(picker, x_ref[...], preferred_element_type=jnp.float32)
    o_ref[...] = picked.astype(jnp.bfloat16).reshape(o_ref.shape)


def pack_kernel(x_ref, o_ref):
    row = lax.broadcasted_iota(jnp.int32, (512, 512), 0)
    col = lax.broadcasted_iota(jnp.int32, (512, 512), 1)
    src = (row % 4) * 128 + (row // 16) * 4 + (row // 4) % 4
    perm = jnp.where(col == src, 1.0, 0.0).astype(jnp.bfloat16)
    for t in range(o_ref.shape[1] // 16):
        got = jnp.dot(perm, x_ref[t * 512:(t + 1) * 512, :], preferred_element_type=jnp.float32)
        o_ref[:, t * 16:(t + 1) * 16, :] = got.astype(jnp.bfloat16).reshape(
            o_ref.shape[0], 16, x_ref.shape[1]
        )


def same_channel():
    a = lax.broadcasted_iota(jnp.int32, (LANES, LANES), 0)
    b = lax.broadcasted_iota(jnp.int32, (LANES, LANES), 1)
    return jnp.where((a // 4) % 4 == (b // 4) % 4, 1.0, 0.0)


LAG_CHUNK = 64


def weighted_stack(c_ref, weights, acc_ref):
    blocks = weights.shape[0]
    for k in range(L // LAG_CHUNK):
        lags = slice(k * LAG_CHUNK, (k + 1) * LAG_CHUNK)
        acc = jnp.zeros((LAG_CHUNK, LANES), jnp.float32)
        for b in range(blocks):
            acc += weights[b:b + 1, :] * c_ref[0, lags, b * LANES:(b + 1) * LANES].astype(jnp.float32)
        acc_ref[lags, :] = acc
    group = same_channel()
    numer = jnp.dot(acc_ref[...], group, precision=HIGHEST, preferred_element_type=jnp.float32)
    weight_sum = jnp.broadcast_to(jnp.sum(weights, axis=0, keepdims=True), (8, LANES))
    denom = jnp.dot(weight_sum, group, precision=HIGHEST, preferred_element_type=jnp.float32)
    return numer / denom[0:1, :]


def residuals(c_ref, stack_ref, r_ref):
    blocks = r_ref.shape[1]
    for b in range(blocks):
        total = jnp.zeros((8, LANES), jnp.float32)
        for k in range(L // LAG_CHUNK):
            lags = slice(k * LAG_CHUNK, (k + 1) * LAG_CHUNK)
            d = c_ref[0, lags, b * LANES:(b + 1) * LANES].astype(jnp.float32) - stack_ref[lags, :]
            total += jnp.sum((d * d).reshape(LAG_CHUNK // 8, 8, LANES), axis=0)
        r_ref[0, b:b + 1, :] = jnp.sum(total, axis=0, keepdims=True) * (1.0 / L)


def finish_residuals(step, last, mask_ref, c_ref, acc_ref, r_ref, part_ref, sum_ref):
    residuals(c_ref, acc_ref, r_ref)
    part = jnp.sum(mask_ref[...] * r_ref[0], axis=0, keepdims=True)

    @pl.when(step == 0)
    def _():
        sum_ref[...] = jnp.zeros_like(sum_ref)

    sum_ref[...] += jnp.broadcast_to(part, sum_ref.shape)

    @pl.when(step == last)
    def _():
        part_ref[...] = jnp.broadcast_to(sum_ref[0:1, :], part_ref.shape)


def correlate_kernel(
    ids_ref, a_ref, x_ref, y_ref, inv_ref, mask_ref, c_ref, r_ref, part_ref, cross_ref, acc_ref, sum_ref
):
    step = pl.program_id(0)
    freq_count = a_ref.shape[1] // 2
    low = lax.broadcasted_iota(jnp.int32, (8, a_ref.shape[1]), 0) < 4

    def fill(s_ref):
        def one(j, carry):
            src = s_ref[0, j].astype(jnp.float32)
            first, last = src[0:8], src[8:16]
            turned = pltpu.roll(first, 4, 0)
            tiles = (
                jnp.where(low, first, turned),
                jnp.where(low, turned, first),
                jnp.where(low, last, pltpu.roll(last, 4, 0)),
            )
            for t in range(3):
                rows = pl.ds(pl.multiple_of(j * 48 + t * 16, 16), 16)
                chan = a_ref[rows, :].astype(jnp.float32)
                tile = jnp.concatenate([tiles[t], tiles[t]], axis=0)
                a, b = tile[:, :freq_count], tile[:, freq_count:]
                u, v = chan[:, :freq_count], chan[:, freq_count:]
                cross_ref[rows, :freq_count] = (a * u + b * v).astype(jnp.bfloat16)
                cross_ref[rows, freq_count:] = (b * u - a * v).astype(jnp.bfloat16)
            return carry

        lax.fori_loop(0, s_ref.shape[1], one, 0, unroll=2)

    @pl.when(step < 4)
    def _():
        fill(x_ref)

    @pl.when(step >= 4)
    def _():
        fill(y_ref)

    for n in range(a_ref.shape[0] // 256):
        got = lax.dot_general(
            inv_ref[...], cross_ref[n * 256:(n + 1) * 256, :], NT, preferred_element_type=jnp.float32
        )
        c_ref[0, :, n * 256:(n + 1) * 256] = got.astype(jnp.bfloat16)
    acc_ref[...] = weighted_stack(c_ref, mask_ref[...], acc_ref)
    finish_residuals(step, pl.num_programs(0) - 1, mask_ref, c_ref, acc_ref, r_ref, part_ref, sum_ref)


def next_weights(total, mask, r, pairs):
    spread = total / (pairs * jnp.sum(mask) * (1.0 / Q)) + epsilon
    return mask * (degrees + 1.0) / (degrees + r / spread)


def iterate_kernel(pairs, all_ref, mask_ref, r_in_ref, c_ref, r_ref, part_ref, acc_ref, sum_ref):
    step = pl.program_id(0)
    weights = next_weights(jnp.sum(all_ref[...]), mask_ref[...], r_in_ref[0], pairs)
    acc_ref[...] = weighted_stack(c_ref, weights, acc_ref)
    finish_residuals(step, pl.num_programs(0) - 1, mask_ref, c_ref, acc_ref, r_ref, part_ref, sum_ref)


def spectrum_kernel(pairs, all_ref, mask_ref, r_in_ref, c_ref, table_ref, o_ref, acc_ref, all_stack_ref):
    step = pl.program_id(0)
    weights = next_weights(jnp.sum(all_ref[...]), mask_ref[...], r_in_ref[0], pairs)
    stack = weighted_stack(c_ref, weights, acc_ref)
    lane = lax.broadcasted_iota(jnp.int32, (L, LANES), 1)
    mine = jnp.where(lane // 16 == step, stack, 0.0)

    @pl.when(step == 0)
    def _():
        all_stack_ref[...] = mine

    @pl.when(step > 0)
    def _():
        all_stack_ref[...] += mine

    @pl.when(step == pl.num_programs(0) - 1)
    def _():
        both = jnp.dot(
            table_ref[...], all_stack_ref[...], precision=HIGHEST, preferred_element_type=jnp.float32
        )
        freq_count = table_ref.shape[0] // 2
        part = lax.broadcasted_iota(jnp.int32, (freq_count, LANES), 1) % 4
        o_ref[...] = jnp.where(part == 0, both[:freq_count], jnp.where(part == 1, both[freq_count:], 0.0))


def beam_kernel(gain, x_ref, cos_ref, sin_ref, fine_cos_ref, fine_sin_ref, o_ref):
    x = x_ref[...]
    yc = lax.dot_general(x, cos_ref[...], TN, precision=HIGHEST, preferred_element_type=jnp.float32)
    ys = lax.dot_general(x, sin_ref[...], TN, precision=HIGHEST, preferred_element_type=jnp.float32)
    c, s = fine_cos_ref[...], fine_sin_ref[...]
    u = yc * c - ys * s
    v = ys * c + yc * s
    rows = o_ref.shape[0]
    out = lax.broadcasted_iota(jnp.int32, (rows, LANES), 0)
    lane = lax.broadcasted_iota(jnp.int32, (rows, LANES), 1)
    same = lane // 16 == out // 2
    imag, part = out % 2, lane % 4
    pick_u = jnp.where(same & (part == imag), 1.0, 0.0)
    pick_v = jnp.where(same & (part == 0) & (imag == 1), 1.0, 0.0) - jnp.where(
        same & (part == 1) & (imag == 0), 1.0, 0.0
    )
    beams = jnp.dot(pick_u, u, precision=HIGHEST, preferred_element_type=jnp.float32) + jnp.dot(
        pick_v, v, precision=HIGHEST, preferred_element_type=jnp.float32
    )
    o_ref[...] = beams * gain


def cos_sin(freq_id, chan_ids, slow_count, modulus):
    slow_ids = jnp.arange(slow_count, dtype=jnp.int32) - slow_count // 2
    phase_ids = jnp.mod((freq_id * chan_ids)[:, None] * slow_ids[None, :], modulus)
    angles = 2.0 * math.pi / modulus * phase_ids.astype(jnp.float32)
    return jnp.cos(angles), jnp.sin(angles)


def full(shape):
    return pl.BlockSpec(shape, lambda *_: (0,) * len(shape))


def by_source(shape):
    return pl.BlockSpec((1,) + shape, lambda s, *_: (s,) + (0,) * len(shape))


def body(spectra, sources, valid):
    win_dev, chan_dev, width = spectra.shape
    freq_count = width // 2
    source_total = sources.shape[0]
    n_win = lax.axis_size("win")
    n_ch = lax.axis_size("ch")
    n_all = n_win * n_ch
    chans = chan_dev * n_ch
    pairs = float(source_total * chans)
    ch = lax.axis_index("ch")
    y, core = ch // 2, ch % 2
    inverse_np, forward_np = tables(freq_count, L)
    flat = spectra.reshape(win_dev * chan_dev, width)
    rows_dev = win_dev * Q
    rows = n_win * rows_dev
    blocks = rows // LANES

    ids = jnp.concatenate([sources.astype(jnp.int32), (ch * chan_dev).astype(jnp.int32)[None]])
    picked = pl.pallas_call(
        pick_kernel,
        grid_spec=pltpu.PrefetchScalarGridSpec(
            num_scalar_prefetch=1,
            grid=(1,),
            in_specs=[full(flat.shape)],
            out_specs=full((source_total, 16, width)),
        ),
        out_shape=jax.ShapeDtypeStruct((source_total, 16, width), jnp.bfloat16),
        name="pick",
    )(ids, flat)
    got = lax.all_to_all(picked, "ch", 0, 0, tiled=True)
    own = jnp.sum(got.astype(jnp.float32), axis=0)
    mask_row = jnp.pad(valid.astype(jnp.float32), (0, width - win_dev))
    own = jnp.where(jnp.arange(16)[:, None] == win_dev, mask_row[None], own).astype(jnp.bfloat16)
    own = lax.all_to_all(jnp.broadcast_to(own[None], (n_win, 16, width)), "win", 0, 0, tiled=True)

    def turn(d):
        return [(i * 2 + c, ((i + d) % 4) * 2 + c) for i in range(n_ch // 2) for c in range(2)]

    mine = jnp.stack([own] + [lax.ppermute(own, "ch", turn(d)) for d in (1, 2, 3)])
    theirs = lax.ppermute(mine, "ch", [(i, i ^ 1) for i in range(n_ch)])
    steps = jnp.arange(4, dtype=jnp.int32)
    slot_y = 2 * ((y - steps) % 4)
    slots = jnp.concatenate([slot_y + core, slot_y + 1 - core]).astype(jnp.int32)
    mask = own[:, win_dev, :win_dev].astype(jnp.float32).reshape(n_win, win_dev // 4, 1, 4)
    mask = jnp.broadcast_to(mask, (n_win, win_dev // 4, Q, 4)).reshape(blocks, LANES)

    packed = pl.pallas_call(
        pack_kernel,
        out_shape=jax.ShapeDtypeStruct((n_win, rows_dev, width), jnp.bfloat16),
        name="pack",
    )(flat)
    moved = lax.all_to_all(packed, "win", 0, 0, tiled=True).reshape(rows, width)

    corr_shape = jax.ShapeDtypeStruct((source_total, L, rows), jnp.bfloat16)
    r_shape = jax.ShapeDtypeStruct((source_total, blocks, LANES), jnp.float32)
    part_shape = jax.ShapeDtypeStruct((n_all, LANES), jnp.float32)
    slot = lambda s, ids_ref: (ids_ref[s], 0, 0)
    corr, r, part = pl.pallas_call(
        correlate_kernel,
        grid_spec=pltpu.PrefetchScalarGridSpec(
            num_scalar_prefetch=1,
            grid=(source_total,),
            in_specs=[
                full((rows, width)),
                pl.BlockSpec((1, n_win, 16, width), lambda s, _: (jnp.minimum(s, 3), 0, 0, 0)),
                pl.BlockSpec((1, n_win, 16, width), lambda s, _: (jnp.maximum(s - 4, 0), 0, 0, 0)),
                full((L, width)),
                full((blocks, LANES)),
            ],
            out_specs=[
                pl.BlockSpec((1, L, rows), slot),
                pl.BlockSpec((1, blocks, LANES), slot),
                full((n_all, LANES)),
            ],
            scratch_shapes=[
                pltpu.VMEM((rows, width), jnp.bfloat16),
                pltpu.VMEM((L, LANES), jnp.float32),
                pltpu.VMEM((8, LANES), jnp.float32),
            ],
        ),
        out_shape=[corr_shape, r_shape, part_shape],
        name="correlate",
    )(slots, moved, mine, theirs, jnp.asarray(inverse_np, jnp.bfloat16), mask)

    for _ in range(ITERS - 1):
        parts = lax.all_to_all(part, ("win", "ch"), 0, 0, tiled=True)
        r, part = pl.pallas_call(
            lambda *refs: iterate_kernel(pairs, *refs),
            grid=(source_total,),
            in_specs=[
                full((n_all, LANES)),
                full((blocks, LANES)),
                by_source((blocks, LANES)),
                by_source((L, rows)),
            ],
            out_specs=[by_source((blocks, LANES)), full((n_all, LANES))],
            out_shape=[r_shape, part_shape],
            scratch_shapes=[pltpu.VMEM((L, LANES), jnp.float32), pltpu.VMEM((8, LANES), jnp.float32)],
            name="iterate",
        )(parts, mask, r, corr)

    sums = jnp.sum(lax.all_to_all(part[:n_ch], "ch", 0, 0, tiled=True), axis=(0, 1))
    home = jnp.swapaxes(r.reshape(source_total, n_win, rows_dev), 0, 1)
    tail = jnp.broadcast_to(sums, (n_win, source_total, LANES - rows_dev))
    back = lax.all_to_all(jnp.concatenate([home, tail], axis=2), "win", 0, 0, tiled=True)
    total = jnp.sum(back[:, 0, rows_dev])
    parts = jnp.zeros((8, LANES), jnp.float32).at[0, 0].set(total)

    spectrum = pl.pallas_call(
        lambda *refs: spectrum_kernel(pairs, *refs),
        grid=(source_total,),
        in_specs=[
            full((8, LANES)),
            full((blocks, LANES)),
            by_source((blocks, LANES)),
            by_source((L, rows)),
            full(forward_np.shape),
        ],
        out_specs=full((freq_count, LANES)),
        out_shape=jax.ShapeDtypeStruct((freq_count, LANES), jnp.float32),
        scratch_shapes=[pltpu.VMEM((L, LANES), jnp.float32), pltpu.VMEM((L, LANES), jnp.float32)],
        name="spectrum",
    )(parts, mask, r, corr, jnp.asarray(forward_np))
    pieces = lax.all_to_all(spectrum, ("win", "ch"), 0, 0, tiled=True)

    freq_id = lax.axis_index("win") * n_ch + ch
    modulus = 4 * freq_count * P_SIZE
    device = jnp.arange(n_all, dtype=jnp.int32)
    coarse = (device % n_ch) * chan_dev + (device // n_ch) * Q
    cosines, sines = cos_sin(freq_id, coarse, P_SIZE, modulus)
    fine_cos, fine_sin = cos_sin(freq_id, (jnp.arange(LANES, dtype=jnp.int32) // 4) % Q, P_SIZE, modulus)
    beamed = pl.pallas_call(
        lambda *refs: beam_kernel(chans ** (-0.5), *refs),
        out_shape=jax.ShapeDtypeStruct((source_total * 2, P_SIZE), jnp.float32),
        name="beam",
    )(pieces, cosines, sines, fine_cos, fine_sin)

    window_count = jnp.sum(mask) * (1.0 / Q)
    spread_sq = total / (pairs * window_count) + epsilon
    mine_mask = valid.astype(jnp.float32)
    residual = back[:, :, :rows_dev].reshape(n_win, source_total, win_dev // 4, Q, 4)
    residual = residual.transpose(2, 4, 1, 0, 3).reshape(win_dev, source_total, chan_dev)
    weights = mine_mask[:, None, None] * (degrees + 1.0) / (degrees + residual / spread_sq)
    return (weights, beamed.reshape(1, source_total, 2, P_SIZE))


def solution(mesh):
    return jax.shard_map(
        body,
        mesh=mesh,
        in_specs=(P("win", "ch", None), P(), P("win")),
        out_specs=(P("win", None, "ch"), P(("win", "ch"), None, None, None)),
        check_vma=False,
    )
```

time: 1040 us -> 231 us (0.22)
  blocking collectives: 482 us -> 0 us
  waiting for transfers between devices: 394 us -> 88.4 us
  Pallas kernels: 0 us -> 58.3 us
  other arithmetic: 68.5 us -> 10.3 us
  starting transfers between devices: 10 us -> 59.2 us
  matrix products: 45.6 us -> 0 us
  between operations: 16.7 us -> 2.13 us
    psum x7 -> x0, blocking collectives: 482 us -> none  [the longest x3 237 us: body(): lax.psum(jnp.sum(window_mask[:, None, None] * residual_sq), ('win', 'ch'))]
    psum x5 -> x0, waiting for transfers between devices: 389 us -> none  [the longest x3 240 us: body(): numer, denom = lax.psum((numer_local, denom_local), 'win')]
    all_to_all x1 -> x8, waiting for transfers between devices: 4.85 us -> 65.7 us  [the longest x2 22.5 us: body(): parts = lax.all_to_all(part, ('win', 'ch'), 0, 0, tiled=True)]
    pallas_call x0 -> x7, Pallas kernels: none -> 58.3 us  [the longest x2 19.7 us: body(): pl.pallas_call(lambda *refs: iterate_kernel(pairs, *refs), grid=(source_t...]
    dot_general x18 -> x0, matrix products: 45.6 us -> none  [the longest x1 9.22 us: beam_one(): jnp.dot(spectrum[0], sines, precision=highest, preferred_element_type=jnp...]
    all_to_all x1 -> x8, starting transfers between devices: 9.8 us -> 54.4 us  [the longest x2 15.5 us: body(): parts = lax.all_to_all(part, ('win', 'ch'), 0, 0, tiled=True)]
    reduce_sum x13 -> x4, other arithmetic: 38.1 us -> 2.06 us  [the longest x1 0.73 us: body(): total = jnp.sum(back[:, 0, rows_dev])]
    ppermute x0 -> x4, waiting for transfers between devices: none -> 22.8 us  [the longest x3 22.7 us: body(): lax.ppermute(own, 'ch', turn(d))]
  transfers between devices with their start and end apart: 6 -> 12, of which waited for: 6 -> 11; matrix products, arithmetic and copies ran while one was open for 0% -> 5% of each run, Pallas kernels for 0% -> 2%
where the time goes in v1:
time: 231 us; the launch traced here: 230 us
  waiting for transfers between devices  88.4 us (38%)
  starting transfers between devices  59.2 us (26%)
  Pallas kernels  58.3 us (25%)
  local copies, waits for them, and re-layouts  11.3 us (5%)
  other arithmetic  10.3 us (4%)
    ppermute x3, waiting for transfers between devices, body(): lax.ppermute(own, 'ch', turn(d))  22.7 us
    all_to_all x2, waiting for transfers between devices, body(): parts = lax.all_to_all(part, ('win', 'ch'), 0, 0, tiled=True)  22.5 us
    pallas_call x2, Pallas kernels, body(): pl.pallas_call(lambda *refs: iterate_kernel(pairs, *refs), grid=(source_t...  19.7 us
    pallas_call x1, Pallas kernels, body(): pl.pallas_call(correlate_kernel, grid_spec=pltpu.PrefetchScalarGridSpec(n...  19.4 us
    all_to_all x2, starting transfers between devices, body(): parts = lax.all_to_all(part, ('win', 'ch'), 0, 0, tiled=True)  15.5 us
    all_to_all x1, waiting for transfers between devices, body(): lax.all_to_all(jnp.broadcast_to(own[None], (n_win, 16, width)), 'win', 0,...  11 us
    all_to_all x1, waiting for transfers between devices, body(): pieces = lax.all_to_all(spectrum, ('win', 'ch'), 0, 0, tiled=True)  10.8 us
    all_to_all x1, starting transfers between devices, body(): lax.all_to_all(jnp.broadcast_to(own[None], (n_win, 16, width)), 'win', 0,...  10.5 us
  transfers between devices with their start and end apart: 12, of which 11 were waited for; matrix products, arithmetic and copies ran while one was open for 5% of the time, Pallas kernels for 2%

profile of v1, /device:TPU:1, one launch (start us, length us, event | category | flops | bytes accessed | tf_op | source)
XLA Modules:
  0.0 229.6 jit_solution(10395738498183703915)
XLA Ops:
  0.6 1.2 pad_add_fusion.1.ids_ref
  1.9 3.1 %pick.1 = bf16[8,16,512]{2,1,0:T(8,128)(2,1)} custom-call(s32[9]{0:T(128)} %pad_add_fusion.1.ids_ref, bf16[1536,512]{1,0:T(8,128)(2,1)} %bitcast.29), custom_call_target="tpu_custom_call" | custom-call | tf_op jit(solution)/shard_map/pick/pallas_call | solution.py:255
  5.0 6.5 %all-to-all-start.1 = ((bf16[8,16,512]{2,1,0:T(8,128)(2,1)}), bf16[8,16,512]{2,1,0:T(8,128)(2,1)S(1)}, u32[]{:S(2)}, u32[]{:S(2)}) async-start(bf16[8,16,512]{2,1,0:T(8,128)(2,1)} %pick.1), calls=%async_computation.1 | async-start | bytes 262144 | tf_op jit(solution)/shard_map/all_to_all | solution.py:266
  11.5 0.7 convert_element_type.32
  12.1 4.6 %all-to-all-done.1 = bf16[8,16,512]{2,1,0:T(8,128)(2,1)S(1)} async-done(((bf16[8,16,512]{2,1,0:T(8,128)(2,1)}), bf16[8,16,512]{2,1,0:T(8,128)(2,1)S(1)}, u32[]{:S(2)}, u32[]{:S(2)}) %all-to-all-start.1) | async-done | bytes 131104 | tf_op jit(solution)/shard_map/all_to_all | solution.py:266
  16.8 0.9 broadcast_in_dim.25
  17.7 10.5 %all-to-all-start.2 = ((bf16[32,16,512]{2,1,0:T(8,128)(2,1)}), bf16[32,16,512]{2,1,0:T(8,128)(2,1)S(1)}, u32[]{:S(2)}, u32[]{:S(2)}) async-start(bf16[32,16,512]{2,1,0:T(8,128)(2,1)} %broadcast_in_dim.25), calls=%async_computation.2 | async-start | bytes 1048576 | tf_op jit(solution)/shard_map/all_to_all | solution.py:270
  28.2 3.6 %pack.1 = bf16[32,48,512]{2,1,0:T(8,128)(2,1)} custom-call(bf16[1536,512]{1,0:T(8,128)(2,1)} %bitcast.30), custom_call_target="tpu_custom_call" | custom-call | tf_op jit(solution)/shard_map/pack/pallas_call | solution.py:283
  31.8 11.0 %all-to-all-done.2 = bf16[32,16,512]{2,1,0:T(8,128)(2,1)S(1)} async-done(((bf16[32,16,512]{2,1,0:T(8,128)(2,1)}), bf16[32,16,512]{2,1,0:T(8,128)(2,1)S(1)}, u32[]{:S(2)}, u32[]{:S(2)}) %all-to-all-start.2) | async-done | bytes 524320 | tf_op jit(solution)/shard_map/all_to_all | solution.py:270
  42.8 7.4 %all-to-all-start = ((bf16[32,48,512]{2,1,0:T(8,128)(2,1)}), bf16[32,48,512]{2,1,0:T(8,128)(2,1)}, u32[]{:S(2)}, u32[]{:S(2)}) async-start(bf16[32,48,512]{2,1,0:T(8,128)(2,1)} %pack.1), calls=%async_computation | async-start | bytes 3145728 | tf_op jit(solution)/shard_map/all_to_all | solution.py:288
  50.6 1.8 collective-permute-start.1
  52.3 0.8 collective-permute-start.2
  53.1 11.0 %collective-permute-done = bf16[32,16,512]{2,1,0:T(8,128)(2,1)S(1)} collective-permute-done((bf16[32,16,512]{2,1,0:T(8,128)(2,1)S(1)}, bf16[32,16,512]{2,1,0:T(8,128)(2,1)S(1)}, u32[]{:S(2)}, u32[]{:S(2)}) %collective-permute-start) | collective-permute-done | bytes 524320 | tf_op jit(solution)/shard_map/ppermute | solution.py:275
  64.1 10.0 %collective-permute-done.1 = bf16[32,16,512]{2,1,0:T(8,128)(2,1)S(1)} collective-permute-done((bf16[32,16,512]{2,1,0:T(8,128)(2,1)S(1)}, bf16[32,16,512]{2,1,0:T(8,128)(2,1)S(1)}, u32[]{:S(2)}, u32[]{:S(2)}) %collective-permute-start.1) | collective-permute-done | bytes 524320 | tf_op jit(solution)/shard_map/ppermute | solution.py:275
  74.0 1.8 collective-permute-done.2
  76.1 1.9 collective-permute-start.3
  78.1 0.6 pad_add_fusion.ids_ref
  78.8 0.8 reshape.170.mask_ref.refs_1_
  79.6 7.4 %all-to-all-done = bf16[32,48,512]{2,1,0:T(8,128)(2,1)} async-done(((bf16[32,48,512]{2,1,0:T(8,128)(2,1)}), bf16[32,48,512]{2,1,0:T(8,128)(2,1)}, u32[]{:S(2)}, u32[]{:S(2)}) %all-to-all-start) | async-done | bytes 1572896 | tf_op jit(solution)/shard_map/all_to_all | solution.py:288
  87.0 19.4 %correlate.1 = (bf16[8,256,1536]{2,1,0:T(8,128)(2,1)}, f32[8,12,128]{2,1,0:T(8,128)}, f32[256,128]{1,0:T(8,128)}) custom-call(s32[8]{0:T(128)} %pad_add_fusion.ids_ref, bf16[1536,512]{1,0:T(8,128)(2,1)} %bitcast.1.a_ref, bf16[4,32,16,512]{3,2,1,0:T(8,128)(2,1)} %copy-done, bf16[4,32,16,512]{3,2,1,0:T(8,128)(2,1)} %collective-permute-done.3.y_ref, ...), custom_call_target="tpu_custom_call" | custom-call | tf_op jit(solution)/shard_map/correlate/pallas_call | solution.py:294
  106.4 9.9 %all-to-all-start.3 = ((f32[256,1,128]{2,1,0:T(1,128)}), f32[256,1,128]{2,1,0:T(1,128)S(1)}, u32[]{:S(2)}, u32[]{:S(2)}) async-start(f32[256,1,128]{2,1,0:T(1,128)} %bitcast.43), calls=%async_computation.3 | async-start | bytes 262144 | tf_op jit(solution)/shard_map/all_to_all | solution.py:322
  116.4 12.8 %all-to-all-done.3 = f32[256,1,128]{2,1,0:T(1,128)S(1)} async-done(((f32[256,1,128]{2,1,0:T(1,128)}), f32[256,1,128]{2,1,0:T(1,128)S(1)}, u32[]{:S(2)}, u32[]{:S(2)}) %all-to-all-start.3) | async-done | bytes 131104 | tf_op jit(solution)/shard_map/all_to_all | solution.py:322
  129.2 0.6 copy-done.1
  129.9 9.9 %iterate.2 = (f32[8,12,128]{2,1,0:T(8,128)}, f32[256,128]{1,0:T(8,128)}) custom-call(f32[256,128]{1,0:T(8,128)} %bitcast.35, f32[12,128]{1,0:T(8,128)} %reshape.170.mask_ref.refs_1_, f32[8,12,128]{2,1,0:T(8,128)} %get-tuple-element.22.refs_2_, bf16[8,256,1536]{2,1,0:T(8,128)(2,1)} %get-tuple-element.23.refs_3_), custom_call_target="tpu_custom_call" | custom-call | tf_op jit(solution)/shard_map/iterate/pallas_call | solution.py:323
  139.7 5.5 %all-to-all-start.4 = ((f32[256,1,128]{2,1,0:T(1,128)}), f32[256,1,128]{2,1,0:T(1,128)S(1)}, u32[]{:S(2)}, u32[]{:S(2)}) async-start(f32[256,1,128]{2,1,0:T(1,128)} %bitcast.44), calls=%async_computation.4 | async-start | bytes 262144 | tf_op jit(solution)/shard_map/all_to_all | solution.py:322
  145.3 3.3 %fusion.6 = (f32[256,512]{1,0:T(8,128)}, f32[256,512]{1,0:T(8,128)}) fusion(s32[512]{0:T(512)S(1)} %iota_add_fusion, s32[256]{0:T(256)S(1)} %fusion.15), kind=kLoop, calls=%fused_computation.18 | loop fusion | flops 1835008 | bytes 1051648 | tf_op jit(solution)/shard_map/sin | solution.py:226
  148.6 9.7 %all-to-all-done.4 = f32[256,1,128]{2,1,0:T(1,128)S(1)} async-done(((f32[256,1,128]{2,1,0:T(1,128)}), f32[256,1,128]{2,1,0:T(1,128)S(1)}, u32[]{:S(2)}, u32[]{:S(2)}) %all-to-all-start.4) | async-done | bytes 131104 | tf_op jit(solution)/shard_map/all_to_all | solution.py:322
  158.3 0.7 copy-done.2
  158.9 9.9 %iterate.3 = (f32[8,12,128]{2,1,0:T(8,128)}, f32[256,128]{1,0:T(8,128)}) custom-call(f32[256,128]{1,0:T(8,128)} %bitcast.37, f32[12,128]{1,0:T(8,128)} %reshape.170.mask_ref.refs_1_, f32[8,12,128]{2,1,0:T(8,128)} %get-tuple-element.25.refs_2_, bf16[8,256,1536]{2,1,0:T(8,128)(2,1)} %get-tuple-element.23.refs_3_), custom_call_target="tpu_custom_call" | custom-call | tf_op jit(solution)/shard_map/iterate/pallas_call | solution.py:323
  168.8 1.3 slice.29
  170.1 3.7 %all-to-all-start.5 = ((f32[8,1,128]{2,1,0:T(1,128)}), f32[8,1,128]{2,1,0:T(1,128)S(1)}, u32[]{:S(2)}, u32[]{:S(2)}) async-start(f32[8,1,128]{2,1,0:T(1,128)} %bitcast.15), calls=%async_computation.5 | async-start | bytes 8192 | tf_op jit(solution)/shard_map/all_to_all | solution.py:338
  173.7 1.9 fusion.8
  175.6 0.9 reshape.171
  176.7 1.6 all-to-all-done.5
  178.3 0.6 reduce_sum.37
  178.9 1.3 concatenate.13.clone
  180.2 3.9 %all-to-all-start.6 = ((f32[32,8,128]{2,1,0:T(8,128)}), f32[32,8,128]{2,1,0:T(8,128)S(1)}, u32[]{:S(2)}, u32[]{:S(2)}) async-start(f32[32,8,128]{2,1,0:T(8,128)} %concatenate.13.clone), calls=%async_computation.6 | async-start | bytes 262144 | tf_op jit(solution)/shard_map/all_to_all | solution.py:341
  184.1 0.7 broadcast_reduce_fusion
  185.4 7.8 %all-to-all-done.6 = f32[32,8,128]{2,1,0:T(8,128)S(1)} async-done(((f32[32,8,128]{2,1,0:T(8,128)}), f32[32,8,128]{2,1,0:T(8,128)S(1)}, u32[]{:S(2)}, u32[]{:S(2)}) %all-to-all-start.6) | async-done | bytes 131104 | tf_op jit(solution)/shard_map/all_to_all | solution.py:341
  193.2 0.7 slice_reduce_fusion
  194.0 1.2 scatter.4.refs_0_
  195.2 9.3 %spectrum.1 = f32[256,128]{1,0:T(8,128)} custom-call(f32[8,128]{1,0:T(8,128)} %scatter.4.refs_0_, f32[12,128]{1,0:T(8,128)} %reshape.170.mask_ref.refs_1_, f32[8,12,128]{2,1,0:T(8,128)} %get-tuple-element.26.refs_2_, bf16[8,256,1536]{2,1,0:T(8,128)(2,1)} %get-tuple-element.23.refs_3_, f32[512,256]{1,0:T(8,128)} %constant.177.clone.refs_4_), custom_call_target="tpu_custom_call" | custom-call | tf_op jit(solution)/shard_map/spectrum/pallas_call | solution.py:345
  204.5 7.1 %all-to-all-start.7 = ((f32[256,1,128]{2,1,0:T(1,128)}), f32[256,1,128]{2,1,0:T(1,128)S(1)}, u32[]{:S(2)}, u32[]{:S(2)}) async-start(f32[256,1,128]{2,1,0:T(1,128)} %bitcast.36), calls=%async_computation.7 | async-start | bytes 262144 | tf_op jit(solution)/shard_map/all_to_all | solution.py:360
  212.9 0.9 copy.32
  213.7 10.8 %all-to-all-done.7 = f32[256,1,128]{2,1,0:T(1,128)S(1)} async-done(((f32[256,1,128]{2,1,0:T(1,128)}), f32[256,1,128]{2,1,0:T(1,128)S(1)}, u32[]{:S(2)}, u32[]{:S(2)}) %all-to-all-start.7) | async-done | bytes 131104 | tf_op jit(solution)/shard_map/all_to_all | solution.py:360
  224.5 0.7 copy-done.3
  225.2 3.1 %beam.1 = f32[16,512]{1,0:T(8,128)} custom-call(f32[256,128]{1,0:T(8,128)} %bitcast.39, f32[256,512]{1,0:T(8,128)} %get-tuple-element.35.refs_1_, f32[256,512]{1,0:T(8,128)} %get-tuple-element.34.refs_2_, f32[128,512]{1,0:T(8,128)} %get-tuple-element.37.refs_3_, f32[128,512]{1,0:T(8,128)} %get-tuple-element.36.refs_4_), custom_call_target="tpu_custom_call" | custom-call | tf_op jit(solution)/shard_map/beam/pallas_call | solution.py:368
  228.3 1.4 reshape.173
  (27 shorter events, 1.7 us)
Async XLA Ops:
  5.0 11.7 %all-to-all-start.1 = ((bf16[8,16,512]{2,1,0:T(8,128)(2,1)}), bf16[8,16,512]{2,1,0:T(8,128)(2,1)S(1)}, u32[]{:S(2)}, u32[]{:S(2)}) async-start(bf16[8,16,512]{2,1,0:T(8,128)(2,1)} %pick.1), calls=%async_computation.1 | async-start | bytes 262144 | tf_op jit(solution)/shard_map/all_to_all | solution.py:266
  17.7 25.1 %all-to-all-start.2 = ((bf16[32,16,512]{2,1,0:T(8,128)(2,1)}), bf16[32,16,512]{2,1,0:T(8,128)(2,1)S(1)}, u32[]{:S(2)}, u32[]{:S(2)}) async-start(bf16[32,16,512]{2,1,0:T(8,128)(2,1)} %broadcast_in_dim.25), calls=%async_computation.2 | async-start | bytes 1048576 | tf_op jit(solution)/shard_map/all_to_all | solution.py:270
  42.8 44.2 %all-to-all-start = ((bf16[32,48,512]{2,1,0:T(8,128)(2,1)}), bf16[32,48,512]{2,1,0:T(8,128)(2,1)}, u32[]{:S(2)}, u32[]{:S(2)}) async-start(bf16[32,48,512]{2,1,0:T(8,128)(2,1)} %pack.1), calls=%async_computation | async-start | bytes 3145728 | tf_op jit(solution)/shard_map/all_to_all | solution.py:288
  50.2 13.9 %collective-permute-start = (bf16[32,16,512]{2,1,0:T(8,128)(2,1)S(1)}, bf16[32,16,512]{2,1,0:T(8,128)(2,1)S(1)}, u32[]{:S(2)}, u32[]{:S(2)}) collective-permute-start(bf16[32,16,512]{2,1,0:T(8,128)(2,1)S(1)} %all-to-all-done.2), channel_id=1, source_target_pairs={{0,2},{1,3},{2,4},{3,5},{4,6},{5,7},{6,0},{7,1},{8,10},{9,11},{10,... | collective-permute-start | bytes 1572872 | tf_op jit(solution)/shard_map/ppermute | solution.py:275
  50.6 23.5 %collective-permute-start.1 = (bf16[32,16,512]{2,1,0:T(8,128)(2,1)S(1)}, bf16[32,16,512]{2,1,0:T(8,128)(2,1)S(1)}, u32[]{:S(2)}, u32[]{:S(2)}) collective-permute-start(bf16[32,16,512]{2,1,0:T(8,128)(2,1)S(1)} %all-to-all-done.2), channel_id=1, source_target_pairs={{0,4},{1,5},{2,6},{3,7},{4,0},{5,1},{6,2},{7,3},{8,12},{9,13},{10,... | collective-permute-start | bytes 1572872 | tf_op jit(solution)/shard_map/ppermute | solution.py:275
  52.3 23.5 %collective-permute-start.2 = (bf16[32,16,512]{2,1,0:T(8,128)(2,1)S(1)}, bf16[32,16,512]{2,1,0:T(8,128)(2,1)S(1)}, u32[]{:S(2)}, u32[]{:S(2)}) collective-permute-start(bf16[32,16,512]{2,1,0:T(8,128)(2,1)S(1)} %all-to-all-done.2), channel_id=1, source_target_pairs={{0,6},{1,7},{2,0},{3,1},{4,2},{5,3},{6,4},{7,5},{8,14},{9,15},{10,... | collective-permute-start | bytes 1572872 | tf_op jit(solution)/shard_map/ppermute | solution.py:275
  76.1 10.9 %copy-start = (bf16[4,32,16,512]{3,2,1,0:T(8,128)(2,1)}, bf16[4,32,16,512]{3,2,1,0:T(8,128)(2,1)S(1)}, u32[]{:S(2)}) copy-start(bf16[4,32,16,512]{3,2,1,0:T(8,128)(2,1)S(1)} %pad_maximum_fusion.x_ref) | copy-start | bytes 6291460
  76.1 10.9 %collective-permute-start.3 = (bf16[4,32,16,512]{3,2,1,0:T(8,128)(2,1)S(1)}, bf16[4,32,16,512]{3,2,1,0:T(8,128)(2,1)}, u32[]{:S(2)}, u32[]{:S(2)}) collective-permute-start(bf16[4,32,16,512]{3,2,1,0:T(8,128)(2,1)S(1)} %pad_maximum_fusion.x_ref), channel_id=1, source_target_pairs={{0,1},{1,0},{2,3},{3,2},{4,5},{5,4},{6,7},{7,6},{8,9},{9,8},{10,11... | collective-permute-start | bytes 6291464 | tf_op jit(solution)/shard_map/ppermute | solution.py:276
  106.4 22.8 %all-to-all-start.3 = ((f32[256,1,128]{2,1,0:T(1,128)}), f32[256,1,128]{2,1,0:T(1,128)S(1)}, u32[]{:S(2)}, u32[]{:S(2)}) async-start(f32[256,1,128]{2,1,0:T(1,128)} %bitcast.43), calls=%async_computation.3 | async-start | bytes 262144 | tf_op jit(solution)/shard_map/all_to_all | solution.py:322
  129.2 0.7 copy-start.1
  139.7 18.6 %all-to-all-start.4 = ((f32[256,1,128]{2,1,0:T(1,128)}), f32[256,1,128]{2,1,0:T(1,128)S(1)}, u32[]{:S(2)}, u32[]{:S(2)}) async-start(f32[256,1,128]{2,1,0:T(1,128)} %bitcast.44), calls=%async_computation.4 | async-start | bytes 262144 | tf_op jit(solution)/shard_map/all_to_all | solution.py:322
  158.3 0.7 copy-start.2
  158.9 25.1 %copy-start.4 = (s32[12]{0:T(128)S(1)}, s32[12]{0:T(128)}, u32[]{:S(2)}) copy-start(s32[12]{0:T(128)} %param.9) | copy-start | bytes 148
  170.1 8.2 %all-to-all-start.5 = ((f32[8,1,128]{2,1,0:T(1,128)}), f32[8,1,128]{2,1,0:T(1,128)S(1)}, u32[]{:S(2)}, u32[]{:S(2)}) async-start(f32[8,1,128]{2,1,0:T(1,128)} %bitcast.15), calls=%async_computation.5 | async-start | bytes 8192 | tf_op jit(solution)/shard_map/all_to_all | solution.py:338
  180.2 13.0 %all-to-all-start.6 = ((f32[32,8,128]{2,1,0:T(8,128)}), f32[32,8,128]{2,1,0:T(8,128)S(1)}, u32[]{:S(2)}, u32[]{:S(2)}) async-start(f32[32,8,128]{2,1,0:T(8,128)} %concatenate.13.clone), calls=%async_computation.6 | async-start | bytes 262144 | tf_op jit(solution)/shard_map/all_to_all | solution.py:341
  204.5 20.0 %all-to-all-start.7 = ((f32[256,1,128]{2,1,0:T(1,128)}), f32[256,1,128]{2,1,0:T(1,128)S(1)}, u32[]{:S(2)}, u32[]{:S(2)}) async-start(f32[256,1,128]{2,1,0:T(1,128)} %bitcast.36), calls=%async_computation.7 | async-start | bytes 262144 | tf_op jit(solution)/shard_map/all_to_all | solution.py:360
  224.5 0.7 copy-start.3

commit v2 on v1

v2 whole, which is shorter than its diff:
```python
import math

import jax
import jax.numpy as jnp
import numpy as np
from jax import lax
from jax.experimental import pallas as pl
from jax.experimental.pallas import tpu as pltpu
from jax.sharding import PartitionSpec as P

L = 256
P_SIZE = 512
ITERS = 3
Q = 4
LANES = 128
PARAMS = pltpu.CompilerParams(vmem_limit_bytes=20 << 20)
BIG = pltpu.CompilerParams(vmem_limit_bytes=59 << 20)

degrees = 3.0
epsilon = 1e-06
HIGHEST = lax.Precision.HIGHEST
NT = (((1,), (1,)), ((), ()))
TN = (((0,), (0,)), ((), ()))


def tables(freq_count, lag_count):
    freq_ids = np.arange(freq_count, dtype=np.int64)
    delays = np.arange(lag_count, dtype=np.int64) - lag_count // 2
    phase_ids = np.mod(freq_ids[:, None] * delays[None, :], 2 * freq_count)
    angles = np.float32(2.0 * math.pi / (2 * freq_count)) * phase_ids.astype(np.float32)
    cosines = np.cos(angles.astype(np.float64)).astype(np.float32)
    sines = np.sin(angles.astype(np.float64)).astype(np.float32)
    inverse_factor = np.float32(1.0 / math.sqrt(freq_count))
    forward_factor = np.float32(1.0 / math.sqrt(lag_count))
    inverse = np.concatenate([cosines * inverse_factor, -sines * inverse_factor], axis=0)
    forward = np.concatenate([cosines * forward_factor, -sines * forward_factor], axis=0)
    return np.ascontiguousarray(inverse.T), forward


def pick_kernel(sources_ref, x_ref, o_ref):
    rows, count = x_ref.shape[0], o_ref.shape[0]
    chan_dev = 128
    row = lax.broadcasted_iota(jnp.int32, (24, rows), 0)
    col = lax.broadcasted_iota(jnp.int32, (24, rows), 1)
    window = (row // 8) * 4 + row % 4
    shift = lax.axis_index("ch") * chan_dev
    blocks = []
    for s in range(count):
        base = sources_ref[s] - shift
        base = jnp.where((base >= 0) & (base < chan_dev), base, -(1 << 20))
        blocks.append(jnp.where(col == window * chan_dev + base, 1.0, 0.0))
    picker = jnp.concatenate(blocks, axis=0).astype(jnp.bfloat16)
    picked = jnp.dot(picker, x_ref[...], preferred_element_type=jnp.float32).reshape(count, 24, 512)
    low = lax.broadcasted_iota(jnp.int32, (8, LANES), 0) < 4
    for s in range(count):
        for t in range(3):
            tile = picked[s, t * 8:(t + 1) * 8, :]
            pair = [
                jnp.where(low, tile[:, p * 256:p * 256 + 128], tile[:, p * 256 + 128:p * 256 + 256])
                for p in range(2)
            ]
            o_ref[s, t * 16:(t + 1) * 16, :] = jnp.concatenate(pair, axis=0).astype(jnp.bfloat16)


def own_kernel(x_ref, mask_ref, o_ref):
    total = x_ref[0].astype(jnp.float32)
    for g in range(1, x_ref.shape[0]):
        total += x_ref[g].astype(jnp.float32)
    rows = total.shape[0]
    masks = jnp.broadcast_to(mask_ref[...], (8, LANES))
    block = jnp.concatenate([total, masks], axis=0).astype(jnp.bfloat16)
    for j in range(o_ref.shape[0]):
        o_ref[j] = block


def pack_kernel(x_ref, o_ref):
    row = lax.broadcasted_iota(jnp.int32, (512, 512), 0)
    col = lax.broadcasted_iota(jnp.int32, (512, 512), 1)
    src = (row % 4) * 128 + (row // 16) * 4 + (row // 4) % 4
    perm = jnp.where(col == src, 1.0, 0.0).astype(jnp.bfloat16)
    for t in range(o_ref.shape[1] // 16):
        got = jnp.dot(perm, x_ref[t * 512:(t + 1) * 512, :], preferred_element_type=jnp.float32)
        o_ref[:, t * 16:(t + 1) * 16, :] = got.astype(jnp.bfloat16).reshape(
            o_ref.shape[0], 16, x_ref.shape[1]
        )


LAG_CHUNK = 64


def three_terms(x):
    high = x.astype(jnp.bfloat16)
    rest = x - high.astype(jnp.float32)
    middle = rest.astype(jnp.bfloat16)
    low = (rest - middle.astype(jnp.float32)).astype(jnp.bfloat16)
    return high, middle, low


def same_channel():
    a = lax.broadcasted_iota(jnp.int32, (3 * LANES, LANES), 0)
    b = lax.broadcasted_iota(jnp.int32, (3 * LANES, LANES), 1)
    return jnp.where((a // 4) % 4 == (b // 4) % 4, 1.0, 0.0).astype(jnp.bfloat16)


def weighted_sums(c_ref, s, w_rows, terms_ref):
    weights = [w_rows[b:b + 1, :] for b in range(w_rows.shape[0])]
    for k in range(L // LAG_CHUNK):
        lags = slice(k * LAG_CHUNK, (k + 1) * LAG_CHUNK)
        acc = jnp.zeros((LAG_CHUNK, LANES), jnp.float32)
        for b, w in enumerate(weights):
            acc += w * c_ref[s, lags, b * LANES:(b + 1) * LANES].astype(jnp.float32)
        for i, term in enumerate(three_terms(acc)):
            terms_ref[s, lags, i * LANES:(i + 1) * LANES] = term
    weight_sum = jnp.broadcast_to(jnp.sum(w_rows[...], axis=0, keepdims=True), (16, LANES))
    for i, term in enumerate(three_terms(weight_sum)):
        terms_ref[s, L:L + 16, i * LANES:(i + 1) * LANES] = term


def finish_stacks(terms_ref, stack_ref):
    group = same_channel()
    for s in range(terms_ref.shape[0]):
        sums = jnp.dot(terms_ref[s], group, preferred_element_type=jnp.float32)
        stack_ref[s] = sums[:L] * (1.0 / sums[L:L + 1])


def residuals(c_ref, s, stack_ref, r_ref):
    for b in range(r_ref.shape[1]):
        total = jnp.zeros((8, LANES), jnp.float32)
        for k in range(L // LAG_CHUNK):
            lags = slice(k * LAG_CHUNK, (k + 1) * LAG_CHUNK)
            d = c_ref[s, lags, b * LANES:(b + 1) * LANES].astype(jnp.float32) - stack_ref[s, lags, :]
            total += jnp.sum((d * d).reshape(LAG_CHUNK // 8, 8, LANES), axis=0)
        r_ref[s, b:b + 1, :] = jnp.sum(total, axis=0, keepdims=True) * (1.0 / L)


def masked_sum(mask_ref, r_ref):
    return jnp.sum(mask_ref[...][None] * r_ref[...])


def correlate_kernel(
    ids_ref, a_ref, x_ref, inv_ref, c_hbm, r_ref, part_ref, mask_ref, even_ref, odd_ref, c_ref, terms_ref, stack_ref, sems
):
    n_win, rows = x_ref.shape[1], a_ref.shape[0]
    half = a_ref.shape[1] // 2
    rows_dev = rows // n_win
    low = lax.broadcasted_iota(jnp.int32, (8, LANES), 0) < 4

    lane = lax.broadcasted_iota(jnp.int32, (8, LANES), 1)
    pieces = [jnp.zeros((8, LANES), jnp.float32) for _ in range(rows // LANES)]
    for j in range(n_win):
        row = x_ref[0, j, 48:56, :].astype(jnp.float32)
        b, off = divmod(j * rows_dev, LANES)
        turned = pltpu.roll(row, off, 1) if off else row
        end = off + rows_dev
        pieces[b] = jnp.where((lane >= off) & (lane < end), turned, pieces[b])
        if end > LANES:
            pieces[b + 1] = jnp.where(lane < end - LANES, turned, pieces[b + 1])
    for b, piece in enumerate(pieces):
        mask_ref[b:b + 1, :] = piece[0:1, :]

    count, half_rows = c_ref.shape[0], rows // 2
    half_win = n_win // 2

    def fill(cross_ref, k, side):
        for j in range(half_win):
            for t in range(3):
                quarters = []
                for p in range(2):
                    at = t * 16 + p * 8
                    tile = x_ref[k, side * half_win + j, at:at + 8, :].astype(jnp.float32)
                    turned = pltpu.roll(tile, 4, 0)
                    quarters += [jnp.where(low, tile, turned), jnp.where(low, turned, tile)]
                at = slice(j * rows_dev + t * 16, j * rows_dev + t * 16 + 16)
                src = slice(at.start + side * half_rows, at.stop + side * half_rows)
                for i in range(2):
                    a = jnp.concatenate([quarters[i]] * 2, axis=0)
                    b = jnp.concatenate([quarters[2 + i]] * 2, axis=0)
                    first = slice(i * LANES, (i + 1) * LANES)
                    second = slice(half + i * LANES, half + (i + 1) * LANES)
                    u = a_ref[src, first].astype(jnp.float32)
                    v = a_ref[src, second].astype(jnp.float32)
                    cross_ref[at, first] = (a * u + b * v).astype(jnp.bfloat16)
                    cross_ref[at, second] = (b * u - a * v).astype(jnp.bfloat16)

    def correlate(cross_ref, s, side):
        for n in range(half_rows // 256):
            got = lax.dot_general(
                inv_ref[...], cross_ref[n * 256:(n + 1) * 256, :], NT, preferred_element_type=jnp.float32
            )
            at = side * half_rows + n * 256
            c_ref[s, :, at:at + 256] = got.astype(jnp.bfloat16)

    fill(even_ref, 0, 0)

    def slot(k, carry):
        s = ids_ref[k]
        correlate(even_ref, s, 0)
        fill(odd_ref, k, 1)
        correlate(odd_ref, s, 1)
        fill(even_ref, jnp.minimum(k + 1, count - 1), 0)
        pltpu.make_async_copy(c_ref.at[s], c_hbm.at[s], sems.at[s]).start()
        weighted_sums(c_ref, s, mask_ref, terms_ref)
        return carry

    lax.fori_loop(0, count, slot, 0)
    finish_stacks(terms_ref, stack_ref)

    def last(s, carry):
        residuals(c_ref, s, stack_ref, r_ref)
        return carry

    lax.fori_loop(0, count, last, 0)
    part_ref[...] = jnp.full(part_ref.shape, masked_sum(mask_ref, r_ref), jnp.float32)
    for s in range(c_ref.shape[0]):
        pltpu.make_async_copy(c_ref.at[s], c_hbm.at[s], sems.at[s]).wait()


def set_weights(pairs, total, mask_ref, r_ref, w_ref):
    mask = mask_ref[...]
    spread = total / (pairs * jnp.sum(mask) * (1.0 / Q)) + epsilon
    w_ref[...] = mask[None] * (degrees + 1.0) / (degrees + r_ref[...] / spread)


def start_all(c_hbm, c_ref, sems):
    for s in range(c_ref.shape[0]):
        pltpu.make_async_copy(c_hbm.at[s], c_ref.at[s], sems.at[s]).start()


def iterate_core(pairs, all_ref, mask_ref, r_in_ref, c_hbm, r_ref, c_ref, w_ref, terms_ref, stack_ref, sems):
    start_all(c_hbm, c_ref, sems)
    set_weights(pairs, jnp.sum(all_ref[...]) * (1.0 / LANES), mask_ref, r_in_ref, w_ref)

    def one(s, carry):
        pltpu.make_async_copy(c_hbm.at[s], c_ref.at[s], sems.at[s]).wait()
        weighted_sums(c_ref, s, w_ref.at[s], terms_ref)
        return carry

    lax.fori_loop(0, c_ref.shape[0], one, 0)
    finish_stacks(terms_ref, stack_ref)

    def last(s, carry):
        residuals(c_ref, s, stack_ref, r_ref)
        return carry

    lax.fori_loop(0, c_ref.shape[0], last, 0)


def iterate_kernel(pairs, all_ref, mask_ref, r_in_ref, c_hbm, r_ref, part_ref, c_ref, w_ref, terms_ref, stack_ref, sems):
    iterate_core(pairs, all_ref, mask_ref, r_in_ref, c_hbm, r_ref, c_ref, w_ref, terms_ref, stack_ref, sems)
    part_ref[...] = jnp.full(part_ref.shape, masked_sum(mask_ref, r_ref), jnp.float32)


def last_residual_kernel(pairs, all_ref, mask_ref, r_in_ref, c_hbm, r_ref, home_ref, c_ref, w_ref, terms_ref, stack_ref, sems):
    iterate_core(pairs, all_ref, mask_ref, r_in_ref, c_hbm, r_ref, c_ref, w_ref, terms_ref, stack_ref, sems)
    part = masked_sum(mask_ref, r_ref)
    n_win, count = home_ref.shape[0], home_ref.shape[1]
    rows_dev = r_ref.shape[1] * LANES // n_win
    lane = lax.broadcasted_iota(jnp.int32, (count, LANES), 1)
    for j in range(n_win):
        b, off = divmod(j * rows_dev, LANES)
        piece = r_ref[:, b, :]
        if off:
            piece = pltpu.roll(piece, LANES - off, 1)
        if off + rows_dev > LANES:
            more = pltpu.roll(r_ref[:, b + 1, :], LANES - off, 1)
            piece = jnp.where(lane < LANES - off, piece, more)
        home_ref[j] = jnp.where(lane < rows_dev, piece, part)


def spectrum_kernel(
    pairs, all_ref, mask_ref, r_in_ref, c_hbm, table_ref, o_ref, c_ref, w_ref, terms_ref, stack_ref, sems
):
    start_all(c_hbm, c_ref, sems)
    set_weights(pairs, jnp.sum(all_ref[...]) * (1.0 / LANES), mask_ref, r_in_ref, w_ref)

    def one(s, carry):
        pltpu.make_async_copy(c_hbm.at[s], c_ref.at[s], sems.at[s]).wait()
        weighted_sums(c_ref, s, w_ref.at[s], terms_ref)
        return carry

    lax.fori_loop(0, c_ref.shape[0], one, 0)
    finish_stacks(terms_ref, stack_ref)
    lane = lax.broadcasted_iota(jnp.int32, (L, LANES), 1)
    stacks = stack_ref[0]
    for s in range(1, c_ref.shape[0]):
        stacks = jnp.where(lane // 16 == s, stack_ref[s], stacks)
    both = jnp.dot(table_ref[...], stacks, precision=HIGHEST, preferred_element_type=jnp.float32)
    freq_count = table_ref.shape[0] // 2
    part = lax.broadcasted_iota(jnp.int32, (freq_count, LANES), 1) % 4
    o_ref[...] = jnp.where(part == 0, both[:freq_count], jnp.where(part == 1, both[freq_count:], 0.0))


def beam_kernel(gain, x_ref, cos_ref, sin_ref, fine_cos_ref, fine_sin_ref, o_ref):
    x = x_ref[...]
    yc = lax.dot_general(x, cos_ref[...], TN, precision=HIGHEST, preferred_element_type=jnp.float32)
    ys = lax.dot_general(x, sin_ref[...], TN, precision=HIGHEST, preferred_element_type=jnp.float32)
    c, s = fine_cos_ref[...], fine_sin_ref[...]
    u = yc * c - ys * s
    v = ys * c + yc * s
    rows = o_ref.shape[1] * 2
    out = lax.broadcasted_iota(jnp.int32, (rows, LANES), 0)
    lane = lax.broadcasted_iota(jnp.int32, (rows, LANES), 1)
    same = lane // 16 == out // 2
    imag, part = out % 2, lane % 4
    pick_u = jnp.where(same & (part == imag), 1.0, 0.0)
    pick_v = jnp.where(same & (part == 0) & (imag == 1), 1.0, 0.0) - jnp.where(
        same & (part == 1) & (imag == 0), 1.0, 0.0
    )
    beams = jnp.dot(pick_u, u, precision=HIGHEST, preferred_element_type=jnp.float32) + jnp.dot(
        pick_v, v, precision=HIGHEST, preferred_element_type=jnp.float32
    )
    for i in range(o_ref.shape[1]):
        o_ref[0, i] = beams[2 * i:2 * i + 2] * gain


def cos_sin(freq_id, chan_ids, slow_count, modulus):
    slow_ids = jnp.arange(slow_count, dtype=jnp.int32) - slow_count // 2
    phase_ids = jnp.mod((freq_id * chan_ids)[:, None] * slow_ids[None, :], modulus)
    angles = 2.0 * math.pi / modulus * phase_ids.astype(jnp.float32)
    return jnp.cos(angles), jnp.sin(angles)


VMEM = pl.BlockSpec(memory_space=pltpu.VMEM)
SMEM = pl.BlockSpec(memory_space=pltpu.SMEM)
ANY = pl.BlockSpec(memory_space=pl.ANY)


def body(spectra, sources, valid):
    win_dev, chan_dev, width = spectra.shape
    freq_count = width // 2
    source_total = sources.shape[0]
    n_win = lax.axis_size("win")
    n_ch = lax.axis_size("ch")
    n_all = n_win * n_ch
    chans = chan_dev * n_ch
    pairs = float(source_total * chans)
    win, ch = lax.axis_index("win"), lax.axis_index("ch")
    y, core = ch // 2, ch % 2
    inverse_np, forward_np = tables(freq_count, L)
    flat = spectra.reshape(win_dev * chan_dev, width)
    rows_dev = win_dev * Q
    rows = n_win * rows_dev
    piece = win_dev * width // LANES

    picked = pl.pallas_call(
        pick_kernel,
        in_specs=[SMEM, VMEM],
        out_specs=VMEM,
        out_shape=jax.ShapeDtypeStruct((source_total, piece, LANES), jnp.bfloat16),
        compiler_params=PARAMS,
        name="pick",
    )(sources, flat)
    got = lax.all_to_all(picked, "ch", 0, 0, tiled=True)
    own_mask = valid.astype(jnp.float32)
    mask_lanes = jnp.broadcast_to(own_mask.reshape(win_dev // 4, 1, 4), (win_dev // 4, Q, 4)).reshape(1, rows_dev)
    own = pl.pallas_call(
        own_kernel,
        in_specs=[VMEM, VMEM],
        out_specs=VMEM,
        out_shape=jax.ShapeDtypeStruct((n_win, piece + 8, LANES), jnp.bfloat16),
        compiler_params=PARAMS,
        name="own",
    )(got, jnp.pad(mask_lanes, ((0, 0), (0, LANES - rows_dev))))

    own = lax.all_to_all(own, "win", 0, 0, tiled=True)

    def turn_y(d):
        return [(i * 2 + c, ((i + d) % 4) * 2 + c) for i in range(n_ch // 2) for c in range(2)]

    with jax.named_scope("along_y"):
        mine = jnp.stack([own] + [lax.ppermute(own, "ch", turn_y(d)) for d in (1, 2, 3)])
    with jax.named_scope("cores"):
        theirs = lax.ppermute(mine, "ch", [(i, i ^ 1) for i in range(n_ch)])
    steps = jnp.arange(4, dtype=jnp.int32)
    slot_y = 2 * ((y - steps) % 4)
    ids = jnp.concatenate([slot_y + core, slot_y + 1 - core]).astype(jnp.int32)

    with jax.named_scope("main"):
        packed = pl.pallas_call(
            pack_kernel,
            in_specs=[VMEM],
            out_specs=VMEM,
            out_shape=jax.ShapeDtypeStruct((n_win, rows_dev, width), jnp.bfloat16),
            compiler_params=PARAMS,
            name="pack",
        )(flat)
        moved = lax.all_to_all(packed, "win", 0, 0, tiled=True)

    corr_shape = jax.ShapeDtypeStruct((source_total, L, rows), jnp.bfloat16)
    r_shape = jax.ShapeDtypeStruct((source_total, rows // LANES, LANES), jnp.float32)
    mask_shape = jax.ShapeDtypeStruct((rows // LANES, LANES), jnp.float32)
    part_shape = jax.ShapeDtypeStruct((n_all, LANES), jnp.float32)
    held = pltpu.VMEM(corr_shape.shape, jnp.bfloat16)
    row_weights = pltpu.VMEM(r_shape.shape, jnp.float32)
    terms = pltpu.VMEM((source_total, L + 16, 3 * LANES), jnp.bfloat16)
    stack = pltpu.VMEM((source_total, L, LANES), jnp.float32)
    cross = pltpu.VMEM((rows // 2, width), jnp.bfloat16)
    sems = pltpu.SemaphoreType.DMA((source_total,))
    corr, r, part, mask = pl.pallas_call(
        correlate_kernel,
        in_specs=[SMEM, VMEM, VMEM, VMEM],
        out_specs=[ANY, VMEM, VMEM, VMEM],
        out_shape=[corr_shape, r_shape, part_shape, mask_shape],
        scratch_shapes=[cross, cross, held, terms, stack, sems],
        compiler_params=pltpu.CompilerParams(vmem_limit_bytes=56 << 20),
        name="correlate",
    )(ids, moved.reshape(rows, width), jnp.concatenate([mine, theirs]), jnp.asarray(inverse_np, jnp.bfloat16))

    parts = lax.all_to_all(part, ("win", "ch"), 0, 0, tiled=True)
    for kernel, shape in (
        (iterate_kernel, part_shape),
        (last_residual_kernel, jax.ShapeDtypeStruct((n_win, source_total, LANES), jnp.float32)),
    ):
        r, part = pl.pallas_call(
            lambda *refs: kernel(pairs, *refs),
            in_specs=[VMEM, VMEM, VMEM, ANY],
            out_specs=[VMEM, VMEM],
            out_shape=[r_shape, shape],
            scratch_shapes=[held, row_weights, terms, stack, sems],
            compiler_params=BIG,
            name="iterate",
        )(parts, mask, r, corr)
        if kernel is iterate_kernel:
            parts = lax.all_to_all(part, ("win", "ch"), 0, 0, tiled=True)

    back = lax.all_to_all(part, "win", 0, 0, tiled=True)
    over_win = jnp.sum(back[:, 0, rows_dev])
    parts = lax.all_to_all(jnp.broadcast_to(over_win, (n_ch, LANES)), "ch", 0, 0, tiled=True)

    spectrum = pl.pallas_call(
        lambda *refs: spectrum_kernel(pairs, *refs),
        in_specs=[VMEM, VMEM, VMEM, ANY, VMEM],
        out_specs=VMEM,
        out_shape=jax.ShapeDtypeStruct((freq_count, LANES), jnp.float32),
        scratch_shapes=[held, row_weights, terms, stack, sems],
        compiler_params=BIG,
        name="spectrum",
    )(parts, mask, r, corr, jnp.asarray(forward_np))
    pieces = lax.all_to_all(spectrum, ("win", "ch"), 0, 0, tiled=True)

    freq_id = win * n_ch + ch
    modulus = 4 * freq_count * P_SIZE
    device = jnp.arange(n_all, dtype=jnp.int32)
    coarse = (device % n_ch) * chan_dev + (device // n_ch) * Q
    cosines, sines = cos_sin(freq_id, coarse, P_SIZE, modulus)
    fine_cos, fine_sin = cos_sin(freq_id, (jnp.arange(LANES, dtype=jnp.int32) // 4) % Q, P_SIZE, modulus)
    beamed = pl.pallas_call(
        lambda *refs: beam_kernel(chans ** (-0.5), *refs),
        in_specs=[VMEM] * 5,
        out_specs=VMEM,
        out_shape=jax.ShapeDtypeStruct((1, source_total, 2, P_SIZE), jnp.float32),
        compiler_params=PARAMS,
        name="beam",
    )(pieces, cosines, sines, fine_cos, fine_sin)

    window_count = jnp.sum(mask) * (1.0 / Q)
    spread_sq = jnp.sum(parts[:, 0]) / (pairs * window_count) + epsilon
    residual = back[:, :, :rows_dev].reshape(n_win, source_total, win_dev // 4, Q, 4)
    residual = residual.transpose(2, 4, 1, 0, 3).reshape(win_dev, source_total, chan_dev)
    weights = own_mask[:, None, None] * (degrees + 1.0) / (degrees + residual / spread_sq)
    return (weights, beamed)


def solution(mesh):
    return jax.shard_map(
        body,
        mesh=mesh,
        in_specs=(P("win", "ch", None), P(), P("win")),
        out_specs=(P("win", None, "ch"), P(("win", "ch"), None, None, None)),
        check_vma=False,
    )
```

time: 231 us -> 212 us (0.918)
  Pallas kernels: 58.3 us -> 43.5 us
  waiting for transfers between devices: 88.4 us -> 84.6 us
    pallas_call x7 -> x8, Pallas kernels: 58.3 us -> 43.5 us  [the longest x1 16.2 us: body(): pl.pallas_call(correlate_kernel, in_specs=[SMEM, VMEM, VMEM, VMEM], out_s...]
    unnamed x13 -> x23, local copies, waits for them, and re-layouts: 3.05 us -> 8.69 us
    reshape x3 -> x1, local copies, waits for them, and re-layouts: 3.13 us -> 0.09 us  [body(): jnp.broadcast_to(own_mask.reshape(win_dev // 4, 1, 4), (win_dev // 4, Q, 4))]
    ppermute x3, waiting for transfers between devices: 22.7 us -> 20 us  [body(): lax.ppermute(own, 'ch', turn_y(d))]
    all_to_all x4, waiting for transfers between devices: 27.7 us -> 24.9 us  [the longest x1 10.9 us: body(): own = lax.all_to_all(own, 'win', 0, 0, tiled=True)]
  transfers between devices with their start and end apart: 12 -> 12, of which waited for: 11 -> 11; matrix products, arithmetic and copies ran while one was open for 5% -> 7% of each run, Pallas kernels for 2% -> 1%
where the time goes in v2:
time: 212 us; the launch traced here: 211 us
  waiting for transfers between devices  84.6 us (40%)
  starting transfers between devices  59.5 us (28%)
  Pallas kernels  43.5 us (21%)
  local copies, waits for them, and re-layouts  13.6 us (6%)
  other arithmetic  8.17 us (4%)
  between operations  2.17 us (1%)
    all_to_all x2, waiting for transfers between devices, body(): parts = lax.all_to_all(part, ('win', 'ch'), 0, 0, tiled=True)  24.7 us
    ppermute x3, waiting for transfers between devices, body(): lax.ppermute(own, 'ch', turn_y(d))  20 us
    pallas_call x1, Pallas kernels, body(): pl.pallas_call(correlate_kernel, in_specs=[SMEM, VMEM, VMEM, VMEM], out_s...  16.2 us
    all_to_all x2, starting transfers between devices, body(): parts = lax.all_to_all(part, ('win', 'ch'), 0, 0, tiled=True)  15.3 us
    pallas_call x2, Pallas kernels, body(): pl.pallas_call(lambda *refs: kernel(pairs, *refs), in_specs=[VMEM, VMEM,...  14.7 us
    all_to_all x1, waiting for transfers between devices, body(): own = lax.all_to_all(own, 'win', 0, 0, tiled=True)  10.9 us
    all_to_all x1, waiting for transfers between devices, body(): pieces = lax.all_to_all(spectrum, ('win', 'ch'), 0, 0, tiled=True)  10.8 us
    all_to_all x1, starting transfers between devices, body(): own = lax.all_to_all(own, 'win', 0, 0, tiled=True)  10.5 us
  transfers between devices with their start and end apart: 12, of which 11 were waited for; matrix products, arithmetic and copies ran while one was open for 7% of the time, Pallas kernels for 1%

profile of v2, /device:TPU:1, one launch (start us, length us, event | category | flops | bytes accessed | tf_op | source)
XLA Modules:
  0.0 211.5 jit_solution(9975345965959871977)
XLA Ops:
  0.6 1.4 copy-done
  2.0 0.7 copy-done.2
  2.7 1.7 pick.1
  4.4 6.5 %all-to-all-start.1 = ((bf16[8,48,128]{2,1,0:T(8,128)(2,1)}), bf16[8,48,128]{2,1,0:T(8,128)(2,1)S(1)}, u32[]{:S(2)}, u32[]{:S(2)}) async-start(bf16[8,48,128]{2,1,0:T(8,128)(2,1)} %pick.1), calls=%async_computation.1 | async-start | bytes 196608 | tf_op jit(solution)/shard_map/all_to_all | solution.py:353
  10.8 0.7 convert_element_type.11
  11.7 4.1 %all-to-all-done.1.x_ref = bf16[8,48,128]{2,1,0:T(8,128)(2,1)S(1)} async-done(((bf16[8,48,128]{2,1,0:T(8,128)(2,1)}), bf16[8,48,128]{2,1,0:T(8,128)(2,1)S(1)}, u32[]{:S(2)}, u32[]{:S(2)}) %all-to-all-start.1) | async-done | bytes 98336 | tf_op jit(solution)/shard_map/all_to_all | solution.py:353
  15.8 0.8 own.1
  16.6 10.5 %all-to-all-start.2 = ((bf16[32,56,128]{2,1,0:T(8,128)(2,1)}), bf16[32,56,128]{2,1,0:T(8,128)(2,1)S(1)}, u32[]{:S(2)}, u32[]{:S(2)}) async-start(bf16[32,56,128]{2,1,0:T(8,128)(2,1)} %own.1), calls=%async_computation.2 | async-start | bytes 917504 | tf_op jit(solution)/shard_map/all_to_all | solution.py:365
  27.2 2.2 %pack.1 = bf16[32,48,512]{2,1,0:T(8,128)(2,1)} custom-call(bf16[1536,512]{1,0:T(8,128)(2,1)S(1)} %bitcast.28), custom_call_target="tpu_custom_call" | custom-call | tf_op jit(solution)/shard_map/main/pack/pallas_call | solution.py:379
  29.4 10.9 %all-to-all-done.2 = bf16[32,56,128]{2,1,0:T(8,128)(2,1)S(1)} async-done(((bf16[32,56,128]{2,1,0:T(8,128)(2,1)}), bf16[32,56,128]{2,1,0:T(8,128)(2,1)S(1)}, u32[]{:S(2)}, u32[]{:S(2)}) %all-to-all-start.2) | async-done | bytes 458784 | tf_op jit(solution)/shard_map/all_to_all | solution.py:365
  40.3 7.6 %all-to-all-start = ((bf16[32,48,512]{2,1,0:T(8,128)(2,1)}), bf16[32,48,512]{2,1,0:T(8,128)(2,1)S(1)}, u32[]{:S(2)}, u32[]{:S(2)}) async-start(bf16[32,48,512]{2,1,0:T(8,128)(2,1)} %pack.1), calls=%async_computation | async-start | bytes 3145728 | tf_op jit(solution)/shard_map/main/all_to_all | solution.py:387
  48.2 1.8 collective-permute-start.1
  50.0 0.8 collective-permute-start.2
  50.8 9.7 %collective-permute-done = bf16[32,56,128]{2,1,0:T(8,128)(2,1)S(1)} collective-permute-done((bf16[32,56,128]{2,1,0:T(8,128)(2,1)S(1)}, bf16[32,56,128]{2,1,0:T(8,128)(2,1)S(1)}, u32[]{:S(2)}, u32[]{:S(2)}) %collective-permute-start) | collective-permute-done | bytes 458784 | tf_op jit(solution)/shard_map/along_y/ppermute | solution.py:371
  60.4 8.7 %collective-permute-done.1 = bf16[32,56,128]{2,1,0:T(8,128)(2,1)S(1)} collective-permute-done((bf16[32,56,128]{2,1,0:T(8,128)(2,1)S(1)}, bf16[32,56,128]{2,1,0:T(8,128)(2,1)S(1)}, u32[]{:S(2)}, u32[]{:S(2)}) %collective-permute-start.1) | collective-permute-done | bytes 458784 | tf_op jit(solution)/shard_map/along_y/ppermute | solution.py:371
  69.1 1.6 collective-permute-done.2
  70.7 1.5 pad_maximum_fusion
  72.2 1.8 collective-permute-start.3
  74.6 0.8 constant_dynamic-update-slice_fusion.4
  75.4 0.8 constant_dynamic-update-slice_fusion.3
  76.2 0.8 constant_dynamic-update-slice_fusion.2
  77.0 0.9 constant_dynamic-update-slice_fusion.1
  77.9 2.9 %constant_dynamic-update-slice_fusion.x_ref = bf16[8,32,56,128]{3,2,1,0:T(8,128)(2,1)} fusion(bf16[8,32,56,128]{3,2,1,0:T(8,128)(2,1)} %constant_dynamic-update-slice_fusion.1, bf16[4,32,56,128]{3,2,1,0:T(8,128)(2,1)} %collective-permute-done.3), kind=kLoop, calls=%fused_computation.25 | loop fusion | bytes 3670016 | tf_op jit(solution)/shard_map/concatenate | solution.py:407
  80.8 3.9 %all-to-all-done = bf16[32,48,512]{2,1,0:T(8,128)(2,1)S(1)} async-done(((bf16[32,48,512]{2,1,0:T(8,128)(2,1)}), bf16[32,48,512]{2,1,0:T(8,128)(2,1)S(1)}, u32[]{:S(2)}, u32[]{:S(2)}) %all-to-all-start) | async-done | bytes 1572896 | tf_op jit(solution)/shard_map/main/all_to_all | solution.py:387
  84.7 1.2 copy-done.3
  85.8 16.2 %correlate.1 = (bf16[8,256,1536]{2,1,0:T(8,128)(2,1)}, f32[8,12,128]{2,1,0:T(8,128)}, f32[256,128]{1,0:T(8,128)}, f32[12,128]{1,0:T(8,128)}) custom-call(s32[8]{0:T(128)} %pad_add_fusion.ids_ref, bf16[1536,512]{1,0:T(8,128)(2,1)} %bitcast.30, bf16[8,32,56,128]{3,2,1,0:T(8,128)(2,1)} %constant_dynamic-update-slice_fusion.x_ref, ...), custom_call_target="tpu_custom_call" | custom-call | tf_op jit(solution)/shard_map/correlate/pallas_call | solution.py:399
  102.0 9.9 %all-to-all-start.3 = ((f32[256,1,128]{2,1,0:T(1,128)}), f32[256,1,128]{2,1,0:T(1,128)S(1)}, u32[]{:S(2)}, u32[]{:S(2)}) async-start(f32[256,1,128]{2,1,0:T(1,128)} %bitcast.40), calls=%async_computation.3 | async-start | bytes 262144 | tf_op jit(solution)/shard_map/all_to_all | solution.py:409
  111.9 12.8 %all-to-all-done.3 = f32[256,1,128]{2,1,0:T(1,128)S(1)} async-done(((f32[256,1,128]{2,1,0:T(1,128)}), f32[256,1,128]{2,1,0:T(1,128)S(1)}, u32[]{:S(2)}, u32[]{:S(2)}) %all-to-all-start.3) | async-done | bytes 131104 | tf_op jit(solution)/shard_map/all_to_all | solution.py:409
  124.8 0.7 copy-done.4
  125.4 7.3 %iterate.2 = (f32[8,12,128]{2,1,0:T(8,128)}, f32[256,128]{1,0:T(8,128)}) custom-call(f32[256,128]{1,0:T(8,128)} %bitcast.37, f32[12,128]{1,0:T(8,128)} %get-tuple-element.11.refs_1_, f32[8,12,128]{2,1,0:T(8,128)} %get-tuple-element.12.refs_2_, bf16[8,256,1536]{2,1,0:T(8,128)(2,1)} %get-tuple-element.13.refs_3_), custom_call_target="tpu_custom_call" | custom-call | tf_op jit(solution)/shard_map/iterate/pallas_call | solution.py:414
  132.8 5.4 %all-to-all-start.4 = ((f32[256,1,128]{2,1,0:T(1,128)}), f32[256,1,128]{2,1,0:T(1,128)S(1)}, u32[]{:S(2)}, u32[]{:S(2)}) async-start(f32[256,1,128]{2,1,0:T(1,128)} %bitcast.41), calls=%async_computation.4 | async-start | bytes 262144 | tf_op jit(solution)/shard_map/all_to_all | solution.py:424
  138.2 1.1 fusion.9
  139.3 11.9 %all-to-all-done.4 = f32[256,1,128]{2,1,0:T(1,128)S(1)} async-done(((f32[256,1,128]{2,1,0:T(1,128)}), f32[256,1,128]{2,1,0:T(1,128)S(1)}, u32[]{:S(2)}, u32[]{:S(2)}) %all-to-all-start.4) | async-done | bytes 131104 | tf_op jit(solution)/shard_map/all_to_all | solution.py:424
  151.2 0.7 copy-done.5
  151.9 7.4 %iterate.3 = (f32[8,12,128]{2,1,0:T(8,128)}, f32[32,8,128]{2,1,0:T(8,128)}) custom-call(f32[256,128]{1,0:T(8,128)} %bitcast.39, f32[12,128]{1,0:T(8,128)} %get-tuple-element.11.refs_1_, f32[8,12,128]{2,1,0:T(8,128)} %get-tuple-element.15.refs_2_, bf16[8,256,1536]{2,1,0:T(8,128)(2,1)} %get-tuple-element.13.refs_3_), custom_call_target="tpu_custom_call" | custom-call | tf_op jit(solution)/shard_map/iterate/pallas_call | solution.py:414
  159.3 3.9 %all-to-all-start.5 = ((f32[32,8,128]{2,1,0:T(8,128)}), f32[32,8,128]{2,1,0:T(8,128)S(1)}, u32[]{:S(2)}, u32[]{:S(2)}) async-start(f32[32,8,128]{2,1,0:T(8,128)} %get-tuple-element.16), calls=%async_computation.5 | async-start | bytes 262144 | tf_op jit(solution)/shard_map/all_to_all | solution.py:426
  163.1 2.1 %fusion.6 = (f32[256,512]{1,0:T(8,128)S(1)}, f32[256,512]{1,0:T(8,128)S(1)}) fusion(s32[512]{0:T(512)S(1)} %iota_add_fusion, s32[256]{0:T(256)S(1)} %fusion.15), kind=kLoop, calls=%fused_computation.18 | loop fusion | flops 1835008 | bytes 1051648 | tf_op jit(solution)/shard_map/sin | solution.py:320
  165.3 7.0 %all-to-all-done.5 = f32[32,8,128]{2,1,0:T(8,128)S(1)} async-done(((f32[32,8,128]{2,1,0:T(8,128)}), f32[32,8,128]{2,1,0:T(8,128)S(1)}, u32[]{:S(2)}, u32[]{:S(2)}) %all-to-all-start.5) | async-done | bytes 131104 | tf_op jit(solution)/shard_map/all_to_all | solution.py:426
  172.3 0.8 slice_reduce_fusion
  173.0 1.3 broadcast_in_dim.8
  174.3 5.3 %all-to-all-start.6 = ((f32[8,1,128]{2,1,0:T(1,128)}), f32[8,1,128]{2,1,0:T(1,128)S(1)}, u32[]{:S(2)}, u32[]{:S(2)}) async-start(f32[8,1,128]{2,1,0:T(1,128)} %broadcast_in_dim.8), calls=%async_computation.6 | async-start | bytes 8192 | tf_op jit(solution)/shard_map/all_to_all | solution.py:428
  179.7 0.7 reduce_sum.29
  181.1 3.2 %all-to-all-done.6 = f32[8,1,128]{2,1,0:T(1,128)S(1)} async-done(((f32[8,1,128]{2,1,0:T(1,128)}), f32[8,1,128]{2,1,0:T(1,128)S(1)}, u32[]{:S(2)}, u32[]{:S(2)}) %all-to-all-start.6) | async-done | bytes 4128 | tf_op jit(solution)/shard_map/all_to_all | solution.py:428
  184.8 6.2 %spectrum.1 = f32[256,128]{1,0:T(8,128)} custom-call(f32[8,128]{1,0:T(8,128)} %bitcast.43, f32[12,128]{1,0:T(8,128)} %get-tuple-element.11.refs_1_, f32[8,12,128]{2,1,0:T(8,128)} %get-tuple-element.17.refs_2_, bf16[8,256,1536]{2,1,0:T(8,128)(2,1)} %get-tuple-element.13.refs_3_, f32[512,256]{1,0:T(8,128)} %constant.146.clone.refs_4_), custom_call_target="tpu_custom_call" | custom-call | tf_op jit(solution)/shard_map/spectrum/pallas_call | solution.py:430
  191.0 5.7 %all-to-all-start.7 = ((f32[256,1,128]{2,1,0:T(1,128)}), f32[256,1,128]{2,1,0:T(1,128)S(1)}, u32[]{:S(2)}, u32[]{:S(2)}) async-start(f32[256,1,128]{2,1,0:T(1,128)} %bitcast.38), calls=%async_computation.7 | async-start | bytes 262144 | tf_op jit(solution)/shard_map/all_to_all | solution.py:439
  198.1 0.9 copy.16
  198.9 10.8 %all-to-all-done.7 = f32[256,1,128]{2,1,0:T(1,128)S(1)} async-done(((f32[256,1,128]{2,1,0:T(1,128)}), f32[256,1,128]{2,1,0:T(1,128)S(1)}, u32[]{:S(2)}, u32[]{:S(2)}) %all-to-all-start.7) | async-done | bytes 131104 | tf_op jit(solution)/shard_map/all_to_all | solution.py:439
  209.8 1.7 beam.1
  (30 shorter events, 2.4 us)
Async XLA Ops:
  0.6 1.4 copy-start
  2.0 0.7 copy-start.2
  2.7 24.5 %copy-start.1 = (bf16[12,128,512]{2,1,0:T(8,128)(2,1)S(1)}, bf16[12,128,512]{2,1,0:T(8,128)(2,1)}, u32[]{:S(2)}) copy-start(bf16[12,128,512]{2,1,0:T(8,128)(2,1)} %param.5) | copy-start | bytes 4718596
  4.4 11.5 %all-to-all-start.1 = ((bf16[8,48,128]{2,1,0:T(8,128)(2,1)}), bf16[8,48,128]{2,1,0:T(8,128)(2,1)S(1)}, u32[]{:S(2)}, u32[]{:S(2)}) async-start(bf16[8,48,128]{2,1,0:T(8,128)(2,1)} %pick.1), calls=%async_computation.1 | async-start | bytes 196608 | tf_op jit(solution)/shard_map/all_to_all | solution.py:353
  16.6 23.6 %all-to-all-start.2 = ((bf16[32,56,128]{2,1,0:T(8,128)(2,1)}), bf16[32,56,128]{2,1,0:T(8,128)(2,1)S(1)}, u32[]{:S(2)}, u32[]{:S(2)}) async-start(bf16[32,56,128]{2,1,0:T(8,128)(2,1)} %own.1), calls=%async_computation.2 | async-start | bytes 917504 | tf_op jit(solution)/shard_map/all_to_all | solution.py:365
  40.3 44.4 %all-to-all-start = ((bf16[32,48,512]{2,1,0:T(8,128)(2,1)}), bf16[32,48,512]{2,1,0:T(8,128)(2,1)S(1)}, u32[]{:S(2)}, u32[]{:S(2)}) async-start(bf16[32,48,512]{2,1,0:T(8,128)(2,1)} %pack.1), calls=%async_computation | async-start | bytes 3145728 | tf_op jit(solution)/shard_map/main/all_to_all | solution.py:387
  47.8 12.6 %collective-permute-start = (bf16[32,56,128]{2,1,0:T(8,128)(2,1)S(1)}, bf16[32,56,128]{2,1,0:T(8,128)(2,1)S(1)}, u32[]{:S(2)}, u32[]{:S(2)}) collective-permute-start(bf16[32,56,128]{2,1,0:T(8,128)(2,1)S(1)} %all-to-all-done.2), channel_id=1, source_target_pairs={{0,2},{1,3},{2,4},{3,5},{4,6},{5,7},{6,0},{7,1},{8,10},{9,11},{10,... | collective-permute-start | bytes 1376264 | tf_op jit(solution)/shard_map/along_y/ppermute | solution.py:371
  48.2 20.9 %collective-permute-start.1 = (bf16[32,56,128]{2,1,0:T(8,128)(2,1)S(1)}, bf16[32,56,128]{2,1,0:T(8,128)(2,1)S(1)}, u32[]{:S(2)}, u32[]{:S(2)}) collective-permute-start(bf16[32,56,128]{2,1,0:T(8,128)(2,1)S(1)} %all-to-all-done.2), channel_id=1, source_target_pairs={{0,4},{1,5},{2,6},{3,7},{4,0},{5,1},{6,2},{7,3},{8,12},{9,13},{10,... | collective-permute-start | bytes 1376264 | tf_op jit(solution)/shard_map/along_y/ppermute | solution.py:371
  50.0 20.7 %collective-permute-start.2 = (bf16[32,56,128]{2,1,0:T(8,128)(2,1)S(1)}, bf16[32,56,128]{2,1,0:T(8,128)(2,1)S(1)}, u32[]{:S(2)}, u32[]{:S(2)}) collective-permute-start(bf16[32,56,128]{2,1,0:T(8,128)(2,1)S(1)} %all-to-all-done.2), channel_id=1, source_target_pairs={{0,6},{1,7},{2,0},{3,1},{4,2},{5,3},{6,4},{7,5},{8,14},{9,15},{10,... | collective-permute-start | bytes 1376264 | tf_op jit(solution)/shard_map/along_y/ppermute | solution.py:371
  72.2 5.7 %collective-permute-start.3 = (bf16[4,32,56,128]{3,2,1,0:T(8,128)(2,1)}, bf16[4,32,56,128]{3,2,1,0:T(8,128)(2,1)}, u32[]{:S(2)}, u32[]{:S(2)}) collective-permute-start(bf16[4,32,56,128]{3,2,1,0:T(8,128)(2,1)} %pad_maximum_fusion), channel_id=1, source_target_pairs={{0,1},{1,0},{2,3},{3,2},{4,5},{5,4},{6,7},{7,6},{8,9},{9,8},{10,11... | collective-permute-start | bytes 5505032 | tf_op jit(solution)/shard_map/cores/ppermute | solution.py:373
  84.7 1.2 copy-start.3
  102.0 22.7 %all-to-all-start.3 = ((f32[256,1,128]{2,1,0:T(1,128)}), f32[256,1,128]{2,1,0:T(1,128)S(1)}, u32[]{:S(2)}, u32[]{:S(2)}) async-start(f32[256,1,128]{2,1,0:T(1,128)} %bitcast.40), calls=%async_computation.3 | async-start | bytes 262144 | tf_op jit(solution)/shard_map/all_to_all | solution.py:409
  124.8 0.7 copy-start.4
  132.8 18.4 %all-to-all-start.4 = ((f32[256,1,128]{2,1,0:T(1,128)}), f32[256,1,128]{2,1,0:T(1,128)S(1)}, u32[]{:S(2)}, u32[]{:S(2)}) async-start(f32[256,1,128]{2,1,0:T(1,128)} %bitcast.41), calls=%async_computation.4 | async-start | bytes 262144 | tf_op jit(solution)/shard_map/all_to_all | solution.py:424
  151.2 0.7 copy-start.5
  151.9 27.8 %copy-start.8 = (s32[12]{0:T(128)S(1)}, s32[12]{0:T(128)}, u32[]{:S(2)}) copy-start(s32[12]{0:T(128)} %param.7) | copy-start | bytes 148
  151.9 27.8 %copy-start.6 = (f32[12,128]{1,0:T(8,128)S(1)}, f32[12,128]{1,0:T(8,128)}, u32[]{:S(2)}) copy-start(f32[12,128]{1,0:T(8,128)} %get-tuple-element.11.refs_1_) | copy-start | bytes 18436
  159.3 13.0 %all-to-all-start.5 = ((f32[32,8,128]{2,1,0:T(8,128)}), f32[32,8,128]{2,1,0:T(8,128)S(1)}, u32[]{:S(2)}, u32[]{:S(2)}) async-start(f32[32,8,128]{2,1,0:T(8,128)} %get-tuple-element.16), calls=%async_computation.5 | async-start | bytes 262144 | tf_op jit(solution)/shard_map/all_to_all | solution.py:426
  174.3 9.9 %all-to-all-start.6 = ((f32[8,1,128]{2,1,0:T(1,128)}), f32[8,1,128]{2,1,0:T(1,128)S(1)}, u32[]{:S(2)}, u32[]{:S(2)}) async-start(f32[8,1,128]{2,1,0:T(1,128)} %broadcast_in_dim.8), calls=%async_computation.6 | async-start | bytes 8192 | tf_op jit(solution)/shard_map/all_to_all | solution.py:428
  184.2 0.6 copy-start.7
  191.0 18.7 %all-to-all-start.7 = ((f32[256,1,128]{2,1,0:T(1,128)}), f32[256,1,128]{2,1,0:T(1,128)S(1)}, u32[]{:S(2)}, u32[]{:S(2)}) async-start(f32[256,1,128]{2,1,0:T(1,128)} %bitcast.38), calls=%async_computation.7 | async-start | bytes 262144 | tf_op jit(solution)/shard_map/all_to_all | solution.py:439

commit v3 on v2

--- a/solution.py
+++ b/solution.py
@@ -13,8 +13,7 @@
 ITERS = 3
 Q = 4
 LANES = 128
-PARAMS = pltpu.CompilerParams(vmem_limit_bytes=20 << 20)
-BIG = pltpu.CompilerParams(vmem_limit_bytes=59 << 20)
+PARAMS = pltpu.CompilerParams(vmem_limit_bytes=16 << 20)
 
 degrees = 3.0
 epsilon = 1e-06
@@ -138,7 +137,7 @@
 
 
 def correlate_kernel(
-    ids_ref, a_ref, x_ref, inv_ref, c_hbm, r_ref, part_ref, mask_ref, even_ref, odd_ref, c_ref, terms_ref, stack_ref, sems
+    ids_ref, a_ref, x_ref, y_ref, inv_ref, c_ref, r_ref, part_ref, mask_ref, even_ref, odd_ref, terms_ref, stack_ref
 ):
     n_win, rows = x_ref.shape[1], a_ref.shape[0]
     half = a_ref.shape[1] // 2
@@ -161,13 +160,13 @@
     count, half_rows = c_ref.shape[0], rows // 2
     half_win = n_win // 2
 
-    def fill(cross_ref, k, side):
+    def fill(cross_ref, s_ref, k, side):
         for j in range(half_win):
             for t in range(3):
                 quarters = []
                 for p in range(2):
                     at = t * 16 + p * 8
-                    tile = x_ref[k, side * half_win + j, at:at + 8, :].astype(jnp.float32)
+                    tile = s_ref[k, side * half_win + j, at:at + 8, :].astype(jnp.float32)
                     turned = pltpu.roll(tile, 4, 0)
                     quarters += [jnp.where(low, tile, turned), jnp.where(low, turned, tile)]
                 at = slice(j * rows_dev + t * 16, j * rows_dev + t * 16 + 16)
@@ -190,19 +189,23 @@
             at = side * half_rows + n * 256
             c_ref[s, :, at:at + 256] = got.astype(jnp.bfloat16)
 
-    fill(even_ref, 0, 0)
+    fill(even_ref, x_ref, 0, 0)
+    pairs_of_slots = count // 2
 
     def slot(k, carry):
-        s = ids_ref[k]
-        correlate(even_ref, s, 0)
-        fill(odd_ref, k, 1)
-        correlate(odd_ref, s, 1)
-        fill(even_ref, jnp.minimum(k + 1, count - 1), 0)
-        pltpu.make_async_copy(c_ref.at[s], c_hbm.at[s], sems.at[s]).start()
-        weighted_sums(c_ref, s, mask_ref, terms_ref)
+        after = jnp.minimum(k + 1, pairs_of_slots - 1)
+        for s, s_ref, next_ref, next_k in (
+            (ids_ref[k], x_ref, y_ref, k),
+            (ids_ref[pairs_of_slots + k], y_ref, x_ref, after),
+        ):
+            correlate(even_ref, s, 0)
+            fill(odd_ref, s_ref, k, 1)
+            correlate(odd_ref, s, 1)
+            fill(even_ref, next_ref, next_k, 0)
+            weighted_sums(c_ref, s, mask_ref, terms_ref)
         return carry
 
-    lax.fori_loop(0, count, slot, 0)
+    lax.fori_loop(0, pairs_of_slots, slot, 0)
     finish_stacks(terms_ref, stack_ref)
 
     def last(s, carry):
@@ -211,27 +214,19 @@
 
     lax.fori_loop(0, count, last, 0)
     part_ref[...] = jnp.full(part_ref.shape, masked_sum(mask_ref, r_ref), jnp.float32)
-    for s in range(c_ref.shape[0]):
-        pltpu.make_async_copy(c_ref.at[s], c_hbm.at[s], sems.at[s]).wait()
 
 
 def set_weights(pairs, total, mask_ref, r_ref, w_ref):
     mask = mask_ref[...]
     spread = total / (pairs * jnp.sum(mask) * (1.0 / Q)) + epsilon
     w_ref[...] = mask[None] * (degrees + 1.0) / (degrees + r_ref[...] / spread)
-
-
-def start_all(c_hbm, c_ref, sems):
-    for s in range(c_ref.shape[0]):
-        pltpu.make_async_copy(c_hbm.at[s], c_ref.at[s], sems.at[s]).start()
-
-
-def iterate_core(pairs, all_ref, mask_ref, r_in_ref, c_hbm, r_ref, c_ref, w_ref, terms_ref, stack_ref, sems):
-    start_all(c_hbm, c_ref, sems)
+    return spread
+
+
+def iterate_core(pairs, all_ref, mask_ref, r_in_ref, c_ref, r_ref, w_ref, terms_ref, stack_ref):
     set_weights(pairs, jnp.sum(all_ref[...]) * (1.0 / LANES), mask_ref, r_in_ref, w_ref)
 
     def one(s, carry):
-        pltpu.make_async_copy(c_hbm.at[s], c_ref.at[s], sems.at[s]).wait()
         weighted_sums(c_ref, s, w_ref.at[s], terms_ref)
         return carry
 
@@ -245,13 +240,13 @@
     lax.fori_loop(0, c_ref.shape[0], last, 0)
 
 
-def iterate_kernel(pairs, all_ref, mask_ref, r_in_ref, c_hbm, r_ref, part_ref, c_ref, w_ref, terms_ref, stack_ref, sems):
-    iterate_core(pairs, all_ref, mask_ref, r_in_ref, c_hbm, r_ref, c_ref, w_ref, terms_ref, stack_ref, sems)
+def iterate_kernel(pairs, all_ref, mask_ref, r_in_ref, c_ref, r_ref, part_ref, w_ref, terms_ref, stack_ref):
+    iterate_core(pairs, all_ref, mask_ref, r_in_ref, c_ref, r_ref, w_ref, terms_ref, stack_ref)
     part_ref[...] = jnp.full(part_ref.shape, masked_sum(mask_ref, r_ref), jnp.float32)
 
 
-def last_residual_kernel(pairs, all_ref, mask_ref, r_in_ref, c_hbm, r_ref, home_ref, c_ref, w_ref, terms_ref, stack_ref, sems):
-    iterate_core(pairs, all_ref, mask_ref, r_in_ref, c_hbm, r_ref, c_ref, w_ref, terms_ref, stack_ref, sems)
+def last_residual_kernel(pairs, all_ref, mask_ref, r_in_ref, c_ref, r_ref, home_ref, w_ref, terms_ref, stack_ref):
+    iterate_core(pairs, all_ref, mask_ref, r_in_ref, c_ref, r_ref, w_ref, terms_ref, stack_ref)
     part = masked_sum(mask_ref, r_ref)
     n_win, count = home_ref.shape[0], home_ref.shape[1]
     rows_dev = r_ref.shape[1] * LANES // n_win
@@ -267,19 +262,25 @@
         home_ref[j] = jnp.where(lane < rows_dev, piece, part)
 
 
+def carry_kernel(lane_id, x_ref, o_ref):
+    total = jnp.sum(x_ref[...], axis=0)
+    lane = lax.broadcasted_iota(jnp.int32, total.shape, 1)
+    row = lax.broadcasted_iota(jnp.int32, total.shape, 0)
+    o_ref[...] = jnp.full(o_ref.shape, jnp.sum(jnp.where((lane == lane_id) & (row == 0), total, 0.0)), jnp.float32)
+
+
 def spectrum_kernel(
-    pairs, all_ref, mask_ref, r_in_ref, c_hbm, table_ref, o_ref, c_ref, w_ref, terms_ref, stack_ref, sems
+    pairs, all_ref, mask_ref, r_in_ref, c_ref, table_ref, o_ref, spread_ref, w_ref, terms_ref, stack_ref
 ):
-    start_all(c_hbm, c_ref, sems)
-    set_weights(pairs, jnp.sum(all_ref[...]) * (1.0 / LANES), mask_ref, r_in_ref, w_ref)
+    spread = set_weights(pairs, jnp.sum(all_ref[...]) * (1.0 / LANES), mask_ref, r_in_ref, w_ref)
 
     def one(s, carry):
-        pltpu.make_async_copy(c_hbm.at[s], c_ref.at[s], sems.at[s]).wait()
         weighted_sums(c_ref, s, w_ref.at[s], terms_ref)
         return carry
 
     lax.fori_loop(0, c_ref.shape[0], one, 0)
     finish_stacks(terms_ref, stack_ref)
+    spread_ref[...] = jnp.full(spread_ref.shape, spread, jnp.float32)
     lane = lax.broadcasted_iota(jnp.int32, (L, LANES), 1)
     stacks = stack_ref[0]
     for s in range(1, c_ref.shape[0]):
@@ -322,7 +323,6 @@
 
 VMEM = pl.BlockSpec(memory_space=pltpu.VMEM)
 SMEM = pl.BlockSpec(memory_space=pltpu.SMEM)
-ANY = pl.BlockSpec(memory_space=pl.ANY)
 
 
 def body(spectra, sources, valid):
@@ -386,25 +386,33 @@
         )(flat)
         moved = lax.all_to_all(packed, "win", 0, 0, tiled=True)
 
+    freq_id = win * n_ch + ch
+    modulus = 4 * freq_count * P_SIZE
+    device = jnp.arange(n_all, dtype=jnp.int32)
+    coarse = (device % n_ch) * chan_dev + (device // n_ch) * Q
+    cosines, sines = cos_sin(freq_id, coarse, P_SIZE, modulus)
+    fine_cos, fine_sin = cos_sin(freq_id, (jnp.arange(LANES, dtype=jnp.int32) // 4) % Q, P_SIZE, modulus)
+    moved, cosines, sines, fine_cos, fine_sin = lax.optimization_barrier(
+        (moved, cosines, sines, fine_cos, fine_sin)
+    )
+
     corr_shape = jax.ShapeDtypeStruct((source_total, L, rows), jnp.bfloat16)
     r_shape = jax.ShapeDtypeStruct((source_total, rows // LANES, LANES), jnp.float32)
     mask_shape = jax.ShapeDtypeStruct((rows // LANES, LANES), jnp.float32)
     part_shape = jax.ShapeDtypeStruct((n_all, LANES), jnp.float32)
-    held = pltpu.VMEM(corr_shape.shape, jnp.bfloat16)
     row_weights = pltpu.VMEM(r_shape.shape, jnp.float32)
     terms = pltpu.VMEM((source_total, L + 16, 3 * LANES), jnp.bfloat16)
     stack = pltpu.VMEM((source_total, L, LANES), jnp.float32)
     cross = pltpu.VMEM((rows // 2, width), jnp.bfloat16)
-    sems = pltpu.SemaphoreType.DMA((source_total,))
     corr, r, part, mask = pl.pallas_call(
         correlate_kernel,
-        in_specs=[SMEM, VMEM, VMEM, VMEM],
-        out_specs=[ANY, VMEM, VMEM, VMEM],
+        in_specs=[SMEM] + [VMEM] * 4,
+        out_specs=[VMEM] * 4,
         out_shape=[corr_shape, r_shape, part_shape, mask_shape],
-        scratch_shapes=[cross, cross, held, terms, stack, sems],
-        compiler_params=pltpu.CompilerParams(vmem_limit_bytes=56 << 20),
+        scratch_shapes=[cross, cross, terms, stack],
+        compiler_params=PARAMS,
         name="correlate",
-    )(ids, moved.reshape(rows, width), jnp.concatenate([mine, theirs]), jnp.asarray(inverse_np, jnp.bfloat16))
+    )(ids, moved.reshape(rows, width), mine, theirs, jnp.asarray(inverse_np, jnp.bfloat16))
 
     parts = lax.all_to_all(part, ("win", "ch"), 0, 0, tiled=True)
     for kernel, shape in (
@@ -413,37 +421,41 @@
     ):
         r, part = pl.pallas_call(
             lambda *refs: kernel(pairs, *refs),
-            in_specs=[VMEM, VMEM, VMEM, ANY],
+            in_specs=[VMEM] * 4,
             out_specs=[VMEM, VMEM],
             out_shape=[r_shape, shape],
-            scratch_shapes=[held, row_weights, terms, stack, sems],
-            compiler_params=BIG,
+            scratch_shapes=[row_weights, terms, stack],
+            compiler_params=PARAMS,
             name="iterate",
         )(parts, mask, r, corr)
         if kernel is iterate_kernel:
             parts = lax.all_to_all(part, ("win", "ch"), 0, 0, tiled=True)
 
     back = lax.all_to_all(part, "win", 0, 0, tiled=True)
-    over_win = jnp.sum(back[:, 0, rows_dev])
-    parts = lax.all_to_all(jnp.broadcast_to(over_win, (n_ch, LANES)), "ch", 0, 0, tiled=True)
-
-    spectrum = pl.pallas_call(
+    over_win = pl.pallas_call(
+        lambda *refs: carry_kernel(rows_dev, *refs),
+        in_specs=[VMEM],
+        out_specs=VMEM,
+        out_shape=jax.ShapeDtypeStruct((n_ch, LANES), jnp.float32),
+        compiler_params=PARAMS,
+        name="carry",
+    )(back)
+    parts = lax.all_to_all(over_win, "ch", 0, 0, tiled=True)
+
+    spectrum, spread_sq = pl.pallas_call(
         lambda *refs: spectrum_kernel(pairs, *refs),
-        in_specs=[VMEM, VMEM, VMEM, ANY, VMEM],
-        out_specs=VMEM,
-        out_shape=jax.ShapeDtypeStruct((freq_count, LANES), jnp.float32),
-        scratch_shapes=[held, row_weights, terms, stack, sems],
-        compiler_params=BIG,
+        in_specs=[VMEM] * 5,
+        out_specs=[VMEM] * 2,
+        out_shape=[
+            jax.ShapeDtypeStruct((freq_count, LANES), jnp.float32),
+            jax.ShapeDtypeStruct((8, LANES), jnp.float32),
+        ],
+        scratch_shapes=[row_weights, terms, stack],
+        compiler_params=PARAMS,
         name="spectrum",
     )(parts, mask, r, corr, jnp.asarray(forward_np))
     pieces = lax.all_to_all(spectrum, ("win", "ch"), 0, 0, tiled=True)
 
-    freq_id = win * n_ch + ch
-    modulus = 4 * freq_count * P_SIZE
-    device = jnp.arange(n_all, dtype=jnp.int32)
-    coarse = (device % n_ch) * chan_dev + (device // n_ch) * Q
-    cosines, sines = cos_sin(freq_id, coarse, P_SIZE, modulus)
-    fine_cos, fine_sin = cos_sin(freq_id, (jnp.arange(LANES, dtype=jnp.int32) // 4) % Q, P_SIZE, modulus)
     beamed = pl.pallas_call(
         lambda *refs: beam_kernel(chans ** (-0.5), *refs),
         in_specs=[VMEM] * 5,
@@ -453,8 +465,7 @@
         name="beam",
     )(pieces, cosines, sines, fine_cos, fine_sin)
 
-    window_count = jnp.sum(mask) * (1.0 / Q)
-    spread_sq = jnp.sum(parts[:, 0]) / (pairs * window_count) + epsilon
+    own_mask, back, spread_sq = lax.optimization_barrier((own_mask, back, spread_sq[0, 0]))
     residual = back[:, :, :rows_dev].reshape(n_win, source_total, win_dev // 4, Q, 4)
     residual = residual.transpose(2, 4, 1, 0, 3).reshape(win_dev, source_total, chan_dev)
     weights = own_mask[:, None, None] * (degrees + 1.0) / (degrees + residual / spread_sq)

time: 212 us -> 196 us (0.925)
  blocking collectives: 0 us -> 62.2 us
  waiting for transfers between devices: 84.6 us -> 54.1 us
  starting transfers between devices: 59.5 us -> 32.9 us
  Pallas kernels: 43.5 us -> 33.3 us
  local copies, waits for them, and re-layouts: 13.6 us -> 5.07 us
    all_to_all x0 -> x4, blocking collectives: none -> 62.2 us  [the longest x2 40.8 us: body(): parts = lax.all_to_all(part, ('win', 'ch'), 0, 0, tiled=True)]
    all_to_all x4 -> x0, waiting for transfers between devices: 34.9 us -> none  [the longest x2 24.7 us: body(): parts = lax.all_to_all(part, ('win', 'ch'), 0, 0, tiled=True)]
    all_to_all x4 -> x0, starting transfers between devices: 24.5 us -> none  [the longest x2 15.3 us: body(): parts = lax.all_to_all(part, ('win', 'ch'), 0, 0, tiled=True)]
    pallas_call x3 -> x4, Pallas kernels: 30.9 us -> 23.2 us  [the longest x1 14.1 us: body(): pl.pallas_call(correlate_kernel, in_specs=[SMEM] + [VMEM] * 4, out_specs=...]
    unnamed x23, local copies, waits for them, and re-layouts: 8.69 us -> 3.9 us
    concatenate x1 -> x0, local copies, waits for them, and re-layouts: 2.93 us -> none  [body(): jnp.concatenate([mine, theirs])]
    ppermute x3, waiting for transfers between devices: 20 us -> 22.6 us  [body(): lax.ppermute(own, 'ch', turn_y(d))]
    pallas_call x1, Pallas kernels: 6.17 us -> 3.73 us  [body(): pl.pallas_call(lambda *refs: spectrum_kernel(pairs, *refs), in_specs=[VME...]
  transfers between devices with their start and end apart: 12 -> 8, of which waited for: 11 -> 7; matrix products, arithmetic and copies ran while one was open for 7% -> 4% of each run, Pallas kernels for 1% -> 1%
where the time goes in v3:
time: 196 us
  blocking collectives  62.2 us (32%)
  waiting for transfers between devices  54.1 us (28%)
  Pallas kernels  33.3 us (17%)
  starting transfers between devices  32.9 us (17%)
  other arithmetic  7.26 us (4%)
  local copies, waits for them, and re-layouts  5.07 us (3%)
    all_to_all x2, blocking collectives, body(): parts = lax.all_to_all(part, ('win', 'ch'), 0, 0, tiled=True)  40.8 us
    ppermute x3, waiting for transfers between devices, body(): lax.ppermute(own, 'ch', turn_y(d))  22.6 us
    pallas_call x1, Pallas kernels, body(): pl.pallas_call(correlate_kernel, in_specs=[SMEM] + [VMEM] * 4, out_specs=...  14.1 us
    all_to_all x1, blocking collectives, body(): back = lax.all_to_all(part, 'win', 0, 0, tiled=True)  12.4 us
    all_to_all x1, waiting for transfers between devices, body(): own = lax.all_to_all(own, 'win', 0, 0, tiled=True)  10.9 us
    all_to_all x1, waiting for transfers between devices, body(): pieces = lax.all_to_all(spectrum, ('win', 'ch'), 0, 0, tiled=True)  10.8 us
    all_to_all x1, starting transfers between devices, body(): own = lax.all_to_all(own, 'win', 0, 0, tiled=True)  10.5 us
    all_to_all x1, blocking collectives, body(): parts = lax.all_to_all(over_win, 'ch', 0, 0, tiled=True)  9.06 us
  transfers between devices with their start and end apart: 8, of which 7 were waited for; matrix products, arithmetic and copies ran while one was open for 4% of the time, Pallas kernels for 1%

profile of v3, /device:TPU:1, one launch (start us, length us, event | category | flops | bytes accessed | tf_op | source)
XLA Modules:
  0.0 195.7 jit_solution(15675202175713106401)
XLA Ops:
  0.6 1.4 copy-done
  2.1 0.7 copy-done.8
  2.7 1.7 pick.1
  4.4 6.5 %all-to-all-start.1 = ((bf16[8,48,128]{2,1,0:T(8,128)(2,1)}), bf16[8,48,128]{2,1,0:T(8,128)(2,1)S(1)}, u32[]{:S(2)}, u32[]{:S(2)}) async-start(bf16[8,48,128]{2,1,0:T(8,128)(2,1)} %pick.1), calls=%async_computation.1 | async-start | bytes 196608 | tf_op jit(solution)/shard_map/all_to_all | solution.py:353
  10.8 0.1 broadcast_in_dim.4
  10.9 0.1 reshape.90
  11.0 4.8 %all-to-all-done.1.x_ref = bf16[8,48,128]{2,1,0:T(8,128)(2,1)S(1)} async-done(((bf16[8,48,128]{2,1,0:T(8,128)(2,1)}), bf16[8,48,128]{2,1,0:T(8,128)(2,1)S(1)}, u32[]{:S(2)}, u32[]{:S(2)}) %all-to-all-start.1) | async-done | bytes 98336 | tf_op jit(solution)/shard_map/all_to_all | solution.py:353
  15.8 0.8 own.1
  16.7 10.5 %all-to-all-start.2 = ((bf16[32,56,128]{2,1,0:T(8,128)(2,1)}), bf16[32,56,128]{2,1,0:T(8,128)(2,1)S(1)}, u32[]{:S(2)}, u32[]{:S(2)}) async-start(bf16[32,56,128]{2,1,0:T(8,128)(2,1)} %own.1), calls=%async_computation.2 | async-start | bytes 917504 | tf_op jit(solution)/shard_map/all_to_all | solution.py:365
  27.2 0.0 copy-done.1
  27.2 2.2 %pack.1 = bf16[32,48,512]{2,1,0:T(8,128)(2,1)} custom-call(bf16[1536,512]{1,0:T(8,128)(2,1)S(1)} %bitcast.28), custom_call_target="tpu_custom_call" | custom-call | tf_op jit(solution)/shard_map/main/pack/pallas_call | solution.py:379
  29.4 10.9 %all-to-all-done.2 = bf16[32,56,128]{2,1,0:T(8,128)(2,1)S(1)} async-done(((bf16[32,56,128]{2,1,0:T(8,128)(2,1)}), bf16[32,56,128]{2,1,0:T(8,128)(2,1)S(1)}, u32[]{:S(2)}, u32[]{:S(2)}) %all-to-all-start.2) | async-done | bytes 458784 | tf_op jit(solution)/shard_map/all_to_all | solution.py:365
  40.3 7.6 %all-to-all-start = ((bf16[32,48,512]{2,1,0:T(8,128)(2,1)}), bf16[32,48,512]{2,1,0:T(8,128)(2,1)S(1)}, u32[]{:S(2)}, u32[]{:S(2)}) async-start(bf16[32,48,512]{2,1,0:T(8,128)(2,1)} %pack.1), calls=%async_computation | async-start | bytes 3145728 | tf_op jit(solution)/shard_map/main/all_to_all | solution.py:387
  47.8 1.0 collective-permute-start.2
  48.8 1.2 collective-permute-start.1
  50.0 0.0 collective-permute-start
  50.0 8.6 %collective-permute-done.2 = bf16[32,56,128]{2,1,0:T(8,128)(2,1)S(1)} collective-permute-done((bf16[32,56,128]{2,1,0:T(8,128)(2,1)S(1)}, bf16[32,56,128]{2,1,0:T(8,128)(2,1)S(1)}, u32[]{:S(2)}, u32[]{:S(2)}) %collective-permute-start.2) | collective-permute-done | bytes 458784 | tf_op jit(solution)/shard_map/along_y/ppermute | solution.py:371
  58.6 2.2 %collective-permute-done.1 = bf16[32,56,128]{2,1,0:T(8,128)(2,1)S(1)} collective-permute-done((bf16[32,56,128]{2,1,0:T(8,128)(2,1)S(1)}, bf16[32,56,128]{2,1,0:T(8,128)(2,1)S(1)}, u32[]{:S(2)}, u32[]{:S(2)}) %collective-permute-start.1) | collective-permute-done | bytes 458784 | tf_op jit(solution)/shard_map/along_y/ppermute | solution.py:371
  60.8 11.8 %collective-permute-done = bf16[32,56,128]{2,1,0:T(8,128)(2,1)S(1)} collective-permute-done((bf16[32,56,128]{2,1,0:T(8,128)(2,1)S(1)}, bf16[32,56,128]{2,1,0:T(8,128)(2,1)S(1)}, u32[]{:S(2)}, u32[]{:S(2)}) %collective-permute-start) | collective-permute-done | bytes 458784 | tf_op jit(solution)/shard_map/along_y/ppermute | solution.py:371
  72.6 0.0 copy-done.9
  72.6 1.2 pad_maximum_fusion.x_ref
  73.8 0.6 collective-permute-start.3
  74.4 0.1 pad_add_fusion.ids_ref
  74.5 1.9 fusion.8
  76.4 3.2 %fusion.6 = (f32[256,512]{1,0:T(8,128)}, f32[256,512]{1,0:T(8,128)}) fusion(s32[512]{0:T(512)S(1)} %iota_add_fusion, s32[256]{0:T(256)S(1)} %fusion.14), kind=kLoop, calls=%fused_computation.18 | loop fusion | flops 1835008 | bytes 1051648 | tf_op jit(solution)/shard_map/sin | solution.py:321
  79.6 5.0 %all-to-all-done = bf16[32,48,512]{2,1,0:T(8,128)(2,1)S(1)} async-done(((bf16[32,48,512]{2,1,0:T(8,128)(2,1)}), bf16[32,48,512]{2,1,0:T(8,128)(2,1)S(1)}, u32[]{:S(2)}, u32[]{:S(2)}) %all-to-all-start) | async-done | bytes 1572896 | tf_op jit(solution)/shard_map/main/all_to_all | solution.py:387
  84.7 0.0 collective-permute-done.3.y_ref
  84.7 0.9 copy-done.7
  85.6 14.1 %correlate.1 = (bf16[8,256,1536]{2,1,0:T(8,128)(2,1)S(1)}, f32[8,12,128]{2,1,0:T(8,128)S(1)}, f32[256,128]{1,0:T(8,128)S(1)}, f32[12,128]{1,0:T(8,128)S(1)}) custom-call(s32[8]{0:T(128)S(1)} %pad_add_fusion.ids_ref, bf16[1536,512]{1,0:T(8,128)(2,1)S(1)} %bitcast.29, bf16[4,32,56,128]{3,2,1,0:T(8,128)(2,1)S(1)} %pad_maximum_fusion.x_ref, ...), custom_call_target="tpu_custom_call" | custom-call | tf_op jit(solution)/shard_map/correlate/pallas_call | solution.py:407
  99.7 22.5 %all_to_all.64 = f32[256,1,128]{2,1,0:T(1,128)S(1)} all-to-all(f32[256,1,128]{2,1,0:T(1,128)S(1)} %bitcast.33), channel_id=1, replica_groups=mesh['win'=32,'ch'=8] {'win','ch'}, dimensions={0} | all-to-all | bytes 262144 | tf_op jit(solution)/shard_map/all_to_all | solution.py:417
  122.3 4.5 %iterate.2 = (f32[8,12,128]{2,1,0:T(8,128)S(1)}, f32[256,128]{1,0:T(8,128)S(1)}) custom-call(f32[256,128]{1,0:T(8,128)S(1)} %bitcast.30, f32[12,128]{1,0:T(8,128)S(1)} %get-tuple-element.22.refs_1_, f32[8,12,128]{2,1,0:T(8,128)S(1)} %get-tuple-element.23.refs_2_, bf16[8,256,1536]{2,1,0:T(8,128)(2,1)S(1)} %get-tuple-element.24.refs_3_), custom_call_target="tpu_custom_call" | custom-call | tf_op jit(solution)/shard_map/iterate/pallas_call | solution.py:422
  126.8 18.2 %all_to_all.65 = f32[256,1,128]{2,1,0:T(1,128)S(1)} all-to-all(f32[256,1,128]{2,1,0:T(1,128)S(1)} %bitcast.34), channel_id=1, replica_groups=mesh['win'=32,'ch'=8] {'win','ch'}, dimensions={0} | all-to-all | bytes 262144 | tf_op jit(solution)/shard_map/all_to_all | solution.py:432
  145.0 4.5 %iterate.3 = (f32[8,12,128]{2,1,0:T(8,128)S(1)}, f32[32,8,128]{2,1,0:T(8,128)S(1)}) custom-call(f32[256,128]{1,0:T(8,128)S(1)} %bitcast.31, f32[12,128]{1,0:T(8,128)S(1)} %get-tuple-element.22.refs_1_, f32[8,12,128]{2,1,0:T(8,128)S(1)} %get-tuple-element.26.refs_2_, bf16[8,256,1536]{2,1,0:T(8,128)(2,1)S(1)} %get-tuple-element.24.refs_3_), custom_call_target="tpu_custom_call" | custom-call | tf_op jit(solution)/shard_map/iterate/pallas_call | solution.py:422
  149.5 12.4 %all_to_all.66.refs_0_ = f32[32,8,128]{2,1,0:T(8,128)S(1)} all-to-all(f32[32,8,128]{2,1,0:T(8,128)S(1)} %get-tuple-element.27), channel_id=1, replica_groups=mesh['win'=32,'ch'=8] {'win'}, dimensions={0} | all-to-all | bytes 262144 | tf_op jit(solution)/shard_map/all_to_all | solution.py:434
  161.9 0.2 carry.1
  162.0 9.1 %all_to_all.67 = f32[8,1,128]{2,1,0:T(1,128)S(1)} all-to-all(f32[8,1,128]{2,1,0:T(1,128)S(1)} %bitcast.36), channel_id=1, replica_groups=mesh['win'=32,'ch'=8] {'ch'}, dimensions={0} | all-to-all | bytes 8192 | tf_op jit(solution)/shard_map/all_to_all | solution.py:443
  171.1 3.7 %spectrum.1 = (f32[256,128]{1,0:T(8,128)}, f32[8,128]{1,0:T(8,128)S(1)}) custom-call(f32[8,128]{1,0:T(8,128)S(1)} %bitcast.35, f32[12,128]{1,0:T(8,128)S(1)} %get-tuple-element.22.refs_1_, f32[8,12,128]{2,1,0:T(8,128)S(1)} %get-tuple-element.28.refs_2_, bf16[8,256,1536]{2,1,0:T(8,128)(2,1)S(1)} %get-tuple-element.24.refs_3_, f32[512,256]{1,0:T(8,128)S(1)} %copy-done.6), custom_call_target="tpu_custom_call" | custom-call | tf_op jit(solution)/shard_map/spectrum/pallas_call | solution.py:445
  174.8 0.5 slice.6
  175.3 5.7 %all-to-all-start.7 = ((f32[256,1,128]{2,1,0:T(1,128)}), f32[256,1,128]{2,1,0:T(1,128)S(1)}, u32[]{:S(2)}, u32[]{:S(2)}) async-start(f32[256,1,128]{2,1,0:T(1,128)} %bitcast.20), calls=%async_computation.7 | async-start | bytes 262144 | tf_op jit(solution)/shard_map/all_to_all | solution.py:457
  181.0 0.7 divide_add_fusion
  181.7 0.0 copy-start.2
  181.7 0.0 copy-start.3
  181.7 0.1 copy.14
  181.9 0.3 copy.15
  182.2 0.1 broadcast_divide_fusion
  182.4 0.9 copy.17
  183.2 10.8 %all-to-all-done.7 = f32[256,1,128]{2,1,0:T(1,128)S(1)} async-done(((f32[256,1,128]{2,1,0:T(1,128)}), f32[256,1,128]{2,1,0:T(1,128)S(1)}, u32[]{:S(2)}, u32[]{:S(2)}) %all-to-all-start.7) | async-done | bytes 131104 | tf_op jit(solution)/shard_map/all_to_all | solution.py:457
  194.0 1.7 beam.1
  (23 shorter events, 0.1 us)
Async XLA Ops:
  0.6 10.2 %copy-start.10 = (s32[12]{0:T(128)S(1)}, s32[12]{0:T(128)}, u32[]{:S(2)}) copy-start(s32[12]{0:T(128)} %param.7) | copy-start | bytes 148
  0.6 1.4 copy-start
  2.1 0.7 copy-start.8
  2.7 24.5 %copy-start.1 = (bf16[12,128,512]{2,1,0:T(8,128)(2,1)S(1)}, bf16[12,128,512]{2,1,0:T(8,128)(2,1)}, u32[]{:S(2)}) copy-start(bf16[12,128,512]{2,1,0:T(8,128)(2,1)} %param.5) | copy-start | bytes 4718596
  4.4 11.5 %all-to-all-start.1 = ((bf16[8,48,128]{2,1,0:T(8,128)(2,1)}), bf16[8,48,128]{2,1,0:T(8,128)(2,1)S(1)}, u32[]{:S(2)}, u32[]{:S(2)}) async-start(bf16[8,48,128]{2,1,0:T(8,128)(2,1)} %pick.1), calls=%async_computation.1 | async-start | bytes 196608 | tf_op jit(solution)/shard_map/all_to_all | solution.py:353
  16.7 23.6 %all-to-all-start.2 = ((bf16[32,56,128]{2,1,0:T(8,128)(2,1)}), bf16[32,56,128]{2,1,0:T(8,128)(2,1)S(1)}, u32[]{:S(2)}, u32[]{:S(2)}) async-start(bf16[32,56,128]{2,1,0:T(8,128)(2,1)} %own.1), calls=%async_computation.2 | async-start | bytes 917504 | tf_op jit(solution)/shard_map/all_to_all | solution.py:365
  40.3 32.3 %copy-start.9 = (bf16[32,56,128]{2,1,0:T(8,128)(2,1)}, bf16[32,56,128]{2,1,0:T(8,128)(2,1)S(1)}, u32[]{:S(2)}) copy-start(bf16[32,56,128]{2,1,0:T(8,128)(2,1)S(1)} %all-to-all-done.2) | copy-start | bytes 1376260
  40.3 44.4 %all-to-all-start = ((bf16[32,48,512]{2,1,0:T(8,128)(2,1)}), bf16[32,48,512]{2,1,0:T(8,128)(2,1)S(1)}, u32[]{:S(2)}, u32[]{:S(2)}) async-start(bf16[32,48,512]{2,1,0:T(8,128)(2,1)} %pack.1), calls=%async_computation | async-start | bytes 3145728 | tf_op jit(solution)/shard_map/main/all_to_all | solution.py:387
  47.8 10.8 %collective-permute-start.2 = (bf16[32,56,128]{2,1,0:T(8,128)(2,1)S(1)}, bf16[32,56,128]{2,1,0:T(8,128)(2,1)S(1)}, u32[]{:S(2)}, u32[]{:S(2)}) collective-permute-start(bf16[32,56,128]{2,1,0:T(8,128)(2,1)S(1)} %all-to-all-done.2), channel_id=1, source_target_pairs={{0,6},{1,7},{2,0},{3,1},{4,2},{5,3},{6,4},{7,5},{8,14},{9,15},{10,... | collective-permute-start | bytes 1376264 | tf_op jit(solution)/shard_map/along_y/ppermute | solution.py:371
  48.8 12.0 %collective-permute-start.1 = (bf16[32,56,128]{2,1,0:T(8,128)(2,1)S(1)}, bf16[32,56,128]{2,1,0:T(8,128)(2,1)S(1)}, u32[]{:S(2)}, u32[]{:S(2)}) collective-permute-start(bf16[32,56,128]{2,1,0:T(8,128)(2,1)S(1)} %all-to-all-done.2), channel_id=1, source_target_pairs={{0,4},{1,5},{2,6},{3,7},{4,0},{5,1},{6,2},{7,3},{8,12},{9,13},{10,... | collective-permute-start | bytes 1376264 | tf_op jit(solution)/shard_map/along_y/ppermute | solution.py:371
  50.0 22.6 %collective-permute-start = (bf16[32,56,128]{2,1,0:T(8,128)(2,1)S(1)}, bf16[32,56,128]{2,1,0:T(8,128)(2,1)S(1)}, u32[]{:S(2)}, u32[]{:S(2)}) collective-permute-start(bf16[32,56,128]{2,1,0:T(8,128)(2,1)S(1)} %all-to-all-done.2), channel_id=1, source_target_pairs={{0,2},{1,3},{2,4},{3,5},{4,6},{5,7},{6,0},{7,1},{8,10},{9,11},{10,... | collective-permute-start | bytes 1376264 | tf_op jit(solution)/shard_map/along_y/ppermute | solution.py:371
  73.8 10.8 %collective-permute-start.3 = (bf16[4,32,56,128]{3,2,1,0:T(8,128)(2,1)S(1)}, bf16[4,32,56,128]{3,2,1,0:T(8,128)(2,1)}, u32[]{:S(2)}, u32[]{:S(2)}) collective-permute-start(bf16[4,32,56,128]{3,2,1,0:T(8,128)(2,1)S(1)} %pad_maximum_fusion.x_ref), channel_id=1, source_target_pairs={{0,1},{1,0},{2,3},{3,2},{4,5},{5,4},{6,7},{7,6},{8,9},{9,8},{10,11... | collective-permute-start | bytes 5505032 | tf_op jit(solution)/shard_map/cores/ppermute | solution.py:373
  84.7 1.0 copy-start.7
  145.0 26.1 %copy-start.6 = (f32[512,256]{1,0:T(8,128)S(1)}, f32[512,256]{1,0:T(8,128)}, u32[]{:S(2)}) copy-start(f32[512,256]{1,0:T(8,128)} %constant.139.clone.refs_4_) | copy-start | bytes 1572868
  175.3 18.7 %all-to-all-start.7 = ((f32[256,1,128]{2,1,0:T(1,128)}), f32[256,1,128]{2,1,0:T(1,128)S(1)}, u32[]{:S(2)}, u32[]{:S(2)}) async-start(f32[256,1,128]{2,1,0:T(1,128)} %bitcast.20), calls=%async_computation.7 | async-start | bytes 262144 | tf_op jit(solution)/shard_map/all_to_all | solution.py:457
  181.7 12.3 %copy-start.2 = (f32[256,512]{1,0:T(8,128)S(1)}, f32[256,512]{1,0:T(8,128)}, u32[]{:S(2)}) copy-start(f32[256,512]{1,0:T(8,128)} %get-tuple-element.35.refs_2_) | copy-start | bytes 1572868
  181.7 12.3 %copy-start.3 = (f32[256,512]{1,0:T(8,128)S(1)}, f32[256,512]{1,0:T(8,128)}, u32[]{:S(2)}) copy-start(f32[256,512]{1,0:T(8,128)} %get-tuple-element.34.refs_1_) | copy-start | bytes 1572868
  181.7 12.3 %copy-start.4 = (f32[128,512]{1,0:T(8,128)S(1)}, f32[128,512]{1,0:T(8,128)}, u32[]{:S(2)}) copy-start(f32[128,512]{1,0:T(8,128)} %get-tuple-element.37.refs_4_) | copy-start | bytes 786436
  181.7 12.3 %copy-start.5 = (f32[128,512]{1,0:T(8,128)S(1)}, f32[128,512]{1,0:T(8,128)}, u32[]{:S(2)}) copy-start(f32[128,512]{1,0:T(8,128)} %get-tuple-element.36.refs_3_) | copy-start | bytes 786436

commit v4 on v3

--- a/solution.py
+++ b/solution.py
@@ -115,11 +115,18 @@
         terms_ref[s, L:L + 16, i * LANES:(i + 1) * LANES] = term
 
 
-def finish_stacks(terms_ref, stack_ref):
-    group = same_channel()
-    for s in range(terms_ref.shape[0]):
-        sums = jnp.dot(terms_ref[s], group, preferred_element_type=jnp.float32)
-        stack_ref[s] = sums[:L] * (1.0 / sums[L:L + 1])
+def finish_stack(terms_ref, s, stack_ref):
+    sums = jnp.dot(terms_ref[s], same_channel(), preferred_element_type=jnp.float32)
+    stack_ref[s] = sums[:L] * (1.0 / sums[L:L + 1])
+
+
+def all_stacks(c_ref, w_ref, terms_ref, stack_ref):
+    count = c_ref.shape[0]
+    for s in range(count):
+        weighted_sums(c_ref, s, w_ref.at[s], terms_ref)
+        if s:
+            finish_stack(terms_ref, s - 1, stack_ref)
+    finish_stack(terms_ref, count - 1, stack_ref)
 
 
 def residuals(c_ref, s, stack_ref, r_ref):
@@ -137,17 +144,21 @@
 
 
 def correlate_kernel(
-    ids_ref, a_ref, x_ref, y_ref, inv_ref, c_ref, r_ref, part_ref, mask_ref, even_ref, odd_ref, terms_ref, stack_ref
+    ids_ref, a_ref, x_ref, y_ref, masks_ref, inv_hbm, c_ref, r_ref, part_ref, mask_ref, even_ref, odd_ref, terms_ref, stack_ref, inv_ref, sem
 ):
+    table = pltpu.make_async_copy(inv_hbm, inv_ref, sem)
+    table.start()
     n_win, rows = x_ref.shape[1], a_ref.shape[0]
     half = a_ref.shape[1] // 2
     rows_dev = rows // n_win
+    z_size, x_size = 8, n_win // 8
+    far = [(ids_ref[8] - x + x_size) % x_size * z_size for x in range(x_size)]
     low = lax.broadcasted_iota(jnp.int32, (8, LANES), 0) < 4
 
     lane = lax.broadcasted_iota(jnp.int32, (8, LANES), 1)
     pieces = [jnp.zeros((8, LANES), jnp.float32) for _ in range(rows // LANES)]
     for j in range(n_win):
-        row = x_ref[0, j, 48:56, :].astype(jnp.float32)
+        row = masks_ref[far[j // z_size] + j % z_size].astype(jnp.float32)
         b, off = divmod(j * rows_dev, LANES)
         turned = pltpu.roll(row, off, 1) if off else row
         end = off + rows_dev
@@ -162,11 +173,12 @@
 
     def fill(cross_ref, s_ref, k, side):
         for j in range(half_win):
+            held = far[(side * half_win + j) // z_size] + j % z_size
             for t in range(3):
                 quarters = []
                 for p in range(2):
                     at = t * 16 + p * 8
-                    tile = s_ref[k, side * half_win + j, at:at + 8, :].astype(jnp.float32)
+                    tile = s_ref[k, held, at:at + 8, :].astype(jnp.float32)
                     turned = pltpu.roll(tile, 4, 0)
                     quarters += [jnp.where(low, tile, turned), jnp.where(low, turned, tile)]
                 at = slice(j * rows_dev + t * 16, j * rows_dev + t * 16 + 16)
@@ -190,6 +202,7 @@
             c_ref[s, :, at:at + 256] = got.astype(jnp.bfloat16)
 
     fill(even_ref, x_ref, 0, 0)
+    table.wait()
     pairs_of_slots = count // 2
 
     def slot(k, carry):
@@ -203,10 +216,10 @@
             correlate(odd_ref, s, 1)
             fill(even_ref, next_ref, next_k, 0)
             weighted_sums(c_ref, s, mask_ref, terms_ref)
+            finish_stack(terms_ref, s, stack_ref)
         return carry
 
     lax.fori_loop(0, pairs_of_slots, slot, 0)
-    finish_stacks(terms_ref, stack_ref)
 
     def last(s, carry):
         residuals(c_ref, s, stack_ref, r_ref)
@@ -226,12 +239,7 @@
 def iterate_core(pairs, all_ref, mask_ref, r_in_ref, c_ref, r_ref, w_ref, terms_ref, stack_ref):
     set_weights(pairs, jnp.sum(all_ref[...]) * (1.0 / LANES), mask_ref, r_in_ref, w_ref)
 
-    def one(s, carry):
-        weighted_sums(c_ref, s, w_ref.at[s], terms_ref)
-        return carry
-
-    lax.fori_loop(0, c_ref.shape[0], one, 0)
-    finish_stacks(terms_ref, stack_ref)
+    all_stacks(c_ref, w_ref, terms_ref, stack_ref)
 
     def last(s, carry):
         residuals(c_ref, s, stack_ref, r_ref)
@@ -274,12 +282,7 @@
 ):
     spread = set_weights(pairs, jnp.sum(all_ref[...]) * (1.0 / LANES), mask_ref, r_in_ref, w_ref)
 
-    def one(s, carry):
-        weighted_sums(c_ref, s, w_ref.at[s], terms_ref)
-        return carry
-
-    lax.fori_loop(0, c_ref.shape[0], one, 0)
-    finish_stacks(terms_ref, stack_ref)
+    all_stacks(c_ref, w_ref, terms_ref, stack_ref)
     spread_ref[...] = jnp.full(spread_ref.shape, spread, jnp.float32)
     lane = lax.broadcasted_iota(jnp.int32, (L, LANES), 1)
     stacks = stack_ref[0]
@@ -341,39 +344,64 @@
     rows_dev = win_dev * Q
     rows = n_win * rows_dev
     piece = win_dev * width // LANES
+    z_size = 8
+    x_size = n_win // z_size
 
     picked = pl.pallas_call(
         pick_kernel,
-        in_specs=[SMEM, VMEM],
-        out_specs=VMEM,
+        grid_spec=pltpu.PrefetchScalarGridSpec(
+            num_scalar_prefetch=1,
+            grid=(1,),
+            in_specs=[pl.BlockSpec(flat.shape, lambda *_: (0, 0))],
+            out_specs=pl.BlockSpec((source_total, piece, LANES), lambda *_: (0, 0, 0)),
+        ),
         out_shape=jax.ShapeDtypeStruct((source_total, piece, LANES), jnp.bfloat16),
-        compiler_params=PARAMS,
         name="pick",
     )(sources, flat)
     got = lax.all_to_all(picked, "ch", 0, 0, tiled=True)
+    freq_id = win * n_ch + ch
+    modulus = 4 * freq_count * P_SIZE
+    device = jnp.arange(n_all, dtype=jnp.int32)
+    coarse = (device % n_ch) * chan_dev + (device // n_ch) * Q
+    cosines, sines = cos_sin(freq_id, coarse, P_SIZE, modulus)
+    fine_cos, fine_sin = cos_sin(freq_id, (jnp.arange(LANES, dtype=jnp.int32) // 4) % Q, P_SIZE, modulus)
+    got, cosines, sines, fine_cos, fine_sin = lax.optimization_barrier((got, cosines, sines, fine_cos, fine_sin))
     own_mask = valid.astype(jnp.float32)
     mask_lanes = jnp.broadcast_to(own_mask.reshape(win_dev // 4, 1, 4), (win_dev // 4, Q, 4)).reshape(1, rows_dev)
     own = pl.pallas_call(
         own_kernel,
         in_specs=[VMEM, VMEM],
         out_specs=VMEM,
-        out_shape=jax.ShapeDtypeStruct((n_win, piece + 8, LANES), jnp.bfloat16),
+        out_shape=jax.ShapeDtypeStruct((z_size, piece + 8, LANES), jnp.bfloat16),
         compiler_params=PARAMS,
         name="own",
     )(got, jnp.pad(mask_lanes, ((0, 0), (0, LANES - rows_dev))))
 
-    own = lax.all_to_all(own, "win", 0, 0, tiled=True)
+    along_z = [[x * z_size + z for z in range(z_size)] for x in range(x_size)]
+    own = lax.all_to_all(own, "win", 0, 0, tiled=True, axis_index_groups=along_z)
+
+    def turn_x(d):
+        return [(x * z_size + z, (x + d) % x_size * z_size + z) for x in range(x_size) for z in range(z_size)]
+
+    own = jnp.stack([own] + [lax.ppermute(own, "win", turn_x(d)) for d in range(1, x_size)])
+    own = own.reshape(n_win, piece + 8, LANES)
+    own, own_masks = own[:, :piece], own[:, piece:]
 
     def turn_y(d):
         return [(i * 2 + c, ((i + d) % 4) * 2 + c) for i in range(n_ch // 2) for c in range(2)]
 
     with jax.named_scope("along_y"):
-        mine = jnp.stack([own] + [lax.ppermute(own, "ch", turn_y(d)) for d in (1, 2, 3)])
+        below, above = lax.ppermute(own, "ch", turn_y(1)), lax.ppermute(own, "ch", turn_y(3))
+        far = [
+            lax.ppermute(below[:n_win // 2], "ch", turn_y(1)),
+            lax.ppermute(above[n_win // 2:], "ch", turn_y(3)),
+        ]
+        mine = jnp.concatenate([own, below] + far + [above]).reshape(4, n_win, piece, LANES)
     with jax.named_scope("cores"):
         theirs = lax.ppermute(mine, "ch", [(i, i ^ 1) for i in range(n_ch)])
     steps = jnp.arange(4, dtype=jnp.int32)
     slot_y = 2 * ((y - steps) % 4)
-    ids = jnp.concatenate([slot_y + core, slot_y + 1 - core]).astype(jnp.int32)
+    ids = jnp.concatenate([slot_y + core, slot_y + 1 - core, (win // z_size)[None]]).astype(jnp.int32)
 
     with jax.named_scope("main"):
         packed = pl.pallas_call(
@@ -386,16 +414,7 @@
         )(flat)
         moved = lax.all_to_all(packed, "win", 0, 0, tiled=True)
 
-    freq_id = win * n_ch + ch
-    modulus = 4 * freq_count * P_SIZE
-    device = jnp.arange(n_all, dtype=jnp.int32)
-    coarse = (device % n_ch) * chan_dev + (device // n_ch) * Q
-    cosines, sines = cos_sin(freq_id, coarse, P_SIZE, modulus)
-    fine_cos, fine_sin = cos_sin(freq_id, (jnp.arange(LANES, dtype=jnp.int32) // 4) % Q, P_SIZE, modulus)
-    moved, cosines, sines, fine_cos, fine_sin = lax.optimization_barrier(
-        (moved, cosines, sines, fine_cos, fine_sin)
-    )
-
+    inverse = pltpu.with_memory_space_constraint(jnp.asarray(inverse_np, jnp.bfloat16), pltpu.HBM)
     corr_shape = jax.ShapeDtypeStruct((source_total, L, rows), jnp.bfloat16)
     r_shape = jax.ShapeDtypeStruct((source_total, rows // LANES, LANES), jnp.float32)
     mask_shape = jax.ShapeDtypeStruct((rows // LANES, LANES), jnp.float32)
@@ -406,13 +425,15 @@
     cross = pltpu.VMEM((rows // 2, width), jnp.bfloat16)
     corr, r, part, mask = pl.pallas_call(
         correlate_kernel,
-        in_specs=[SMEM] + [VMEM] * 4,
+        in_specs=[SMEM] + [VMEM] * 4 + [pl.BlockSpec(memory_space=pl.ANY)],
         out_specs=[VMEM] * 4,
         out_shape=[corr_shape, r_shape, part_shape, mask_shape],
-        scratch_shapes=[cross, cross, terms, stack],
+        scratch_shapes=[
+            cross, cross, terms, stack, pltpu.VMEM((L, width), jnp.bfloat16), pltpu.SemaphoreType.DMA
+        ],
         compiler_params=PARAMS,
         name="correlate",
-    )(ids, moved.reshape(rows, width), mine, theirs, jnp.asarray(inverse_np, jnp.bfloat16))
+    )(ids, moved.reshape(rows, width), mine, theirs, own_masks, inverse)
 
     parts = lax.all_to_all(part, ("win", "ch"), 0, 0, tiled=True)
     for kernel, shape in (
@@ -465,7 +486,8 @@
         name="beam",
     )(pieces, cosines, sines, fine_cos, fine_sin)
 
-    own_mask, back, spread_sq = lax.optimization_barrier((own_mask, back, spread_sq[0, 0]))
+    own_mask, back, spread_sq = lax.optimization_barrier((own_mask, back, spread_sq))
+    spread_sq = spread_sq[0, 0]
     residual = back[:, :, :rows_dev].reshape(n_win, source_total, win_dev // 4, Q, 4)
     residual = residual.transpose(2, 4, 1, 0, 3).reshape(win_dev, source_total, chan_dev)
     weights = own_mask[:, None, None] * (degrees + 1.0) / (degrees + residual / spread_sq)

time: 196 us -> 190 us (0.969)
  waiting for transfers between devices: 54.1 us -> 43.1 us
  starting transfers between devices: 32.9 us -> 36.9 us
  blocking collectives: 62.2 us -> 64.2 us
    ppermute x3 -> x7, starting transfers between devices: 2.15 us -> 9.4 us  [the longest x3 3.68 us: body(): lax.ppermute(own, 'win', turn_x(d))]
    all_to_all x1, waiting for transfers between devices: 10.9 us -> 5.4 us  [body(): lax.all_to_all(own, 'win', 0, 0, tiled=True, axis_index_groups=along_z)]
    all_to_all x1, waiting for transfers between devices: 5.05 us -> 0.01 us  [body(): moved = lax.all_to_all(packed, 'win', 0, 0, tiled=True)]
    all_to_all x1, waiting for transfers between devices: 4.8 us -> 0.01 us  [body(): got = lax.all_to_all(picked, 'ch', 0, 0, tiled=True)]
    unnamed x23 -> x18, local copies, waits for them, and re-layouts: 3.9 us -> 0.99 us
    all_to_all x1, starting transfers between devices: 10.5 us -> 7.68 us  [body(): lax.all_to_all(own, 'win', 0, 0, tiled=True, axis_index_groups=along_z)]
    all_to_all x1, starting transfers between devices: 7.56 us -> 5.13 us  [body(): moved = lax.all_to_all(packed, 'win', 0, 0, tiled=True)]
    pallas_call x2, Pallas kernels: 15.8 us -> 18.1 us  [the longest x1 14.8 us: body(): pl.pallas_call(correlate_kernel, in_specs=[SMEM] + [VMEM] * 4 + [pl.Block...]
  transfers between devices with their start and end apart: 8 -> 12, of which waited for: 7 -> 8; matrix products, arithmetic and copies ran while one was open for 4% -> 5% of each run, Pallas kernels for 1% -> 1%
where the time goes in v4:
time: 190 us; the launch traced here: 189 us
  blocking collectives  64.2 us (34%)
  waiting for transfers between devices  43.1 us (23%)
  starting transfers between devices  36.9 us (19%)
  Pallas kernels  35 us (18%)
  other arithmetic  6.06 us (3%)
  local copies, waits for them, and re-layouts  3.2 us (2%)
    all_to_all x2, blocking collectives, body(): parts = lax.all_to_all(part, ('win', 'ch'), 0, 0, tiled=True)  42.7 us
    pallas_call x1, Pallas kernels, body(): pl.pallas_call(correlate_kernel, in_specs=[SMEM] + [VMEM] * 4 + [pl.Block...  14.8 us
    ppermute x3, waiting for transfers between devices, body(): lax.ppermute(own, 'win', turn_x(d))  12.8 us
    all_to_all x1, blocking collectives, body(): back = lax.all_to_all(part, 'win', 0, 0, tiled=True)  12.4 us
    all_to_all x1, waiting for transfers between devices, body(): pieces = lax.all_to_all(spectrum, ('win', 'ch'), 0, 0, tiled=True)  10.8 us
    all_to_all x1, blocking collectives, body(): parts = lax.all_to_all(over_win, 'ch', 0, 0, tiled=True)  9.06 us
    pallas_call x2, Pallas kernels, body(): pl.pallas_call(lambda *refs: kernel(pairs, *refs), in_specs=[VMEM] * 4, o...  8.62 us
    ppermute x1, waiting for transfers between devices, body(): lax.ppermute(own, 'ch', turn_y(1))  8.47 us
  transfers between devices with their start and end apart: 12, of which 8 were waited for; matrix products, arithmetic and copies ran while one was open for 5% of the time, Pallas kernels for 1%

profile of v4, /device:TPU:1, one launch (start us, length us, event | category | flops | bytes accessed | tf_op | source)
XLA Modules:
  0.0 189.3 jit_solution(14665786567716747215)
XLA Ops:
  0.7 3.3 %pick.1 = bf16[8,48,128]{2,1,0:T(8,128)(2,1)} custom-call(s32[8]{0:T(128)} %sources_ref.1, bf16[1536,512]{1,0:T(8,128)(2,1)} %bitcast.30), custom_call_target="tpu_custom_call" | custom-call | tf_op jit(solution)/shard_map/pick/pallas_call | solution.py:350
  4.0 6.5 %all-to-all-start.1 = ((bf16[8,48,128]{2,1,0:T(8,128)(2,1)}), bf16[8,48,128]{2,1,0:T(8,128)(2,1)S(1)}, u32[]{:S(2)}, u32[]{:S(2)}) async-start(bf16[8,48,128]{2,1,0:T(8,128)(2,1)} %pick.1), calls=%async_computation.1 | async-start | bytes 196608 | tf_op jit(solution)/shard_map/all_to_all | solution.py:361
  10.5 3.2 %fusion.6 = (f32[256,512]{1,0:T(8,128)}, f32[256,512]{1,0:T(8,128)}) fusion(s32[512]{0:T(512)S(1)} %iota_add_fusion, s32[256]{0:T(256)S(1)} %fusion.14), kind=kLoop, calls=%fused_computation.18 | loop fusion | flops 1835008 | bytes 1051648 | tf_op jit(solution)/shard_map/sin | solution.py:324
  13.7 1.8 fusion.8
  15.6 0.1 broadcast_in_dim.7
  15.6 0.1 reshape.96
  15.8 0.7 own.1
  16.4 7.7 %all-to-all-start.2 = ((bf16[8,56,128]{2,1,0:T(8,128)(2,1)}), bf16[8,56,128]{2,1,0:T(8,128)(2,1)S(1)}, u32[]{:S(2)}, u32[]{:S(2)}) async-start(bf16[8,56,128]{2,1,0:T(8,128)(2,1)} %own.1), calls=%async_computation.2 | async-start | bytes 229376 | tf_op jit(solution)/shard_map/all_to_all | solution.py:381
  24.1 2.2 %pack.1 = bf16[32,48,512]{2,1,0:T(8,128)(2,1)} custom-call(bf16[1536,512]{1,0:T(8,128)(2,1)S(1)} %bitcast.31), custom_call_target="tpu_custom_call" | custom-call | tf_op jit(solution)/shard_map/main/pack/pallas_call | solution.py:407
  26.3 5.4 %all-to-all-done.2 = bf16[8,56,128]{2,1,0:T(8,128)(2,1)S(1)} async-done(((bf16[8,56,128]{2,1,0:T(8,128)(2,1)}), bf16[8,56,128]{2,1,0:T(8,128)(2,1)S(1)}, u32[]{:S(2)}, u32[]{:S(2)}) %all-to-all-start.2) | async-done | bytes 114720 | tf_op jit(solution)/shard_map/all_to_all | solution.py:381
  31.7 5.1 %all-to-all-start = ((bf16[32,48,512]{2,1,0:T(8,128)(2,1)}), bf16[32,48,512]{2,1,0:T(8,128)(2,1)S(1)}, u32[]{:S(2)}, u32[]{:S(2)}) async-start(bf16[32,48,512]{2,1,0:T(8,128)(2,1)} %pack.1), calls=%async_computation | async-start | bytes 3145728 | tf_op jit(solution)/shard_map/main/all_to_all | solution.py:415
  36.8 2.6 %collective-permute-start.2 = (bf16[8,56,128]{2,1,0:T(8,128)(2,1)S(1)}, bf16[8,56,128]{2,1,0:T(8,128)(2,1)S(1)}, u32[]{:S(2)}, u32[]{:S(2)}) collective-permute-start(bf16[8,56,128]{2,1,0:T(8,128)(2,1)S(1)} %all-to-all-done.2), channel_id=1, source_target_pairs={{0,192},{8,200},{16,208},{24,216},{32,224},{40,232},{48,240},{56,2... | collective-permute-start | bytes 344072 | tf_op jit(solution)/shard_map/ppermute | solution.py:386
  39.4 0.5 collective-permute-start.1
  39.9 0.6 collective-permute-start
  40.5 1.3 collective-permute-done.2
  41.8 5.4 %collective-permute-done.1 = bf16[8,56,128]{2,1,0:T(8,128)(2,1)S(1)} collective-permute-done((bf16[8,56,128]{2,1,0:T(8,128)(2,1)S(1)}, bf16[8,56,128]{2,1,0:T(8,128)(2,1)S(1)}, u32[]{:S(2)}, u32[]{:S(2)}) %collective-permute-start.1) | collective-permute-done | bytes 114720 | tf_op jit(solution)/shard_map/ppermute | solution.py:386
  47.2 6.1 %collective-permute-done = bf16[8,56,128]{2,1,0:T(8,128)(2,1)S(1)} collective-permute-done((bf16[8,56,128]{2,1,0:T(8,128)(2,1)S(1)}, bf16[8,56,128]{2,1,0:T(8,128)(2,1)S(1)}, u32[]{:S(2)}, u32[]{:S(2)}) %collective-permute-start) | collective-permute-done | bytes 114720 | tf_op jit(solution)/shard_map/ppermute | solution.py:386
  53.4 0.1 pad_maximum_fusion
  53.4 0.1 fusion.20
  53.5 1.6 collective-permute-start.3
  55.1 1.3 collective-permute-start.5
  56.4 8.5 %collective-permute-done.3 = bf16[32,48,128]{2,1,0:T(8,128)(2,1)S(1)} collective-permute-done((bf16[32,48,128]{2,1,0:T(8,128)(2,1)S(1)}, bf16[32,48,128]{2,1,0:T(8,128)(2,1)S(1)}, u32[]{:S(2)}, u32[]{:S(2)}) %collective-permute-start.3) | collective-permute-done | bytes 393248 | tf_op jit(solution)/shard_map/along_y/ppermute | solution.py:394
  64.9 0.4 collective-permute-start.4
  65.3 2.4 %collective-permute-start.6 = (bf16[16,48,128]{2,1,0:T(8,128)(2,1)S(1)}, bf16[16,48,128]{2,1,0:T(8,128)(2,1)S(1)}, u32[]{:S(2)}, u32[]{:S(2)}) collective-permute-start(bf16[16,48,128]{2,1,0:T(8,128)(2,1)S(1)} %slice.26), channel_id=1, source_target_pairs={{0,6},{1,7},{2,0},{3,1},{4,2},{5,3},{6,4},{7,5},{8,14},{9,15},{10,... | collective-permute-start | bytes 589832 | tf_op jit(solution)/shard_map/along_y/ppermute | solution.py:397
  67.8 3.3 %collective-permute-done.4 = bf16[16,48,128]{2,1,0:T(8,128)(2,1)S(1)} collective-permute-done((bf16[16,48,128]{2,1,0:T(8,128)(2,1)S(1)}, bf16[16,48,128]{2,1,0:T(8,128)(2,1)S(1)}, u32[]{:S(2)}, u32[]{:S(2)}) %collective-permute-start.4) | collective-permute-done | bytes 196640 | tf_op jit(solution)/shard_map/along_y/ppermute | solution.py:396
  71.3 0.1 constant_dynamic-update-slice_fusion
  71.3 2.6 %collective-permute-start.7 = (bf16[4,32,48,128]{3,2,1,0:T(8,128)(2,1)S(1)}, bf16[4,32,48,128]{3,2,1,0:T(8,128)(2,1)}, u32[]{:S(2)}, u32[]{:S(2)}) collective-permute-start(bf16[4,32,48,128]{3,2,1,0:T(8,128)(2,1)S(1)} %bitcast.33), channel_id=1, source_target_pairs={{0,1},{1,0},{2,3},{3,2},{4,5},{5,4},{6,7},{7,6},{8,9},{9,8},{10,11... | collective-permute-start | bytes 4718600 | tf_op jit(solution)/shard_map/cores/ppermute | solution.py:401
  74.0 0.1 pad_add_fusion.ids_ref
  74.0 0.8 slice.27.masks_ref
  74.9 2.2 %collective-permute-done.7.y_ref = bf16[4,32,48,128]{3,2,1,0:T(8,128)(2,1)} collective-permute-done((bf16[4,32,48,128]{3,2,1,0:T(8,128)(2,1)S(1)}, bf16[4,32,48,128]{3,2,1,0:T(8,128)(2,1)}, u32[]{:S(2)}, u32[]{:S(2)}) %collective-permute-start.7) | collective-permute-done | bytes 1572896 | tf_op jit(solution)/shard_map/cores/ppermute | solution.py:401
  77.1 14.8 %correlate.1 = (bf16[8,256,1536]{2,1,0:T(8,128)(2,1)S(1)}, f32[8,12,128]{2,1,0:T(8,128)S(1)}, f32[256,128]{1,0:T(8,128)S(1)}, f32[12,128]{1,0:T(8,128)S(1)}) custom-call(s32[9]{0:T(128)S(1)} %pad_add_fusion.ids_ref, bf16[1536,512]{1,0:T(8,128)(2,1)S(1)} %bitcast.32, bf16[4,32,48,128]{3,2,1,0:T(8,128)(2,1)S(1)} %bitcast.34, ...), custom_call_target="tpu_custom_call" | custom-call | tf_op jit(solution)/shard_map/correlate/pallas_call | solution.py:426
  91.9 24.6 %all_to_all.64 = f32[256,1,128]{2,1,0:T(1,128)S(1)} all-to-all(f32[256,1,128]{2,1,0:T(1,128)S(1)} %bitcast.38), channel_id=1, replica_groups=mesh['win'=32,'ch'=8] {'win','ch'}, dimensions={0} | all-to-all | bytes 262144 | tf_op jit(solution)/shard_map/all_to_all | solution.py:438
  116.5 4.3 %iterate.2 = (f32[8,12,128]{2,1,0:T(8,128)S(1)}, f32[256,128]{1,0:T(8,128)S(1)}) custom-call(f32[256,128]{1,0:T(8,128)S(1)} %bitcast.35, f32[12,128]{1,0:T(8,128)S(1)} %get-tuple-element.22.refs_1_, f32[8,12,128]{2,1,0:T(8,128)S(1)} %get-tuple-element.23.refs_2_, bf16[8,256,1536]{2,1,0:T(8,128)(2,1)S(1)} %get-tuple-element.24.refs_3_), custom_call_target="tpu_custom_call" | custom-call | tf_op jit(solution)/shard_map/iterate/pallas_call | solution.py:443
  120.8 18.2 %all_to_all.65 = f32[256,1,128]{2,1,0:T(1,128)S(1)} all-to-all(f32[256,1,128]{2,1,0:T(1,128)S(1)} %bitcast.39), channel_id=1, replica_groups=mesh['win'=32,'ch'=8] {'win','ch'}, dimensions={0} | all-to-all | bytes 262144 | tf_op jit(solution)/shard_map/all_to_all | solution.py:453
  139.0 4.3 %iterate.3 = (f32[8,12,128]{2,1,0:T(8,128)S(1)}, f32[32,8,128]{2,1,0:T(8,128)S(1)}) custom-call(f32[256,128]{1,0:T(8,128)S(1)} %bitcast.36, f32[12,128]{1,0:T(8,128)S(1)} %get-tuple-element.22.refs_1_, f32[8,12,128]{2,1,0:T(8,128)S(1)} %get-tuple-element.26.refs_2_, bf16[8,256,1536]{2,1,0:T(8,128)(2,1)S(1)} %get-tuple-element.24.refs_3_), custom_call_target="tpu_custom_call" | custom-call | tf_op jit(solution)/shard_map/iterate/pallas_call | solution.py:443
  143.3 12.4 %all_to_all.66.refs_0_ = f32[32,8,128]{2,1,0:T(8,128)S(1)} all-to-all(f32[32,8,128]{2,1,0:T(8,128)S(1)} %get-tuple-element.27), channel_id=1, replica_groups=mesh['win'=32,'ch'=8] {'win'}, dimensions={0} | all-to-all | bytes 262144 | tf_op jit(solution)/shard_map/all_to_all | solution.py:455
  155.6 0.2 carry.1
  155.8 9.1 %all_to_all.67 = f32[8,1,128]{2,1,0:T(1,128)S(1)} all-to-all(f32[8,1,128]{2,1,0:T(1,128)S(1)} %bitcast.41), channel_id=1, replica_groups=mesh['win'=32,'ch'=8] {'ch'}, dimensions={0} | all-to-all | bytes 8192 | tf_op jit(solution)/shard_map/all_to_all | solution.py:464
  164.9 3.6 %spectrum.1 = (f32[256,128]{1,0:T(8,128)}, f32[8,128]{1,0:T(8,128)S(1)}) custom-call(f32[8,128]{1,0:T(8,128)S(1)} %bitcast.40, f32[12,128]{1,0:T(8,128)S(1)} %get-tuple-element.22.refs_1_, f32[8,12,128]{2,1,0:T(8,128)S(1)} %get-tuple-element.28.refs_2_, bf16[8,256,1536]{2,1,0:T(8,128)(2,1)S(1)} %get-tuple-element.24.refs_3_, f32[512,256]{1,0:T(8,128)S(1)} %copy-done.4), custom_call_target="tpu_custom_call" | custom-call | tf_op jit(solution)/shard_map/spectrum/pallas_call | solution.py:466
  168.4 0.5 slice.23
  169.0 5.6 %all-to-all-start.7 = ((f32[256,1,128]{2,1,0:T(1,128)}), f32[256,1,128]{2,1,0:T(1,128)S(1)}, u32[]{:S(2)}, u32[]{:S(2)}) async-start(f32[256,1,128]{2,1,0:T(1,128)} %bitcast.23), calls=%async_computation.7 | async-start | bytes 262144 | tf_op jit(solution)/shard_map/all_to_all | solution.py:478
  174.6 0.7 divide_add_fusion
  175.3 0.1 copy.14
  175.5 0.3 copy.15
  175.8 0.1 broadcast_divide_fusion
  175.9 0.9 copy.17
  176.8 10.8 %all-to-all-done.7 = f32[256,1,128]{2,1,0:T(1,128)S(1)} async-done(((f32[256,1,128]{2,1,0:T(1,128)}), f32[256,1,128]{2,1,0:T(1,128)S(1)}, u32[]{:S(2)}, u32[]{:S(2)}) %all-to-all-start.7) | async-done | bytes 131104 | tf_op jit(solution)/shard_map/all_to_all | solution.py:478
  187.6 1.7 beam.1
  (31 shorter events, 0.2 us)
Async XLA Ops:
  0.6 14.9 %copy-start.6 = (s32[12]{0:T(128)S(1)}, s32[12]{0:T(128)}, u32[]{:S(2)}) copy-start(s32[12]{0:T(128)} %param.7) | copy-start | bytes 148
  0.6 23.5 %copy-start = (bf16[12,128,512]{2,1,0:T(8,128)(2,1)S(1)}, bf16[12,128,512]{2,1,0:T(8,128)(2,1)}, u32[]{:S(2)}) copy-start(bf16[12,128,512]{2,1,0:T(8,128)(2,1)} %param.5) | copy-start | bytes 4718596
  4.0 11.8 %all-to-all-start.1 = ((bf16[8,48,128]{2,1,0:T(8,128)(2,1)}), bf16[8,48,128]{2,1,0:T(8,128)(2,1)S(1)}, u32[]{:S(2)}, u32[]{:S(2)}) async-start(bf16[8,48,128]{2,1,0:T(8,128)(2,1)} %pick.1), calls=%async_computation.1 | async-start | bytes 196608 | tf_op jit(solution)/shard_map/all_to_all | solution.py:361
  16.4 15.3 %all-to-all-start.2 = ((bf16[8,56,128]{2,1,0:T(8,128)(2,1)}), bf16[8,56,128]{2,1,0:T(8,128)(2,1)S(1)}, u32[]{:S(2)}, u32[]{:S(2)}) async-start(bf16[8,56,128]{2,1,0:T(8,128)(2,1)} %own.1), calls=%async_computation.2 | async-start | bytes 229376 | tf_op jit(solution)/shard_map/all_to_all | solution.py:381
  31.7 45.4 %all-to-all-start = ((bf16[32,48,512]{2,1,0:T(8,128)(2,1)}), bf16[32,48,512]{2,1,0:T(8,128)(2,1)S(1)}, u32[]{:S(2)}, u32[]{:S(2)}) async-start(bf16[32,48,512]{2,1,0:T(8,128)(2,1)} %pack.1), calls=%async_computation | async-start | bytes 3145728 | tf_op jit(solution)/shard_map/main/all_to_all | solution.py:415
  36.8 4.9 %collective-permute-start.2 = (bf16[8,56,128]{2,1,0:T(8,128)(2,1)S(1)}, bf16[8,56,128]{2,1,0:T(8,128)(2,1)S(1)}, u32[]{:S(2)}, u32[]{:S(2)}) collective-permute-start(bf16[8,56,128]{2,1,0:T(8,128)(2,1)S(1)} %all-to-all-done.2), channel_id=1, source_target_pairs={{0,192},{8,200},{16,208},{24,216},{32,224},{40,232},{48,240},{56,2... | collective-permute-start | bytes 344072 | tf_op jit(solution)/shard_map/ppermute | solution.py:386
  39.4 7.8 %collective-permute-start.1 = (bf16[8,56,128]{2,1,0:T(8,128)(2,1)S(1)}, bf16[8,56,128]{2,1,0:T(8,128)(2,1)S(1)}, u32[]{:S(2)}, u32[]{:S(2)}) collective-permute-start(bf16[8,56,128]{2,1,0:T(8,128)(2,1)S(1)} %all-to-all-done.2), channel_id=1, source_target_pairs={{0,128},{8,136},{16,144},{24,152},{32,160},{40,168},{48,176},{56,1... | collective-permute-start | bytes 344072 | tf_op jit(solution)/shard_map/ppermute | solution.py:386
  39.9 13.4 %collective-permute-start = (bf16[8,56,128]{2,1,0:T(8,128)(2,1)S(1)}, bf16[8,56,128]{2,1,0:T(8,128)(2,1)S(1)}, u32[]{:S(2)}, u32[]{:S(2)}) collective-permute-start(bf16[8,56,128]{2,1,0:T(8,128)(2,1)S(1)} %all-to-all-done.2), channel_id=1, source_target_pairs={{0,64},{8,72},{16,80},{24,88},{32,96},{40,104},{48,112},{56,120},{... | collective-permute-start | bytes 344072 | tf_op jit(solution)/shard_map/ppermute | solution.py:386
  53.4 17.8 %copy-start.5 = (bf16[4,8,56,128]{3,2,1,0:T(8,128)(2,1)}, bf16[4,8,56,128]{3,2,1,0:T(8,128)(2,1)S(1)}, u32[]{:S(2)}) copy-start(bf16[4,8,56,128]{3,2,1,0:T(8,128)(2,1)S(1)} %pad_maximum_fusion) | copy-start | bytes 1376260
  53.5 11.4 %collective-permute-start.3 = (bf16[32,48,128]{2,1,0:T(8,128)(2,1)S(1)}, bf16[32,48,128]{2,1,0:T(8,128)(2,1)S(1)}, u32[]{:S(2)}, u32[]{:S(2)}) collective-permute-start(bf16[32,48,128]{2,1,0:T(8,128)(2,1)S(1)} %get-tuple-element.42), channel_id=1, source_target_pairs={{0,2},{1,3},{2,4},{3,5},{4,6},{5,7},{6,0},{7,1},{8,10},{9,11},{10,... | collective-permute-start | bytes 1179656 | tf_op jit(solution)/shard_map/along_y/ppermute | solution.py:394
  55.1 10.2 %collective-permute-start.5 = (bf16[32,48,128]{2,1,0:T(8,128)(2,1)S(1)}, bf16[32,48,128]{2,1,0:T(8,128)(2,1)S(1)}, u32[]{:S(2)}, u32[]{:S(2)}) collective-permute-start(bf16[32,48,128]{2,1,0:T(8,128)(2,1)S(1)} %get-tuple-element.42), channel_id=1, source_target_pairs={{0,6},{1,7},{2,0},{3,1},{4,2},{5,3},{6,4},{7,5},{8,14},{9,15},{10,... | collective-permute-start | bytes 1179656 | tf_op jit(solution)/shard_map/along_y/ppermute | solution.py:394
  64.9 6.2 %collective-permute-start.4 = (bf16[16,48,128]{2,1,0:T(8,128)(2,1)S(1)}, bf16[16,48,128]{2,1,0:T(8,128)(2,1)S(1)}, u32[]{:S(2)}, u32[]{:S(2)}) collective-permute-start(bf16[16,48,128]{2,1,0:T(8,128)(2,1)S(1)} %slice.25), channel_id=1, source_target_pairs={{0,2},{1,3},{2,4},{3,5},{4,6},{5,7},{6,0},{7,1},{8,10},{9,11},{10,... | collective-permute-start | bytes 589832 | tf_op jit(solution)/shard_map/along_y/ppermute | solution.py:396
  65.3 5.9 %collective-permute-start.6 = (bf16[16,48,128]{2,1,0:T(8,128)(2,1)S(1)}, bf16[16,48,128]{2,1,0:T(8,128)(2,1)S(1)}, u32[]{:S(2)}, u32[]{:S(2)}) collective-permute-start(bf16[16,48,128]{2,1,0:T(8,128)(2,1)S(1)} %slice.26), channel_id=1, source_target_pairs={{0,6},{1,7},{2,0},{3,1},{4,2},{5,3},{6,4},{7,5},{8,14},{9,15},{10,... | collective-permute-start | bytes 589832 | tf_op jit(solution)/shard_map/along_y/ppermute | solution.py:397
  71.3 5.8 %collective-permute-start.7 = (bf16[4,32,48,128]{3,2,1,0:T(8,128)(2,1)S(1)}, bf16[4,32,48,128]{3,2,1,0:T(8,128)(2,1)}, u32[]{:S(2)}, u32[]{:S(2)}) collective-permute-start(bf16[4,32,48,128]{3,2,1,0:T(8,128)(2,1)S(1)} %bitcast.33), channel_id=1, source_target_pairs={{0,1},{1,0},{2,3},{3,2},{4,5},{5,4},{6,7},{7,6},{8,9},{9,8},{10,11... | collective-permute-start | bytes 4718600 | tf_op jit(solution)/shard_map/cores/ppermute | solution.py:401
  139.0 25.9 %copy-start.4 = (f32[512,256]{1,0:T(8,128)S(1)}, f32[512,256]{1,0:T(8,128)}, u32[]{:S(2)}) copy-start(f32[512,256]{1,0:T(8,128)} %constant.146.clone.refs_4_) | copy-start | bytes 1572868
  169.0 18.6 %all-to-all-start.7 = ((f32[256,1,128]{2,1,0:T(1,128)}), f32[256,1,128]{2,1,0:T(1,128)S(1)}, u32[]{:S(2)}, u32[]{:S(2)}) async-start(f32[256,1,128]{2,1,0:T(1,128)} %bitcast.23), calls=%async_computation.7 | async-start | bytes 262144 | tf_op jit(solution)/shard_map/all_to_all | solution.py:478
  175.4 12.2 %copy-start.1 = (f32[256,512]{1,0:T(8,128)S(1)}, f32[256,512]{1,0:T(8,128)}, u32[]{:S(2)}) copy-start(f32[256,512]{1,0:T(8,128)} %get-tuple-element.35.refs_2_) | copy-start | bytes 1572868
  175.4 12.2 %copy-start.2 = (f32[256,512]{1,0:T(8,128)S(1)}, f32[256,512]{1,0:T(8,128)}, u32[]{:S(2)}) copy-start(f32[256,512]{1,0:T(8,128)} %get-tuple-element.34.refs_1_) | copy-start | bytes 1572868
  175.4 12.1 %copy-start.3 = (f32[128,512]{1,0:T(8,128)S(1)}, f32[128,512]{1,0:T(8,128)}, u32[]{:S(2)}) copy-start(f32[128,512]{1,0:T(8,128)} %get-tuple-element.36.refs_3_) | copy-start | bytes 786436

commit v5 on v4

--- a/solution.py
+++ b/solution.py
@@ -30,10 +30,17 @@
     cosines = np.cos(angles.astype(np.float64)).astype(np.float32)
     sines = np.sin(angles.astype(np.float64)).astype(np.float32)
     inverse_factor = np.float32(1.0 / math.sqrt(freq_count))
-    forward_factor = np.float32(1.0 / math.sqrt(lag_count))
     inverse = np.concatenate([cosines * inverse_factor, -sines * inverse_factor], axis=0)
-    forward = np.concatenate([cosines * forward_factor, -sines * forward_factor], axis=0)
-    return np.ascontiguousarray(inverse.T), forward
+    return np.ascontiguousarray(inverse.T)
+
+
+def forward_table(freq_count, lag_count):
+    freq_ids = jnp.arange(freq_count, dtype=jnp.int32)
+    delay_indices = jnp.arange(lag_count, dtype=jnp.int32) - lag_count // 2
+    phase_ids = jnp.mod(freq_ids[:, None] * delay_indices[None, :], 2 * freq_count)
+    angles = 2.0 * math.pi / (2 * freq_count) * phase_ids.astype(jnp.float32)
+    factor = 1.0 / math.sqrt(lag_count)
+    return jnp.cos(angles) * factor, -jnp.sin(angles) * factor
 
 
 def pick_kernel(sources_ref, x_ref, o_ref):
@@ -278,7 +285,7 @@
 
 
 def spectrum_kernel(
-    pairs, all_ref, mask_ref, r_in_ref, c_ref, table_ref, o_ref, spread_ref, w_ref, terms_ref, stack_ref
+    pairs, all_ref, mask_ref, r_in_ref, c_ref, cos_ref, sin_ref, o_ref, spread_ref, w_ref, terms_ref, stack_ref
 ):
     spread = set_weights(pairs, jnp.sum(all_ref[...]) * (1.0 / LANES), mask_ref, r_in_ref, w_ref)
 
@@ -288,10 +295,10 @@
     stacks = stack_ref[0]
     for s in range(1, c_ref.shape[0]):
         stacks = jnp.where(lane // 16 == s, stack_ref[s], stacks)
-    both = jnp.dot(table_ref[...], stacks, precision=HIGHEST, preferred_element_type=jnp.float32)
-    freq_count = table_ref.shape[0] // 2
-    part = lax.broadcasted_iota(jnp.int32, (freq_count, LANES), 1) % 4
-    o_ref[...] = jnp.where(part == 0, both[:freq_count], jnp.where(part == 1, both[freq_count:], 0.0))
+    real = jnp.dot(cos_ref[...], stacks, precision=HIGHEST, preferred_element_type=jnp.float32)
+    imag = jnp.dot(sin_ref[...], stacks, precision=HIGHEST, preferred_element_type=jnp.float32)
+    part = lax.broadcasted_iota(jnp.int32, real.shape, 1) % 4
+    o_ref[...] = jnp.where(part == 0, real, jnp.where(part == 1, imag, 0.0))
 
 
 def beam_kernel(gain, x_ref, cos_ref, sin_ref, fine_cos_ref, fine_sin_ref, o_ref):
@@ -339,7 +346,7 @@
     pairs = float(source_total * chans)
     win, ch = lax.axis_index("win"), lax.axis_index("ch")
     y, core = ch // 2, ch % 2
-    inverse_np, forward_np = tables(freq_count, L)
+    inverse_np = tables(freq_count, L)
     flat = spectra.reshape(win_dev * chan_dev, width)
     rows_dev = win_dev * Q
     rows = n_win * rows_dev
@@ -365,7 +372,9 @@
     coarse = (device % n_ch) * chan_dev + (device // n_ch) * Q
     cosines, sines = cos_sin(freq_id, coarse, P_SIZE, modulus)
     fine_cos, fine_sin = cos_sin(freq_id, (jnp.arange(LANES, dtype=jnp.int32) // 4) % Q, P_SIZE, modulus)
-    got, cosines, sines, fine_cos, fine_sin = lax.optimization_barrier((got, cosines, sines, fine_cos, fine_sin))
+    got, flat, cosines, sines, fine_cos, fine_sin = lax.optimization_barrier(
+        (got, flat, cosines, sines, fine_cos, fine_sin)
+    )
     own_mask = valid.astype(jnp.float32)
     mask_lanes = jnp.broadcast_to(own_mask.reshape(win_dev // 4, 1, 4), (win_dev // 4, Q, 4)).reshape(1, rows_dev)
     own = pl.pallas_call(
@@ -379,6 +388,7 @@
 
     along_z = [[x * z_size + z for z in range(z_size)] for x in range(x_size)]
     own = lax.all_to_all(own, "win", 0, 0, tiled=True, axis_index_groups=along_z)
+    forward_cos, forward_sin = forward_table(freq_count, L)
 
     def turn_x(d):
         return [(x * z_size + z, (x + d) % x_size * z_size + z) for x in range(x_size) for z in range(z_size)]
@@ -412,6 +422,7 @@
             compiler_params=PARAMS,
             name="pack",
         )(flat)
+        packed, forward_cos, forward_sin = lax.optimization_barrier((packed, forward_cos, forward_sin))
         moved = lax.all_to_all(packed, "win", 0, 0, tiled=True)
 
     inverse = pltpu.with_memory_space_constraint(jnp.asarray(inverse_np, jnp.bfloat16), pltpu.HBM)
@@ -465,16 +476,16 @@
 
     spectrum, spread_sq = pl.pallas_call(
         lambda *refs: spectrum_kernel(pairs, *refs),
-        in_specs=[VMEM] * 5,
+        in_specs=[VMEM] * 6,
         out_specs=[VMEM] * 2,
         out_shape=[
             jax.ShapeDtypeStruct((freq_count, LANES), jnp.float32),
-            jax.ShapeDtypeStruct((8, LANES), jnp.float32),
+            jax.ShapeDtypeStruct((n_win, source_total, rows_dev), jnp.float32),
         ],
         scratch_shapes=[row_weights, terms, stack],
         compiler_params=PARAMS,
         name="spectrum",
-    )(parts, mask, r, corr, jnp.asarray(forward_np))
+    )(parts, mask, r, corr, forward_cos, forward_sin)
     pieces = lax.all_to_all(spectrum, ("win", "ch"), 0, 0, tiled=True)
 
     beamed = pl.pallas_call(
@@ -487,10 +498,9 @@
     )(pieces, cosines, sines, fine_cos, fine_sin)
 
     own_mask, back, spread_sq = lax.optimization_barrier((own_mask, back, spread_sq))
-    spread_sq = spread_sq[0, 0]
-    residual = back[:, :, :rows_dev].reshape(n_win, source_total, win_dev // 4, Q, 4)
+    residual = (back[:, :, :rows_dev] / spread_sq).reshape(n_win, source_total, win_dev // 4, Q, 4)
     residual = residual.transpose(2, 4, 1, 0, 3).reshape(win_dev, source_total, chan_dev)
-    weights = own_mask[:, None, None] * (degrees + 1.0) / (degrees + residual / spread_sq)
+    weights = own_mask[:, None, None] * (degrees + 1.0) / (degrees + residual)
     return (weights, beamed)
 
 

time: 190 us -> 189 us (level)
  no operation moved by 1% of the time
where the time goes in v5:
time: 189 us
  blocking collectives  63.3 us (33%)
  waiting for transfers between devices  42 us (22%)
  starting transfers between devices  37.6 us (20%)
  Pallas kernels  35 us (19%)
  other arithmetic  7.31 us (4%)
  local copies, waits for them, and re-layouts  2.68 us (1%)
    all_to_all x2, blocking collectives, body(): parts = lax.all_to_all(part, ('win', 'ch'), 0, 0, tiled=True)  41.8 us
    pallas_call x1, Pallas kernels, body(): pl.pallas_call(correlate_kernel, in_specs=[SMEM] + [VMEM] * 4 + [pl.Block...  14.8 us
    ppermute x3, waiting for transfers between devices, body(): lax.ppermute(own, 'win', turn_x(d))  12.6 us
    all_to_all x1, blocking collectives, body(): back = lax.all_to_all(part, 'win', 0, 0, tiled=True)  12.4 us
    all_to_all x1, waiting for transfers between devices, body(): pieces = lax.all_to_all(spectrum, ('win', 'ch'), 0, 0, tiled=True)  11.4 us
    all_to_all x1, blocking collectives, body(): parts = lax.all_to_all(over_win, 'ch', 0, 0, tiled=True)  9.06 us
    ppermute x1, waiting for transfers between devices, body(): lax.ppermute(own, 'ch', turn_y(1))  8.68 us
    pallas_call x2, Pallas kernels, body(): pl.pallas_call(lambda *refs: kernel(pairs, *refs), in_specs=[VMEM] * 4, o...  8.61 us
  transfers between devices with their start and end apart: 12, of which 8 were waited for; matrix products, arithmetic and copies ran while one was open for 5% of the time, Pallas kernels for 1%

profile of v5, /device:TPU:1, one launch (start us, length us, event | category | flops | bytes accessed | tf_op | source)
XLA Modules:
  0.0 188.8 jit_solution(12048449843325884916)
XLA Ops:
  0.6 3.3 %pick.1 = bf16[8,48,128]{2,1,0:T(8,128)(2,1)} custom-call(s32[8]{0:T(128)} %sources_ref.1, bf16[1536,512]{1,0:T(8,128)(2,1)} %bitcast.29), custom_call_target="tpu_custom_call" | custom-call | tf_op jit(solution)/shard_map/pick/pallas_call | solution.py:357
  4.0 6.6 %all-to-all-start = ((bf16[8,48,128]{2,1,0:T(8,128)(2,1)}), bf16[8,48,128]{2,1,0:T(8,128)(2,1)S(1)}, u32[]{:S(2)}, u32[]{:S(2)}) async-start(bf16[8,48,128]{2,1,0:T(8,128)(2,1)} %pick.1), calls=%async_computation | async-start | bytes 196608 | tf_op jit(solution)/shard_map/all_to_all | solution.py:368
  10.6 0.1 broadcast_in_dim.7
  10.7 0.1 reshape.96
  10.8 1.9 %fusion.14 = (f32[128,512]{1,0:T(8,128)}, f32[128,512]{1,0:T(8,128)}) fusion(s32[512]{0:T(512)S(1)} %iota_add_fusion, s32[128]{0:T(128)S(1)} %fusion.23), kind=kLoop, calls=%fused_computation.32 | loop fusion | flops 917504 | bytes 526848 | tf_op jit(solution)/shard_map/sin | solution.py:331
  12.7 3.2 %fusion.11 = (f32[256,512]{1,0:T(8,128)}, f32[256,512]{1,0:T(8,128)}) fusion(s32[512]{0:T(512)S(1)} %iota_add_fusion, s32[256]{0:T(256)S(1)} %fusion.20), kind=kLoop, calls=%fused_computation.28 | loop fusion | flops 1835008 | bytes 1051648 | tf_op jit(solution)/shard_map/sin | solution.py:331
  16.0 0.7 own.1
  16.7 7.7 %all-to-all-start.2 = ((bf16[8,56,128]{2,1,0:T(8,128)(2,1)}), bf16[8,56,128]{2,1,0:T(8,128)(2,1)S(1)}, u32[]{:S(2)}, u32[]{:S(2)}) async-start(bf16[8,56,128]{2,1,0:T(8,128)(2,1)} %own.1), calls=%async_computation.2 | async-start | bytes 229376 | tf_op jit(solution)/shard_map/all_to_all | solution.py:390
  24.3 1.8 negate_multiply_fusion
  26.1 2.2 %pack.1 = bf16[32,48,512]{2,1,0:T(8,128)(2,1)} custom-call(bf16[1536,512]{1,0:T(8,128)(2,1)S(1)} %bitcast.30), custom_call_target="tpu_custom_call" | custom-call | tf_op jit(solution)/shard_map/main/pack/pallas_call | solution.py:417
  28.3 3.6 %all-to-all-done.2 = bf16[8,56,128]{2,1,0:T(8,128)(2,1)S(1)} async-done(((bf16[8,56,128]{2,1,0:T(8,128)(2,1)}), bf16[8,56,128]{2,1,0:T(8,128)(2,1)S(1)}, u32[]{:S(2)}, u32[]{:S(2)}) %all-to-all-start.2) | async-done | bytes 114720 | tf_op jit(solution)/shard_map/all_to_all | solution.py:390
  31.9 5.9 %all-to-all-start.1 = ((bf16[32,48,512]{2,1,0:T(8,128)(2,1)}), bf16[32,48,512]{2,1,0:T(8,128)(2,1)S(1)}, u32[]{:S(2)}, u32[]{:S(2)}) async-start(bf16[32,48,512]{2,1,0:T(8,128)(2,1)} %pack.1), calls=%async_computation.1 | async-start | bytes 3145728 | tf_op jit(solution)/shard_map/main/all_to_all | solution.py:426
  37.8 2.6 %collective-permute-start.2 = (bf16[8,56,128]{2,1,0:T(8,128)(2,1)S(1)}, bf16[8,56,128]{2,1,0:T(8,128)(2,1)S(1)}, u32[]{:S(2)}, u32[]{:S(2)}) collective-permute-start(bf16[8,56,128]{2,1,0:T(8,128)(2,1)S(1)} %all-to-all-done.2), channel_id=1, source_target_pairs={{0,192},{8,200},{16,208},{24,216},{32,224},{40,232},{48,240},{56,2... | collective-permute-start | bytes 344072 | tf_op jit(solution)/shard_map/ppermute | solution.py:396
  40.4 0.5 collective-permute-start.1
  40.9 0.6 collective-permute-start
  41.5 1.6 collective-permute-done.2
  43.1 4.1 %collective-permute-done.1 = bf16[8,56,128]{2,1,0:T(8,128)(2,1)S(1)} collective-permute-done((bf16[8,56,128]{2,1,0:T(8,128)(2,1)S(1)}, bf16[8,56,128]{2,1,0:T(8,128)(2,1)S(1)}, u32[]{:S(2)}, u32[]{:S(2)}) %collective-permute-start.1) | collective-permute-done | bytes 114720 | tf_op jit(solution)/shard_map/ppermute | solution.py:396
  47.2 6.9 %collective-permute-done = bf16[8,56,128]{2,1,0:T(8,128)(2,1)S(1)} collective-permute-done((bf16[8,56,128]{2,1,0:T(8,128)(2,1)S(1)}, bf16[8,56,128]{2,1,0:T(8,128)(2,1)S(1)}, u32[]{:S(2)}, u32[]{:S(2)}) %collective-permute-start) | collective-permute-done | bytes 114720 | tf_op jit(solution)/shard_map/ppermute | solution.py:396
  54.1 0.1 pad_maximum_fusion
  54.2 0.1 fusion.26
  54.3 1.4 collective-permute-start.3
  55.7 1.3 collective-permute-start.5
  57.0 8.7 %collective-permute-done.3 = bf16[32,48,128]{2,1,0:T(8,128)(2,1)S(1)} collective-permute-done((bf16[32,48,128]{2,1,0:T(8,128)(2,1)S(1)}, bf16[32,48,128]{2,1,0:T(8,128)(2,1)S(1)}, u32[]{:S(2)}, u32[]{:S(2)}) %collective-permute-start.3) | collective-permute-done | bytes 393248 | tf_op jit(solution)/shard_map/along_y/ppermute | solution.py:404
  65.7 0.2 collective-permute-start.4
  66.0 2.6 %collective-permute-start.6 = (bf16[16,48,128]{2,1,0:T(8,128)(2,1)S(1)}, bf16[16,48,128]{2,1,0:T(8,128)(2,1)S(1)}, u32[]{:S(2)}, u32[]{:S(2)}) collective-permute-start(bf16[16,48,128]{2,1,0:T(8,128)(2,1)S(1)} %slice.22), channel_id=1, source_target_pairs={{0,6},{1,7},{2,0},{3,1},{4,2},{5,3},{6,4},{7,5},{8,14},{9,15},{10,... | collective-permute-start | bytes 589832 | tf_op jit(solution)/shard_map/along_y/ppermute | solution.py:407
  68.6 0.1 constant_dynamic-update-slice_fusion.3
  68.7 3.5 %collective-permute-done.4 = bf16[16,48,128]{2,1,0:T(8,128)(2,1)S(1)} collective-permute-done((bf16[16,48,128]{2,1,0:T(8,128)(2,1)S(1)}, bf16[16,48,128]{2,1,0:T(8,128)(2,1)S(1)}, u32[]{:S(2)}, u32[]{:S(2)}) %collective-permute-start.4) | collective-permute-done | bytes 196640 | tf_op jit(solution)/shard_map/along_y/ppermute | solution.py:406
  72.2 0.1 constant_dynamic-update-slice_fusion
  72.3 2.5 %collective-permute-start.7 = (bf16[4,32,48,128]{3,2,1,0:T(8,128)(2,1)S(1)}, bf16[4,32,48,128]{3,2,1,0:T(8,128)(2,1)}, u32[]{:S(2)}, u32[]{:S(2)}) collective-permute-start(bf16[4,32,48,128]{3,2,1,0:T(8,128)(2,1)S(1)} %bitcast.32), channel_id=1, source_target_pairs={{0,1},{1,0},{2,3},{3,2},{4,5},{5,4},{6,7},{7,6},{8,9},{9,8},{10,11... | collective-permute-start | bytes 4718600 | tf_op jit(solution)/shard_map/cores/ppermute | solution.py:411
  74.8 0.1 pad_add_fusion.ids_ref
  74.9 0.8 slice.23.masks_ref
  75.7 2.2 %collective-permute-done.7.y_ref = bf16[4,32,48,128]{3,2,1,0:T(8,128)(2,1)} collective-permute-done((bf16[4,32,48,128]{3,2,1,0:T(8,128)(2,1)S(1)}, bf16[4,32,48,128]{3,2,1,0:T(8,128)(2,1)}, u32[]{:S(2)}, u32[]{:S(2)}) %collective-permute-start.7) | collective-permute-done | bytes 1572896 | tf_op jit(solution)/shard_map/cores/ppermute | solution.py:411
  77.9 14.8 %correlate.1 = (bf16[8,256,1536]{2,1,0:T(8,128)(2,1)S(1)}, f32[8,12,128]{2,1,0:T(8,128)S(1)}, f32[256,128]{1,0:T(8,128)S(1)}, f32[12,128]{1,0:T(8,128)S(1)}) custom-call(s32[9]{0:T(128)S(1)} %pad_add_fusion.ids_ref, bf16[1536,512]{1,0:T(8,128)(2,1)S(1)} %bitcast.31, bf16[4,32,48,128]{3,2,1,0:T(8,128)(2,1)S(1)} %bitcast.33, ...), custom_call_target="tpu_custom_call" | custom-call | tf_op jit(solution)/shard_map/correlate/pallas_call | solution.py:437
  92.7 23.7 %all_to_all.64 = f32[256,1,128]{2,1,0:T(1,128)S(1)} all-to-all(f32[256,1,128]{2,1,0:T(1,128)S(1)} %bitcast.37), channel_id=1, replica_groups=mesh['win'=32,'ch'=8] {'win','ch'}, dimensions={0} | all-to-all | bytes 262144 | tf_op jit(solution)/shard_map/all_to_all | solution.py:449
  116.4 4.3 %iterate.2 = (f32[8,12,128]{2,1,0:T(8,128)S(1)}, f32[256,128]{1,0:T(8,128)S(1)}) custom-call(f32[256,128]{1,0:T(8,128)S(1)} %bitcast.34, f32[12,128]{1,0:T(8,128)S(1)} %get-tuple-element.28.refs_1_, f32[8,12,128]{2,1,0:T(8,128)S(1)} %get-tuple-element.29.refs_2_, bf16[8,256,1536]{2,1,0:T(8,128)(2,1)S(1)} %get-tuple-element.30.refs_3_), custom_call_target="tpu_custom_call" | custom-call | tf_op jit(solution)/shard_map/iterate/pallas_call | solution.py:454
  120.7 18.2 %all_to_all.65 = f32[256,1,128]{2,1,0:T(1,128)S(1)} all-to-all(f32[256,1,128]{2,1,0:T(1,128)S(1)} %bitcast.38), channel_id=1, replica_groups=mesh['win'=32,'ch'=8] {'win','ch'}, dimensions={0} | all-to-all | bytes 262144 | tf_op jit(solution)/shard_map/all_to_all | solution.py:464
  138.9 4.3 %iterate.3 = (f32[8,12,128]{2,1,0:T(8,128)S(1)}, f32[32,8,128]{2,1,0:T(8,128)S(1)}) custom-call(f32[256,128]{1,0:T(8,128)S(1)} %bitcast.35, f32[12,128]{1,0:T(8,128)S(1)} %get-tuple-element.28.refs_1_, f32[8,12,128]{2,1,0:T(8,128)S(1)} %get-tuple-element.32.refs_2_, bf16[8,256,1536]{2,1,0:T(8,128)(2,1)S(1)} %get-tuple-element.30.refs_3_), custom_call_target="tpu_custom_call" | custom-call | tf_op jit(solution)/shard_map/iterate/pallas_call | solution.py:454
  143.2 12.4 %all_to_all.66.refs_0_ = f32[32,8,128]{2,1,0:T(8,128)S(1)} all-to-all(f32[32,8,128]{2,1,0:T(8,128)S(1)} %get-tuple-element.33), channel_id=1, replica_groups=mesh['win'=32,'ch'=8] {'win'}, dimensions={0} | all-to-all | bytes 262144 | tf_op jit(solution)/shard_map/all_to_all | solution.py:466
  155.6 0.2 carry.1
  155.7 9.1 %all_to_all.67 = f32[8,1,128]{2,1,0:T(1,128)S(1)} all-to-all(f32[8,1,128]{2,1,0:T(1,128)S(1)} %bitcast.40), channel_id=1, replica_groups=mesh['win'=32,'ch'=8] {'ch'}, dimensions={0} | all-to-all | bytes 8192 | tf_op jit(solution)/shard_map/all_to_all | solution.py:475
  164.8 3.6 %spectrum.1 = (f32[256,128]{1,0:T(8,128)}, f32[32,8,48]{2,1,0:T(8,128)S(1)}) custom-call(f32[8,128]{1,0:T(8,128)S(1)} %bitcast.39, f32[12,128]{1,0:T(8,128)S(1)} %get-tuple-element.28.refs_1_, f32[8,12,128]{2,1,0:T(8,128)S(1)} %get-tuple-element.34.refs_2_, bf16[8,256,1536]{2,1,0:T(8,128)(2,1)S(1)} %get-tuple-element.30.refs_3_, f32[256,256]{1,0:T(8,128)S(1)} %copy-done.3, ...), custom_call_target="tpu_custom_call" | custom-call | tf_op jit(solution)/shard_map/spectrum/pallas_call | solution.py:477
  168.4 5.7 %all-to-all-start.7 = ((f32[256,1,128]{2,1,0:T(1,128)}), f32[256,1,128]{2,1,0:T(1,128)S(1)}, u32[]{:S(2)}, u32[]{:S(2)}) async-start(f32[256,1,128]{2,1,0:T(1,128)} %bitcast.22), calls=%async_computation.7 | async-start | bytes 262144 | tf_op jit(solution)/shard_map/all_to_all | solution.py:489
  174.1 0.1 copy.13
  174.3 0.3 copy.14
  174.7 0.1 broadcast_divide_fusion
  174.8 0.9 copy.16
  175.7 11.4 %all-to-all-done.7 = f32[256,1,128]{2,1,0:T(1,128)S(1)} async-done(((f32[256,1,128]{2,1,0:T(1,128)}), f32[256,1,128]{2,1,0:T(1,128)S(1)}, u32[]{:S(2)}, u32[]{:S(2)}) %all-to-all-start.7) | async-done | bytes 131104 | tf_op jit(solution)/shard_map/all_to_all | solution.py:489
  187.1 1.7 beam.1
  (34 shorter events, 0.2 us)
Async XLA Ops:
  0.6 10.0 %copy-start.7 = (s32[12]{0:T(128)S(1)}, s32[12]{0:T(128)}, u32[]{:S(2)}) copy-start(s32[12]{0:T(128)} %param.6) | copy-start | bytes 148
  4.0 22.2 %copy-start = (bf16[12,128,512]{2,1,0:T(8,128)(2,1)S(1)}, bf16[12,128,512]{2,1,0:T(8,128)(2,1)}, u32[]{:S(2)}) copy-start(bf16[12,128,512]{2,1,0:T(8,128)(2,1)} %param.4) | copy-start | bytes 4718596
  4.0 12.0 %all-to-all-start = ((bf16[8,48,128]{2,1,0:T(8,128)(2,1)}), bf16[8,48,128]{2,1,0:T(8,128)(2,1)S(1)}, u32[]{:S(2)}, u32[]{:S(2)}) async-start(bf16[8,48,128]{2,1,0:T(8,128)(2,1)} %pick.1), calls=%async_computation | async-start | bytes 196608 | tf_op jit(solution)/shard_map/all_to_all | solution.py:368
  16.7 15.3 %all-to-all-start.2 = ((bf16[8,56,128]{2,1,0:T(8,128)(2,1)}), bf16[8,56,128]{2,1,0:T(8,128)(2,1)S(1)}, u32[]{:S(2)}, u32[]{:S(2)}) async-start(bf16[8,56,128]{2,1,0:T(8,128)(2,1)} %own.1), calls=%async_computation.2 | async-start | bytes 229376 | tf_op jit(solution)/shard_map/all_to_all | solution.py:390
  31.9 46.0 %all-to-all-start.1 = ((bf16[32,48,512]{2,1,0:T(8,128)(2,1)}), bf16[32,48,512]{2,1,0:T(8,128)(2,1)S(1)}, u32[]{:S(2)}, u32[]{:S(2)}) async-start(bf16[32,48,512]{2,1,0:T(8,128)(2,1)} %pack.1), calls=%async_computation.1 | async-start | bytes 3145728 | tf_op jit(solution)/shard_map/main/all_to_all | solution.py:426
  37.8 5.3 %collective-permute-start.2 = (bf16[8,56,128]{2,1,0:T(8,128)(2,1)S(1)}, bf16[8,56,128]{2,1,0:T(8,128)(2,1)S(1)}, u32[]{:S(2)}, u32[]{:S(2)}) collective-permute-start(bf16[8,56,128]{2,1,0:T(8,128)(2,1)S(1)} %all-to-all-done.2), channel_id=1, source_target_pairs={{0,192},{8,200},{16,208},{24,216},{32,224},{40,232},{48,240},{56,2... | collective-permute-start | bytes 344072 | tf_op jit(solution)/shard_map/ppermute | solution.py:396
  40.4 6.8 %collective-permute-start.1 = (bf16[8,56,128]{2,1,0:T(8,128)(2,1)S(1)}, bf16[8,56,128]{2,1,0:T(8,128)(2,1)S(1)}, u32[]{:S(2)}, u32[]{:S(2)}) collective-permute-start(bf16[8,56,128]{2,1,0:T(8,128)(2,1)S(1)} %all-to-all-done.2), channel_id=1, source_target_pairs={{0,128},{8,136},{16,144},{24,152},{32,160},{40,168},{48,176},{56,1... | collective-permute-start | bytes 344072 | tf_op jit(solution)/shard_map/ppermute | solution.py:396
  40.9 13.2 %collective-permute-start = (bf16[8,56,128]{2,1,0:T(8,128)(2,1)S(1)}, bf16[8,56,128]{2,1,0:T(8,128)(2,1)S(1)}, u32[]{:S(2)}, u32[]{:S(2)}) collective-permute-start(bf16[8,56,128]{2,1,0:T(8,128)(2,1)S(1)} %all-to-all-done.2), channel_id=1, source_target_pairs={{0,64},{8,72},{16,80},{24,88},{32,96},{40,104},{48,112},{56,120},{... | collective-permute-start | bytes 344072 | tf_op jit(solution)/shard_map/ppermute | solution.py:396
  54.2 18.0 %copy-start.6 = (bf16[4,8,56,128]{3,2,1,0:T(8,128)(2,1)}, bf16[4,8,56,128]{3,2,1,0:T(8,128)(2,1)S(1)}, u32[]{:S(2)}) copy-start(bf16[4,8,56,128]{3,2,1,0:T(8,128)(2,1)S(1)} %pad_maximum_fusion) | copy-start | bytes 1376260
  54.3 11.4 %collective-permute-start.3 = (bf16[32,48,128]{2,1,0:T(8,128)(2,1)S(1)}, bf16[32,48,128]{2,1,0:T(8,128)(2,1)S(1)}, u32[]{:S(2)}, u32[]{:S(2)}) collective-permute-start(bf16[32,48,128]{2,1,0:T(8,128)(2,1)S(1)} %get-tuple-element.50), channel_id=1, source_target_pairs={{0,2},{1,3},{2,4},{3,5},{4,6},{5,7},{6,0},{7,1},{8,10},{9,11},{10,... | collective-permute-start | bytes 1179656 | tf_op jit(solution)/shard_map/along_y/ppermute | solution.py:404
  55.7 10.2 %collective-permute-start.5 = (bf16[32,48,128]{2,1,0:T(8,128)(2,1)S(1)}, bf16[32,48,128]{2,1,0:T(8,128)(2,1)S(1)}, u32[]{:S(2)}, u32[]{:S(2)}) collective-permute-start(bf16[32,48,128]{2,1,0:T(8,128)(2,1)S(1)} %get-tuple-element.50), channel_id=1, source_target_pairs={{0,6},{1,7},{2,0},{3,1},{4,2},{5,3},{6,4},{7,5},{8,14},{9,15},{10,... | collective-permute-start | bytes 1179656 | tf_op jit(solution)/shard_map/along_y/ppermute | solution.py:404
  65.7 6.4 %collective-permute-start.4 = (bf16[16,48,128]{2,1,0:T(8,128)(2,1)S(1)}, bf16[16,48,128]{2,1,0:T(8,128)(2,1)S(1)}, u32[]{:S(2)}, u32[]{:S(2)}) collective-permute-start(bf16[16,48,128]{2,1,0:T(8,128)(2,1)S(1)} %slice.21), channel_id=1, source_target_pairs={{0,2},{1,3},{2,4},{3,5},{4,6},{5,7},{6,0},{7,1},{8,10},{9,11},{10,... | collective-permute-start | bytes 589832 | tf_op jit(solution)/shard_map/along_y/ppermute | solution.py:406
  66.0 6.2 %collective-permute-start.6 = (bf16[16,48,128]{2,1,0:T(8,128)(2,1)S(1)}, bf16[16,48,128]{2,1,0:T(8,128)(2,1)S(1)}, u32[]{:S(2)}, u32[]{:S(2)}) collective-permute-start(bf16[16,48,128]{2,1,0:T(8,128)(2,1)S(1)} %slice.22), channel_id=1, source_target_pairs={{0,6},{1,7},{2,0},{3,1},{4,2},{5,3},{6,4},{7,5},{8,14},{9,15},{10,... | collective-permute-start | bytes 589832 | tf_op jit(solution)/shard_map/along_y/ppermute | solution.py:407
  72.3 5.7 %collective-permute-start.7 = (bf16[4,32,48,128]{3,2,1,0:T(8,128)(2,1)S(1)}, bf16[4,32,48,128]{3,2,1,0:T(8,128)(2,1)}, u32[]{:S(2)}, u32[]{:S(2)}) collective-permute-start(bf16[4,32,48,128]{3,2,1,0:T(8,128)(2,1)S(1)} %bitcast.32), channel_id=1, source_target_pairs={{0,1},{1,0},{2,3},{3,2},{4,5},{5,4},{6,7},{7,6},{8,9},{9,8},{10,11... | collective-permute-start | bytes 4718600 | tf_op jit(solution)/shard_map/cores/ppermute | solution.py:411
  138.9 25.9 %copy-start.3 = (f32[256,256]{1,0:T(8,128)S(1)}, f32[256,256]{1,0:T(8,128)}, u32[]{:S(2)}) copy-start(f32[256,256]{1,0:T(8,128)} %get-tuple-element.35.refs_4_) | copy-start | bytes 786436
  168.4 18.7 %all-to-all-start.7 = ((f32[256,1,128]{2,1,0:T(1,128)}), f32[256,1,128]{2,1,0:T(1,128)S(1)}, u32[]{:S(2)}, u32[]{:S(2)}) async-start(f32[256,1,128]{2,1,0:T(1,128)} %bitcast.22), calls=%async_computation.7 | async-start | bytes 262144 | tf_op jit(solution)/shard_map/all_to_all | solution.py:489
  174.3 12.8 %copy-start.1 = (f32[256,512]{1,0:T(8,128)S(1)}, f32[256,512]{1,0:T(8,128)}, u32[]{:S(2)}) copy-start(f32[256,512]{1,0:T(8,128)} %get-tuple-element.43.refs_2_) | copy-start | bytes 1572868
  174.3 12.8 %copy-start.2 = (f32[256,512]{1,0:T(8,128)S(1)}, f32[256,512]{1,0:T(8,128)}, u32[]{:S(2)}) copy-start(f32[256,512]{1,0:T(8,128)} %get-tuple-element.42.refs_1_) | copy-start | bytes 1572868
  174.3 12.8 %copy-start.4 = (f32[128,512]{1,0:T(8,128)S(1)}, f32[128,512]{1,0:T(8,128)}, u32[]{:S(2)}) copy-start(f32[128,512]{1,0:T(8,128)} %get-tuple-element.45.refs_4_) | copy-start | bytes 786436
  174.3 12.8 %copy-start.5 = (f32[128,512]{1,0:T(8,128)S(1)}, f32[128,512]{1,0:T(8,128)}, u32[]{:S(2)}) copy-start(f32[128,512]{1,0:T(8,128)} %get-tuple-element.44.refs_3_) | copy-start | bytes 786436

commit v6 on v5

--- a/solution.py
+++ b/solution.py
@@ -151,10 +151,12 @@
 
 
 def correlate_kernel(
-    ids_ref, a_ref, x_ref, y_ref, masks_ref, inv_hbm, c_ref, r_ref, part_ref, mask_ref, even_ref, odd_ref, terms_ref, stack_ref, inv_ref, sem
+    ids_ref, a_ref, x_ref, y_hbm, masks_ref, inv_hbm, c_ref, r_ref, part_ref, mask_ref, even_ref, odd_ref, terms_ref, stack_ref, inv_ref, y_ref, sem, y_sem
 ):
     table = pltpu.make_async_copy(inv_hbm, inv_ref, sem)
     table.start()
+    others = pltpu.make_async_copy(y_hbm, y_ref, y_sem)
+    others.start()
     n_win, rows = x_ref.shape[1], a_ref.shape[0]
     half = a_ref.shape[1] // 2
     rows_dev = rows // n_win
@@ -210,6 +212,7 @@
 
     fill(even_ref, x_ref, 0, 0)
     table.wait()
+    others.wait()
     pairs_of_slots = count // 2
 
     def slot(k, carry):
@@ -436,11 +439,12 @@
     cross = pltpu.VMEM((rows // 2, width), jnp.bfloat16)
     corr, r, part, mask = pl.pallas_call(
         correlate_kernel,
-        in_specs=[SMEM] + [VMEM] * 4 + [pl.BlockSpec(memory_space=pl.ANY)],
+        in_specs=[SMEM, VMEM, VMEM, pl.BlockSpec(memory_space=pl.ANY), VMEM, pl.BlockSpec(memory_space=pl.ANY)],
         out_specs=[VMEM] * 4,
         out_shape=[corr_shape, r_shape, part_shape, mask_shape],
         scratch_shapes=[
-            cross, cross, terms, stack, pltpu.VMEM((L, width), jnp.bfloat16), pltpu.SemaphoreType.DMA
+            cross, cross, terms, stack, pltpu.VMEM((L, width), jnp.bfloat16),
+            pltpu.VMEM((4, n_win, piece, LANES), jnp.bfloat16), pltpu.SemaphoreType.DMA, pltpu.SemaphoreType.DMA
         ],
         compiler_params=PARAMS,
         name="correlate",

time: 189 us -> 189 us (level)
  no operation moved by 1% of the time
where the time goes in v6:
time: 189 us
  blocking collectives  63.3 us (33%)
  waiting for transfers between devices  42 us (22%)
  starting transfers between devices  37.6 us (20%)
  Pallas kernels  34.7 us (18%)
  other arithmetic  7.31 us (4%)
  local copies, waits for them, and re-layouts  2.68 us (1%)
    all_to_all x2, blocking collectives, body(): parts = lax.all_to_all(part, ('win', 'ch'), 0, 0, tiled=True)  41.9 us
    pallas_call x1, Pallas kernels, body(): pl.pallas_call(correlate_kernel, in_specs=[SMEM, VMEM, VMEM, pl.BlockSpec...  14.5 us
    ppermute x3, waiting for transfers between devices, body(): lax.ppermute(own, 'win', turn_x(d))  12.6 us
    all_to_all x1, blocking collectives, body(): back = lax.all_to_all(part, 'win', 0, 0, tiled=True)  12.4 us
    all_to_all x1, waiting for transfers between devices, body(): pieces = lax.all_to_all(spectrum, ('win', 'ch'), 0, 0, tiled=True)  11.4 us
    all_to_all x1, blocking collectives, body(): parts = lax.all_to_all(over_win, 'ch', 0, 0, tiled=True)  9.06 us
    ppermute x1, waiting for transfers between devices, body(): lax.ppermute(own, 'ch', turn_y(1))  8.68 us
    pallas_call x2, Pallas kernels, body(): pl.pallas_call(lambda *refs: kernel(pairs, *refs), in_specs=[VMEM] * 4, o...  8.61 us
  transfers between devices with their start and end apart: 12, of which 8 were waited for; matrix products, arithmetic and copies ran while one was open for 5% of the time, Pallas kernels for 1%

profile of v6, /device:TPU:1, one launch (start us, length us, event | category | flops | bytes accessed | tf_op | source)
XLA Modules:
  0.0 188.5 jit_solution(10815623772535925500)
XLA Ops:
  0.6 3.3 %pick.1 = bf16[8,48,128]{2,1,0:T(8,128)(2,1)} custom-call(s32[8]{0:T(128)} %sources_ref.1, bf16[1536,512]{1,0:T(8,128)(2,1)} %bitcast.29), custom_call_target="tpu_custom_call" | custom-call | tf_op jit(solution)/shard_map/pick/pallas_call | solution.py:360
  4.0 6.6 %all-to-all-start = ((bf16[8,48,128]{2,1,0:T(8,128)(2,1)}), bf16[8,48,128]{2,1,0:T(8,128)(2,1)S(1)}, u32[]{:S(2)}, u32[]{:S(2)}) async-start(bf16[8,48,128]{2,1,0:T(8,128)(2,1)} %pick.1), calls=%async_computation | async-start | bytes 196608 | tf_op jit(solution)/shard_map/all_to_all | solution.py:371
  10.6 0.1 broadcast_in_dim.7
  10.7 0.1 reshape.96
  10.8 1.9 %fusion.14 = (f32[128,512]{1,0:T(8,128)}, f32[128,512]{1,0:T(8,128)}) fusion(s32[512]{0:T(512)S(1)} %iota_add_fusion, s32[128]{0:T(128)S(1)} %fusion.23), kind=kLoop, calls=%fused_computation.32 | loop fusion | flops 917504 | bytes 526848 | tf_op jit(solution)/shard_map/sin | solution.py:334
  12.7 3.2 %fusion.11 = (f32[256,512]{1,0:T(8,128)}, f32[256,512]{1,0:T(8,128)}) fusion(s32[512]{0:T(512)S(1)} %iota_add_fusion, s32[256]{0:T(256)S(1)} %fusion.20), kind=kLoop, calls=%fused_computation.28 | loop fusion | flops 1835008 | bytes 1051648 | tf_op jit(solution)/shard_map/sin | solution.py:334
  16.0 0.7 own.1
  16.7 7.7 %all-to-all-start.2 = ((bf16[8,56,128]{2,1,0:T(8,128)(2,1)}), bf16[8,56,128]{2,1,0:T(8,128)(2,1)S(1)}, u32[]{:S(2)}, u32[]{:S(2)}) async-start(bf16[8,56,128]{2,1,0:T(8,128)(2,1)} %own.1), calls=%async_computation.2 | async-start | bytes 229376 | tf_op jit(solution)/shard_map/all_to_all | solution.py:393
  24.3 1.8 negate_multiply_fusion
  26.1 2.2 %pack.1 = bf16[32,48,512]{2,1,0:T(8,128)(2,1)} custom-call(bf16[1536,512]{1,0:T(8,128)(2,1)S(1)} %bitcast.30), custom_call_target="tpu_custom_call" | custom-call | tf_op jit(solution)/shard_map/main/pack/pallas_call | solution.py:420
  28.3 3.6 %all-to-all-done.2 = bf16[8,56,128]{2,1,0:T(8,128)(2,1)S(1)} async-done(((bf16[8,56,128]{2,1,0:T(8,128)(2,1)}), bf16[8,56,128]{2,1,0:T(8,128)(2,1)S(1)}, u32[]{:S(2)}, u32[]{:S(2)}) %all-to-all-start.2) | async-done | bytes 114720 | tf_op jit(solution)/shard_map/all_to_all | solution.py:393
  31.9 5.9 %all-to-all-start.1 = ((bf16[32,48,512]{2,1,0:T(8,128)(2,1)}), bf16[32,48,512]{2,1,0:T(8,128)(2,1)S(1)}, u32[]{:S(2)}, u32[]{:S(2)}) async-start(bf16[32,48,512]{2,1,0:T(8,128)(2,1)} %pack.1), calls=%async_computation.1 | async-start | bytes 3145728 | tf_op jit(solution)/shard_map/main/all_to_all | solution.py:429
  37.8 2.6 %collective-permute-start.2 = (bf16[8,56,128]{2,1,0:T(8,128)(2,1)S(1)}, bf16[8,56,128]{2,1,0:T(8,128)(2,1)S(1)}, u32[]{:S(2)}, u32[]{:S(2)}) collective-permute-start(bf16[8,56,128]{2,1,0:T(8,128)(2,1)S(1)} %all-to-all-done.2), channel_id=1, source_target_pairs={{0,192},{8,200},{16,208},{24,216},{32,224},{40,232},{48,240},{56,2... | collective-permute-start | bytes 344072 | tf_op jit(solution)/shard_map/ppermute | solution.py:399
  40.4 0.5 collective-permute-start.1
  40.9 0.6 collective-permute-start
  41.5 1.6 collective-permute-done.2
  43.1 4.1 %collective-permute-done.1 = bf16[8,56,128]{2,1,0:T(8,128)(2,1)S(1)} collective-permute-done((bf16[8,56,128]{2,1,0:T(8,128)(2,1)S(1)}, bf16[8,56,128]{2,1,0:T(8,128)(2,1)S(1)}, u32[]{:S(2)}, u32[]{:S(2)}) %collective-permute-start.1) | collective-permute-done | bytes 114720 | tf_op jit(solution)/shard_map/ppermute | solution.py:399
  47.2 6.9 %collective-permute-done = bf16[8,56,128]{2,1,0:T(8,128)(2,1)S(1)} collective-permute-done((bf16[8,56,128]{2,1,0:T(8,128)(2,1)S(1)}, bf16[8,56,128]{2,1,0:T(8,128)(2,1)S(1)}, u32[]{:S(2)}, u32[]{:S(2)}) %collective-permute-start) | collective-permute-done | bytes 114720 | tf_op jit(solution)/shard_map/ppermute | solution.py:399
  54.1 0.1 pad_maximum_fusion
  54.2 0.1 fusion.26
  54.3 1.4 collective-permute-start.3
  55.7 1.3 collective-permute-start.5
  57.0 8.7 %collective-permute-done.3 = bf16[32,48,128]{2,1,0:T(8,128)(2,1)S(1)} collective-permute-done((bf16[32,48,128]{2,1,0:T(8,128)(2,1)S(1)}, bf16[32,48,128]{2,1,0:T(8,128)(2,1)S(1)}, u32[]{:S(2)}, u32[]{:S(2)}) %collective-permute-start.3) | collective-permute-done | bytes 393248 | tf_op jit(solution)/shard_map/along_y/ppermute | solution.py:407
  65.7 0.2 collective-permute-start.4
  66.0 2.6 %collective-permute-start.6 = (bf16[16,48,128]{2,1,0:T(8,128)(2,1)S(1)}, bf16[16,48,128]{2,1,0:T(8,128)(2,1)S(1)}, u32[]{:S(2)}, u32[]{:S(2)}) collective-permute-start(bf16[16,48,128]{2,1,0:T(8,128)(2,1)S(1)} %slice.22), channel_id=1, source_target_pairs={{0,6},{1,7},{2,0},{3,1},{4,2},{5,3},{6,4},{7,5},{8,14},{9,15},{10,... | collective-permute-start | bytes 589832 | tf_op jit(solution)/shard_map/along_y/ppermute | solution.py:410
  68.6 0.1 constant_dynamic-update-slice_fusion.3
  68.7 3.5 %collective-permute-done.4 = bf16[16,48,128]{2,1,0:T(8,128)(2,1)S(1)} collective-permute-done((bf16[16,48,128]{2,1,0:T(8,128)(2,1)S(1)}, bf16[16,48,128]{2,1,0:T(8,128)(2,1)S(1)}, u32[]{:S(2)}, u32[]{:S(2)}) %collective-permute-start.4) | collective-permute-done | bytes 196640 | tf_op jit(solution)/shard_map/along_y/ppermute | solution.py:409
  72.2 0.1 constant_dynamic-update-slice_fusion
  72.3 2.5 %collective-permute-start.7 = (bf16[4,32,48,128]{3,2,1,0:T(8,128)(2,1)S(1)}, bf16[4,32,48,128]{3,2,1,0:T(8,128)(2,1)}, u32[]{:S(2)}, u32[]{:S(2)}) collective-permute-start(bf16[4,32,48,128]{3,2,1,0:T(8,128)(2,1)S(1)} %bitcast.32), channel_id=1, source_target_pairs={{0,1},{1,0},{2,3},{3,2},{4,5},{5,4},{6,7},{7,6},{8,9},{9,8},{10,11... | collective-permute-start | bytes 4718600 | tf_op jit(solution)/shard_map/cores/ppermute | solution.py:414
  74.8 0.1 pad_add_fusion.ids_ref
  74.9 0.8 slice.23.masks_ref
  75.7 2.2 %collective-permute-done.7.y_hbm = bf16[4,32,48,128]{3,2,1,0:T(8,128)(2,1)} collective-permute-done((bf16[4,32,48,128]{3,2,1,0:T(8,128)(2,1)S(1)}, bf16[4,32,48,128]{3,2,1,0:T(8,128)(2,1)}, u32[]{:S(2)}, u32[]{:S(2)}) %collective-permute-start.7) | collective-permute-done | bytes 1572896 | tf_op jit(solution)/shard_map/cores/ppermute | solution.py:414
  77.9 14.5 %correlate.1 = (bf16[8,256,1536]{2,1,0:T(8,128)(2,1)S(1)}, f32[8,12,128]{2,1,0:T(8,128)S(1)}, f32[256,128]{1,0:T(8,128)S(1)}, f32[12,128]{1,0:T(8,128)S(1)}) custom-call(s32[9]{0:T(128)S(1)} %pad_add_fusion.ids_ref, bf16[1536,512]{1,0:T(8,128)(2,1)S(1)} %bitcast.31, bf16[4,32,48,128]{3,2,1,0:T(8,128)(2,1)S(1)} %bitcast.33, ...), custom_call_target="tpu_custom_call" | custom-call | tf_op jit(solution)/shard_map/correlate/pallas_call | solution.py:440
  92.4 23.7 %all_to_all.64 = f32[256,1,128]{2,1,0:T(1,128)S(1)} all-to-all(f32[256,1,128]{2,1,0:T(1,128)S(1)} %bitcast.37), channel_id=1, replica_groups=mesh['win'=32,'ch'=8] {'win','ch'}, dimensions={0} | all-to-all | bytes 262144 | tf_op jit(solution)/shard_map/all_to_all | solution.py:453
  116.1 4.3 %iterate.2 = (f32[8,12,128]{2,1,0:T(8,128)S(1)}, f32[256,128]{1,0:T(8,128)S(1)}) custom-call(f32[256,128]{1,0:T(8,128)S(1)} %bitcast.34, f32[12,128]{1,0:T(8,128)S(1)} %get-tuple-element.28.refs_1_, f32[8,12,128]{2,1,0:T(8,128)S(1)} %get-tuple-element.29.refs_2_, bf16[8,256,1536]{2,1,0:T(8,128)(2,1)S(1)} %get-tuple-element.30.refs_3_), custom_call_target="tpu_custom_call" | custom-call | tf_op jit(solution)/shard_map/iterate/pallas_call | solution.py:458
  120.4 18.2 %all_to_all.65 = f32[256,1,128]{2,1,0:T(1,128)S(1)} all-to-all(f32[256,1,128]{2,1,0:T(1,128)S(1)} %bitcast.38), channel_id=1, replica_groups=mesh['win'=32,'ch'=8] {'win','ch'}, dimensions={0} | all-to-all | bytes 262144 | tf_op jit(solution)/shard_map/all_to_all | solution.py:468
  138.6 4.3 %iterate.3 = (f32[8,12,128]{2,1,0:T(8,128)S(1)}, f32[32,8,128]{2,1,0:T(8,128)S(1)}) custom-call(f32[256,128]{1,0:T(8,128)S(1)} %bitcast.35, f32[12,128]{1,0:T(8,128)S(1)} %get-tuple-element.28.refs_1_, f32[8,12,128]{2,1,0:T(8,128)S(1)} %get-tuple-element.32.refs_2_, bf16[8,256,1536]{2,1,0:T(8,128)(2,1)S(1)} %get-tuple-element.30.refs_3_), custom_call_target="tpu_custom_call" | custom-call | tf_op jit(solution)/shard_map/iterate/pallas_call | solution.py:458
  142.9 12.4 %all_to_all.66.refs_0_ = f32[32,8,128]{2,1,0:T(8,128)S(1)} all-to-all(f32[32,8,128]{2,1,0:T(8,128)S(1)} %get-tuple-element.33), channel_id=1, replica_groups=mesh['win'=32,'ch'=8] {'win'}, dimensions={0} | all-to-all | bytes 262144 | tf_op jit(solution)/shard_map/all_to_all | solution.py:470
  155.3 0.2 carry.1
  155.4 9.1 %all_to_all.67 = f32[8,1,128]{2,1,0:T(1,128)S(1)} all-to-all(f32[8,1,128]{2,1,0:T(1,128)S(1)} %bitcast.40), channel_id=1, replica_groups=mesh['win'=32,'ch'=8] {'ch'}, dimensions={0} | all-to-all | bytes 8192 | tf_op jit(solution)/shard_map/all_to_all | solution.py:479
  164.5 3.6 %spectrum.1 = (f32[256,128]{1,0:T(8,128)}, f32[32,8,48]{2,1,0:T(8,128)S(1)}) custom-call(f32[8,128]{1,0:T(8,128)S(1)} %bitcast.39, f32[12,128]{1,0:T(8,128)S(1)} %get-tuple-element.28.refs_1_, f32[8,12,128]{2,1,0:T(8,128)S(1)} %get-tuple-element.34.refs_2_, bf16[8,256,1536]{2,1,0:T(8,128)(2,1)S(1)} %get-tuple-element.30.refs_3_, f32[256,256]{1,0:T(8,128)S(1)} %copy-done.3, ...), custom_call_target="tpu_custom_call" | custom-call | tf_op jit(solution)/shard_map/spectrum/pallas_call | solution.py:481
  168.1 5.7 %all-to-all-start.7 = ((f32[256,1,128]{2,1,0:T(1,128)}), f32[256,1,128]{2,1,0:T(1,128)S(1)}, u32[]{:S(2)}, u32[]{:S(2)}) async-start(f32[256,1,128]{2,1,0:T(1,128)} %bitcast.22), calls=%async_computation.7 | async-start | bytes 262144 | tf_op jit(solution)/shard_map/all_to_all | solution.py:493
  173.8 0.1 copy.13
  174.0 0.3 copy.14
  174.4 0.1 broadcast_divide_fusion
  174.5 0.9 copy.16
  175.4 11.4 %all-to-all-done.7 = f32[256,1,128]{2,1,0:T(1,128)S(1)} async-done(((f32[256,1,128]{2,1,0:T(1,128)}), f32[256,1,128]{2,1,0:T(1,128)S(1)}, u32[]{:S(2)}, u32[]{:S(2)}) %all-to-all-start.7) | async-done | bytes 131104 | tf_op jit(solution)/shard_map/all_to_all | solution.py:493
  186.8 1.7 beam.1
  (34 shorter events, 0.2 us)
Async XLA Ops:
  0.6 10.0 %copy-start.7 = (s32[12]{0:T(128)S(1)}, s32[12]{0:T(128)}, u32[]{:S(2)}) copy-start(s32[12]{0:T(128)} %param.6) | copy-start | bytes 148
  4.0 22.2 %copy-start = (bf16[12,128,512]{2,1,0:T(8,128)(2,1)S(1)}, bf16[12,128,512]{2,1,0:T(8,128)(2,1)}, u32[]{:S(2)}) copy-start(bf16[12,128,512]{2,1,0:T(8,128)(2,1)} %param.4) | copy-start | bytes 4718596
  4.0 12.0 %all-to-all-start = ((bf16[8,48,128]{2,1,0:T(8,128)(2,1)}), bf16[8,48,128]{2,1,0:T(8,128)(2,1)S(1)}, u32[]{:S(2)}, u32[]{:S(2)}) async-start(bf16[8,48,128]{2,1,0:T(8,128)(2,1)} %pick.1), calls=%async_computation | async-start | bytes 196608 | tf_op jit(solution)/shard_map/all_to_all | solution.py:371
  16.7 15.3 %all-to-all-start.2 = ((bf16[8,56,128]{2,1,0:T(8,128)(2,1)}), bf16[8,56,128]{2,1,0:T(8,128)(2,1)S(1)}, u32[]{:S(2)}, u32[]{:S(2)}) async-start(bf16[8,56,128]{2,1,0:T(8,128)(2,1)} %own.1), calls=%async_computation.2 | async-start | bytes 229376 | tf_op jit(solution)/shard_map/all_to_all | solution.py:393
  31.9 46.0 %all-to-all-start.1 = ((bf16[32,48,512]{2,1,0:T(8,128)(2,1)}), bf16[32,48,512]{2,1,0:T(8,128)(2,1)S(1)}, u32[]{:S(2)}, u32[]{:S(2)}) async-start(bf16[32,48,512]{2,1,0:T(8,128)(2,1)} %pack.1), calls=%async_computation.1 | async-start | bytes 3145728 | tf_op jit(solution)/shard_map/main/all_to_all | solution.py:429
  37.8 5.3 %collective-permute-start.2 = (bf16[8,56,128]{2,1,0:T(8,128)(2,1)S(1)}, bf16[8,56,128]{2,1,0:T(8,128)(2,1)S(1)}, u32[]{:S(2)}, u32[]{:S(2)}) collective-permute-start(bf16[8,56,128]{2,1,0:T(8,128)(2,1)S(1)} %all-to-all-done.2), channel_id=1, source_target_pairs={{0,192},{8,200},{16,208},{24,216},{32,224},{40,232},{48,240},{56,2... | collective-permute-start | bytes 344072 | tf_op jit(solution)/shard_map/ppermute | solution.py:399
  40.4 6.8 %collective-permute-start.1 = (bf16[8,56,128]{2,1,0:T(8,128)(2,1)S(1)}, bf16[8,56,128]{2,1,0:T(8,128)(2,1)S(1)}, u32[]{:S(2)}, u32[]{:S(2)}) collective-permute-start(bf16[8,56,128]{2,1,0:T(8,128)(2,1)S(1)} %all-to-all-done.2), channel_id=1, source_target_pairs={{0,128},{8,136},{16,144},{24,152},{32,160},{40,168},{48,176},{56,1... | collective-permute-start | bytes 344072 | tf_op jit(solution)/shard_map/ppermute | solution.py:399
  40.9 13.2 %collective-permute-start = (bf16[8,56,128]{2,1,0:T(8,128)(2,1)S(1)}, bf16[8,56,128]{2,1,0:T(8,128)(2,1)S(1)}, u32[]{:S(2)}, u32[]{:S(2)}) collective-permute-start(bf16[8,56,128]{2,1,0:T(8,128)(2,1)S(1)} %all-to-all-done.2), channel_id=1, source_target_pairs={{0,64},{8,72},{16,80},{24,88},{32,96},{40,104},{48,112},{56,120},{... | collective-permute-start | bytes 344072 | tf_op jit(solution)/shard_map/ppermute | solution.py:399
  54.2 18.0 %copy-start.6 = (bf16[4,8,56,128]{3,2,1,0:T(8,128)(2,1)}, bf16[4,8,56,128]{3,2,1,0:T(8,128)(2,1)S(1)}, u32[]{:S(2)}) copy-start(bf16[4,8,56,128]{3,2,1,0:T(8,128)(2,1)S(1)} %pad_maximum_fusion) | copy-start | bytes 1376260
  54.3 11.4 %collective-permute-start.3 = (bf16[32,48,128]{2,1,0:T(8,128)(2,1)S(1)}, bf16[32,48,128]{2,1,0:T(8,128)(2,1)S(1)}, u32[]{:S(2)}, u32[]{:S(2)}) collective-permute-start(bf16[32,48,128]{2,1,0:T(8,128)(2,1)S(1)} %get-tuple-element.50), channel_id=1, source_target_pairs={{0,2},{1,3},{2,4},{3,5},{4,6},{5,7},{6,0},{7,1},{8,10},{9,11},{10,... | collective-permute-start | bytes 1179656 | tf_op jit(solution)/shard_map/along_y/ppermute | solution.py:407
  55.7 10.2 %collective-permute-start.5 = (bf16[32,48,128]{2,1,0:T(8,128)(2,1)S(1)}, bf16[32,48,128]{2,1,0:T(8,128)(2,1)S(1)}, u32[]{:S(2)}, u32[]{:S(2)}) collective-permute-start(bf16[32,48,128]{2,1,0:T(8,128)(2,1)S(1)} %get-tuple-element.50), channel_id=1, source_target_pairs={{0,6},{1,7},{2,0},{3,1},{4,2},{5,3},{6,4},{7,5},{8,14},{9,15},{10,... | collective-permute-start | bytes 1179656 | tf_op jit(solution)/shard_map/along_y/ppermute | solution.py:407
  65.7 6.4 %collective-permute-start.4 = (bf16[16,48,128]{2,1,0:T(8,128)(2,1)S(1)}, bf16[16,48,128]{2,1,0:T(8,128)(2,1)S(1)}, u32[]{:S(2)}, u32[]{:S(2)}) collective-permute-start(bf16[16,48,128]{2,1,0:T(8,128)(2,1)S(1)} %slice.21), channel_id=1, source_target_pairs={{0,2},{1,3},{2,4},{3,5},{4,6},{5,7},{6,0},{7,1},{8,10},{9,11},{10,... | collective-permute-start | bytes 589832 | tf_op jit(solution)/shard_map/along_y/ppermute | solution.py:409
  66.0 6.2 %collective-permute-start.6 = (bf16[16,48,128]{2,1,0:T(8,128)(2,1)S(1)}, bf16[16,48,128]{2,1,0:T(8,128)(2,1)S(1)}, u32[]{:S(2)}, u32[]{:S(2)}) collective-permute-start(bf16[16,48,128]{2,1,0:T(8,128)(2,1)S(1)} %slice.22), channel_id=1, source_target_pairs={{0,6},{1,7},{2,0},{3,1},{4,2},{5,3},{6,4},{7,5},{8,14},{9,15},{10,... | collective-permute-start | bytes 589832 | tf_op jit(solution)/shard_map/along_y/ppermute | solution.py:410
  72.3 5.7 %collective-permute-start.7 = (bf16[4,32,48,128]{3,2,1,0:T(8,128)(2,1)S(1)}, bf16[4,32,48,128]{3,2,1,0:T(8,128)(2,1)}, u32[]{:S(2)}, u32[]{:S(2)}) collective-permute-start(bf16[4,32,48,128]{3,2,1,0:T(8,128)(2,1)S(1)} %bitcast.32), channel_id=1, source_target_pairs={{0,1},{1,0},{2,3},{3,2},{4,5},{5,4},{6,7},{7,6},{8,9},{9,8},{10,11... | collective-permute-start | bytes 4718600 | tf_op jit(solution)/shard_map/cores/ppermute | solution.py:414
  138.6 25.9 %copy-start.3 = (f32[256,256]{1,0:T(8,128)S(1)}, f32[256,256]{1,0:T(8,128)}, u32[]{:S(2)}) copy-start(f32[256,256]{1,0:T(8,128)} %get-tuple-element.35.refs_4_) | copy-start | bytes 786436
  168.1 18.7 %all-to-all-start.7 = ((f32[256,1,128]{2,1,0:T(1,128)}), f32[256,1,128]{2,1,0:T(1,128)S(1)}, u32[]{:S(2)}, u32[]{:S(2)}) async-start(f32[256,1,128]{2,1,0:T(1,128)} %bitcast.22), calls=%async_computation.7 | async-start | bytes 262144 | tf_op jit(solution)/shard_map/all_to_all | solution.py:493
  174.0 12.8 %copy-start.1 = (f32[256,512]{1,0:T(8,128)S(1)}, f32[256,512]{1,0:T(8,128)}, u32[]{:S(2)}) copy-start(f32[256,512]{1,0:T(8,128)} %get-tuple-element.43.refs_2_) | copy-start | bytes 1572868
  174.0 12.8 %copy-start.2 = (f32[256,512]{1,0:T(8,128)S(1)}, f32[256,512]{1,0:T(8,128)}, u32[]{:S(2)}) copy-start(f32[256,512]{1,0:T(8,128)} %get-tuple-element.42.refs_1_) | copy-start | bytes 1572868
  174.0 12.8 %copy-start.4 = (f32[128,512]{1,0:T(8,128)S(1)}, f32[128,512]{1,0:T(8,128)}, u32[]{:S(2)}) copy-start(f32[128,512]{1,0:T(8,128)} %get-tuple-element.45.refs_4_) | copy-start | bytes 786436
  174.0 12.8 %copy-start.5 = (f32[128,512]{1,0:T(8,128)S(1)}, f32[128,512]{1,0:T(8,128)}, u32[]{:S(2)}) copy-start(f32[128,512]{1,0:T(8,128)} %get-tuple-element.44.refs_3_) | copy-start | bytes 786436
